TPU v7x, 32 devices: a whole 2x2x4 slice. The times are simulated.
32 devices in a mesh: rep: 2 (over y), sample: 4 (over z), head: 4 (over x, core).
Axes of the slice: x: 2, y: 2, z: 4, core: 2. Of those that a mesh axis runs over, the one named last changes fastest.
Arguments:
- x_pre: bfloat16 [8, 128, 8192], P(('rep', 'sample'), None, 'head'), parts along dimension 0, may hold values from -120 to 120
- z_pre: bfloat16 [8, 128, 8192], P(('rep', 'sample'), None, 'head'), parts along dimension 0, may hold values from -6 to 6
- b_pre: bfloat16 [8, 128, 512], P(('rep', 'sample')), parts along dimension 0, may hold values from -1.796875 to 1.796875
- c_pre: bfloat16 [8, 128, 512], P(('rep', 'sample')), parts along dimension 0, may hold values from -0.5390625 to 0.5390625
- dt_pre: float32 [8, 128, 128], P(('rep', 'sample'), None, 'head'), parts along dimension 0, may hold values from -1.5 to 7.5
- lengths: int32 [8], P(('rep', 'sample')), parts along dimension 0, may hold values from 64 to 128, as said below
- init_state: float32 [8, 128, 8192], P(('rep', 'sample'), None, 'head'), parts along dimension 0, may hold values from -6 to 6
- a_rates: float32 [128], P('head'), may hold values from 0.005 to 0.3
- dt_bias: float32 [128], P('head'), may hold values from -2 to -1
- skip_scale: float32 [128], P('head'), may hold values from 0.5 to 2
- norm_gain: float32 [8192], P('head'), may hold values from 0.5 to 1.5
- x_dec: bfloat16 [8, 4, 8192], P(('rep', 'sample'), None, 'head'), parts along dimension 0, may hold values from -120 to 120
- z_dec: bfloat16 [8, 4, 8192], P(('rep', 'sample'), None, 'head'), parts along dimension 0, may hold values from -6 to 6
- b_dec: bfloat16 [8, 4, 512], P(('rep', 'sample')), parts along dimension 0, may hold values from -6 to 6
- c_dec: bfloat16 [8, 4, 512], P(('rep', 'sample')), parts along dimension 0, may hold values from -0.5390625 to 0.5390625
- dt_dec: float32 [8, 4, 128], P(('rep', 'sample'), None, 'head'), parts along dimension 0, may hold values from -3 to 3
Outputs:
- out_pre: bfloat16 [8, 128, 8192], P(('rep', 'sample'), None, 'head'), parts along dimension 0
- final_state: bfloat16 [8, 128, 8192], P(('rep', 'sample'), None, 'head'), parts along dimension 0
- out_dec: bfloat16 [8, 4, 8192], P(('rep', 'sample'), None, 'head'), parts along dimension 0
There are 2 independent parts, one for each index of `rep`. A program takes and returns all parts, laid end to end along the dimension named above; an argument that names none is the same for every part. Nothing has to cross between parts.
Inputs may be any that keep to these rules, and one draw needn't show every extreme that they name: Each prompt's valid tokens are the first lengths[p] of its 128 positions; some prompt uses all 128.
All inputs are finite; a program needn't handle non-finite values.
Results may differ from a plain program's by a relative error of at most 0.006.
Values may be sent and summed in bfloat16 or wider, within the bound.
No kernel may reach another device: no remote copies, remote signals or barrier semaphores. Data moves between devices by JAX's collectives and lax.ppermute only.
A program may use at most 64 MiB of HBM per device.

v0:
```python
import jax
import jax.numpy as jnp
from jax import lax
from jax.sharding import PartitionSpec as P

H = 128
P_SIZE = 64
G = 4
BLOCK = 128


epsilon = 1e-05
highest = lax.Precision.HIGHEST


def group_owners(first_head, head_count):
    head_ids = first_head + jnp.arange(head_count, dtype=jnp.int32)
    return head_ids // (H // G)


def group_pick(owners):
    return (owners[:, None] == jnp.arange(G, dtype=jnp.int32)[None, :]).astype(jnp.float32)


def scan_prompt(inputs, b_rows, c_rows, step_delta, rates, skip_gain, start_state, owners):
    length = inputs.shape[0]
    head_count = step_delta.shape[1]
    head_width = inputs.shape[1] // head_count
    states = b_rows.shape[1] // G
    blocks = length // BLOCK
    b_groups = b_rows.reshape(blocks, BLOCK, G, states)
    c_groups = c_rows.reshape(blocks, BLOCK, G, states)
    group_scores = jnp.einsum(
        "cign,cjgn->cijg", c_groups, b_groups, preferred_element_type=jnp.float32
    )
    head_scores = jnp.take(group_scores, owners, axis=3)
    b_head = jnp.take(b_groups, owners, axis=2).astype(jnp.float32)
    c_head = jnp.take(c_groups, owners, axis=2).astype(jnp.float32)
    values = inputs.astype(jnp.float32).reshape(blocks, BLOCK, head_count, head_width)
    block_delta = step_delta.reshape(blocks, BLOCK, head_count)
    decays = jnp.cumsum(-block_delta * rates, axis=1)
    causal_mask = (jnp.arange(BLOCK)[:, None] >= jnp.arange(BLOCK)[None, :])[None, :, :, None]
    spread = decays[:, :, None, :] - decays[:, None, :, :]
    weights = jnp.where(causal_mask, jnp.exp(jnp.where(causal_mask, spread, 0.0)), 0.0)
    scores = head_scores * weights * block_delta[:, None, :, :]
    inner_part = jnp.einsum("cijh,cjhp->cihp", scores, values, precision=highest)
    tail_decay = jnp.exp(decays[:, -1:, :] - decays) * block_delta
    block_states = jnp.einsum(
        "cjhn,cjhp->cnhp", b_head * tail_decay[..., None], values, precision=highest
    )
    block_totals = jnp.exp(decays[:, -1, :])

    def carry_step(carried, pieces):
        factor, fresh_term = pieces
        return (factor[None, :, None] * carried + fresh_term, carried)

    final_carry, starts = lax.scan(
        carry_step,
        start_state.reshape(states, head_count, head_width),
        (block_totals, block_states),
    )
    outer_part = (
        jnp.einsum("cihn,cnhp->cihp", c_head, starts, precision=highest)
        * jnp.exp(decays)[..., None]
    )
    result = inner_part + outer_part + skip_gain[None, None, :, None] * values
    return (
        result.reshape(length, head_count * head_width),
        final_carry.reshape(states, head_count * head_width),
    )


def gate_values(result, gate_rows):
    gate_rows = gate_rows.astype(jnp.float32)
    return result * gate_rows * jax.nn.sigmoid(gate_rows)


def select_heads(c_rows, owners):
    shape_front = c_rows.shape[:2]
    states = c_rows.shape[2] // G
    grouped = c_rows.reshape(shape_front[0], shape_front[1], G, states)
    return jnp.take(grouped, owners, axis=2)


def body(
    x_pre,
    z_pre,
    b_pre,
    c_pre,
    dt_pre,
    lengths,
    init_state,
    a_rates,
    dt_bias,
    skip_scale,
    norm_gain,
    x_dec,
    z_dec,
    b_dec,
    c_dec,
    dt_dec,
):
    heads_here = a_rates.shape[0]
    head_width = x_pre.shape[2] // heads_here
    first_head = lax.axis_index("head") * heads_here
    owners = group_owners(first_head, heads_here)
    picker = group_pick(owners)
    length = x_pre.shape[1]
    positions = jnp.arange(length, dtype=jnp.int32)
    valid_mask = (positions[None, :] < lengths[:, None]).astype(jnp.float32)
    step_delta = jax.nn.softplus(dt_pre + dt_bias) * valid_mask[:, :, None]

    def one_prompt(pieces):
        inputs, b_rows, c_rows, prompt_delta, start_state = pieces
        return scan_prompt(
            inputs, b_rows, c_rows, prompt_delta, a_rates, skip_scale, start_state, owners
        )

    result, final_carry = lax.map(one_prompt, (x_pre, b_pre, c_pre, step_delta, init_state))
    final_state = final_carry.astype(jnp.bfloat16)
    gated_rows = gate_values(result, z_pre)
    pre_totals = lax.psum(jnp.sum(gated_rows * gated_rows, axis=-1), "head")
    norm_scale = lax.rsqrt(pre_totals[:, :, None] / (H * P_SIZE) + epsilon)
    out_pre = (gated_rows * norm_scale * norm_gain * valid_mask[:, :, None]).astype(jnp.bfloat16)
    slots_here = x_dec.shape[0]
    prompt_count = x_dec.shape[1]
    prompts_here = final_state.shape[0]
    states = final_state.shape[1]
    cached = final_state.reshape(prompts_here, states, heads_here, head_width)
    queries = lax.all_to_all(c_dec, "sample", split_axis=1, concat_axis=0, tiled=True)
    c_head = select_heads(queries, owners)
    answers = jnp.einsum("sphn,pnhq->sphq", c_head, cached, preferred_element_type=jnp.float32)
    answers = answers.reshape(answers.shape[0], prompts_here, heads_here * head_width)
    state_reads = lax.all_to_all(
        answers.astype(jnp.bfloat16), "sample", split_axis=0, concat_axis=1, tiled=True
    ).astype(answers.dtype)
    state_reads = state_reads.reshape(slots_here, prompt_count, heads_here, head_width)
    c_groups = c_dec.astype(jnp.float32).reshape(slots_here, prompt_count, G, states)
    b_groups = b_dec.astype(jnp.float32).reshape(slots_here, prompt_count, G, states)
    cb_dot = jnp.einsum("spgn,spgn->spg", c_groups, b_groups, precision=highest)
    cb_dot = jnp.einsum("spg,hg->sph", cb_dot, picker, precision=highest)
    step_sizes = jax.nn.softplus(dt_dec + dt_bias)
    decay_rate = jnp.exp(-step_sizes * a_rates)
    values = x_dec.astype(jnp.float32).reshape(slots_here, prompt_count, heads_here, head_width)
    fresh_term = (
        decay_rate[..., None] * state_reads + (step_sizes * cb_dot + skip_scale)[..., None] * values
    )
    gated_dec = gate_values(
        fresh_term.reshape(slots_here, prompt_count, heads_here * head_width), z_dec
    )
    dec_totals = lax.psum(jnp.sum(gated_dec * gated_dec, axis=-1), "head")
    dec_scale = lax.rsqrt(dec_totals[:, :, None] / (H * P_SIZE) + epsilon)
    out_dec = (gated_dec * dec_scale * norm_gain).astype(jnp.bfloat16)
    return (out_pre, final_state, out_dec)


def solution(mesh):
    in_specs = (
        P(("rep", "sample"), None, "head"),
        P(("rep", "sample"), None, "head"),
        P(("rep", "sample"), None, None),
        P(("rep", "sample"), None, None),
        P(("rep", "sample"), None, "head"),
        P(("rep", "sample")),
        P(("rep", "sample"), None, "head"),
        P("head"),
        P("head"),
        P("head"),
        P("head"),
        P(("rep", "sample"), None, "head"),
        P(("rep", "sample"), None, "head"),
        P(("rep", "sample"), None, None),
        P(("rep", "sample"), None, None),
        P(("rep", "sample"), None, "head"),
    )
    out_specs = (
        P(("rep", "sample"), None, "head"),
        P(("rep", "sample"), None, "head"),
        P(("rep", "sample"), None, "head"),
    )
    return jax.shard_map(body, mesh=mesh, in_specs=in_specs, out_specs=out_specs, check_vma=False)
```

profile of v0, /device:TPU:0, one launch (start us, length us, event | category | flops | bytes accessed | tf_op | source)
XLA Modules:
  0.0 61.4 jit_solution(16359119723385610459)
XLA Ops:
  0.7 0.8 %copy.168 = bf16[1,4,512]{2,0,1:T(2,128)(2,1)S(1)} copy(bf16[1,4,512]{2,1,0:T(4,128)(2,1)} %param.32) | data formatting | bytes 8192 | tf_op args[14]
  3.2 6.3 %all-to-all-start = ((bf16[4,2,256]{2,1,0:T(2,128)(2,1)}), bf16[4,2,256]{2,1,0:T(2,128)(2,1)}, u32[]{:S(2)}, u32[]{:S(2)}) async-start(bf16[4,2,256]{2,1,0:T(2,128)(2,1)} %reshape.510), calls=%async_computation | async-start | bytes 8192 | tf_op jit(solution)/shard_map/all_to_all | solution.py:130
  10.2 0.8 %negate_multiply_fusion = f32[1,128,32]{1,2,0:T(8,128)S(1)} fusion(f32[32]{0:T(128)} %param.25, f32[128]{0:T(128)S(1)} %compare_convert_fusion, f32[1,128,32]{1,2,0:T(8,128)} %param.22, f32[32]{0:T(128)} %param.26), kind=kLoop, calls=%fused_computation.73 | loop fusion | flops 40960 | bytes 33536 | tf_op jit(solution)/shard_map/while/body/eval_jaxpr/mul | solution.py:41
  13.2 0.9 %reshape.439 = bf16[128,4,128]{2,1,0:T(4,128)(2,1)S(1)} reshape(bf16[1,128,512]{2,1,0:T(8,128)(2,1)} %param.21) | data formatting | bytes 262144 | tf_op jit(solution)/shard_map/reshape.21
  14.1 1.0 %copy.129 = bf16[1,128,512]{1,2,0:T(8,128)(2,1)S(1)} copy(bf16[1,128,512]{2,1,0:T(8,128)(2,1)} %param.21) | data formatting | bytes 262144 | tf_op args[3]
  15.2 2.0 %copy.127 = bf16[1,128,2048]{1,2,0:T(8,128)(2,1)} copy(bf16[1,128,2048]{2,1,0:T(8,128)(2,1)} %param.18) | data formatting | bytes 1048576 | tf_op args[0]
  17.2 1.2 %copy.133 = f32[1,128,2048]{1,2,0:T(8,128)} copy(bf16[1,128,2048]{2,1,0:T(8,128)(2,1)S(1)} %copy-done.2) | data formatting | bytes 1572864 | tf_op jit(solution)/shard_map/while/body/eval_jaxpr/convert_element_type | solution.py:39
  18.4 0.8 %copy.136 = bf16[1,128,512]{1,2,0:T(8,128)(2,1)} copy(bf16[1,128,512]{2,1,0:T(8,128)(2,1)S(1)} %copy-done.6) | data formatting | bytes 262144 | tf_op args[2]
  20.3 0.7 %copy.125 = f32[128,32]{0,1:T(8,128)} copy(f32[128,32]{1,0:T(8,128)S(1)} %bitcast.135) | data formatting | bytes 32768 | tf_op jit(solution)/shard_map/while/body/eval_jaxpr/sub | solution.py:43
  22.8 0.7 %multiply_bitcast_fusion = (f32[128,32]{0,1:T(8,128)}, f32[128,32]{0,1:T(8,128)}) fusion(f32[1,128,32]{1,2,0:T(8,128)S(1)} %copy.138, f32[32]{0:T(128)S(1)} %slice_bitcast_fusion, f32[128]{0:T(128)S(1)} %compare_convert_fusion, f32[1,128,32]{1,2,0:T(8,128)S(1)} %copy-done.8, f32[32]{0:T(128)S(1)} %copy-done.18), kind=kLoop, calls=%fused_computation.72 | loop fusion | flops 40960 | bytes 66304 | tf_op jit(solution)/shard_map/while/body/eval_jaxpr/mul | solution.py:49
  23.7 0.8 %gather_fusion = f32[32,128,128]{1,2,0:T(8,128)S(1)} fusion(f32[128,128,4]{0,1,2:T(8,128)S(1)} %convolution_bitcast_fusion.1, s32[1024]{0:T(1024)} %pad_clamp_fusion.1), kind=kCustom, calls=%fused_computation.2 | custom fusion | bytes 4194432 | tf_op jit(solution)/shard_map/while/body/eval_jaxpr/jit(_take)/gather | solution.py:36
  24.5 1.9 %gather_fusion.2 = bf16[32,128,128]{2,1,0:T(8,128)(2,1)} fusion(bf16[128,4,128]{2,0,1:T(8,128)(2,1)S(1)} %bitcast.129, s32[1024]{0:T(1024)} %pad_clamp_fusion), kind=kCustom, calls=%fused_computation.clone | custom fusion | bytes 2097280 | tf_op jit(solution)/shard_map/while/body/eval_jaxpr/jit(_take)/gather | solution.py:38
  26.5 4.0 %fusion.12 = f32[1,128,32,64]{1,3,2,0:T(8,128)S(1)} fusion(bf16[128,32,64]{0,2,1:T(8,128)(2,1)} %bitcast.137, f32[32,128,128]{1,2,0:T(8,128)S(1)} %gather_fusion, f32[128,32]{0,1:T(8,128)S(1)} %copy-done.17, f32[128,32]{0,1:T(8,128)S(1)} %copy-done.12, pred[32]{0:T(512)(128)(4,1)S(1)} %copy-done.26, pred[128,128]{0,1:T(8,128)(4,1)S(1)} %copy-done.14), kind=kOutput, calls=%fused_computation.16 | convolution fusion | flops 405798912 | bytes 3719200 | tf_op jit(solution)/shard_map/while/body/eval_jaxpr/cijh,cjhp->cihp/dot_general | solution.py:46
  30.5 2.2 %fusion.17 = f32[1,128,32,64]{1,3,2,0:T(8,128)S(1)} fusion(f32[1,128,32,64]{1,3,2,0:T(8,128)S(1)} %fusion.12, f32[128,32,64]{0,2,1:T(8,128)S(1)} %bitcast.131, bf16[32,128,128]{2,1,0:T(8,128)(2,1)S(1)} %copy-done, f32[1,128,32,64]{1,3,2,0:T(8,128)S(1)} %bitcast.132, pred[32]{0:T(512)(128)(4,1)S(1)} %copy-done.26, f32[32]{0:T(128)S(1)} %copy-done.25, ...), kind=kOutput, calls=%fused_computation.20 | convolution fusion | flops 404226048 | bytes 5259424 | tf_op jit(solution)/shard_map/while/body/eval_jaxpr/cihn,cnhp->cihp/dot_general | solution.py:63
  33.8 1.8 %gather_fusion.3 = bf16[32,128,128]{2,1,0:T(8,128)(2,1)} fusion(bf16[128,4,128]{2,0,1:T(8,128)(2,1)S(1)} %bitcast.130, s32[1024]{0:T(1024)} %pad_clamp_fusion), kind=kCustom, calls=%fused_computation.1.clone | custom fusion | bytes 2097280 | tf_op jit(solution)/shard_map/while/body/eval_jaxpr/jit(_take)/gather | solution.py:37
  36.2 2.7 %fusion = f32[32,128,64]{1,2,0:T(8,128)S(1)} fusion(bf16[128,32,64]{0,2,1:T(8,128)(2,1)S(1)} %bitcast.138, bf16[32,128,128]{2,1,0:T(8,128)(2,1)} %gather_fusion.3, f32[128,32]{0,1:T(8,128)S(1)} %copy-done.16, pred[32]{0:T(512)(128)(4,1)S(1)} %copy-done.27), kind=kOutput, calls=%fused_computation.4 | convolution fusion | flops 404226048 | bytes 2637856 | tf_op jit(solution)/shard_map/while/body/eval_jaxpr/cjhn,cjhp->cnhp/dot_general | solution.py:48
  39.5 0.7 %reshape.511 = bf16[4,1,512]{2,1,0:T(2,128)(2,1)S(1)} reshape(bf16[4,2,256]{2,1,0:T(2,128)(2,1)} %all-to-all-done) | data formatting | bytes 8192
  40.2 0.7 %gather_fusion.1 = bf16[32,4,128]{2,1,0:T(4,128)(2,1)S(1)} fusion(bf16[4,4,128]{2,0,1:T(4,128)(2,1)S(1)} %bitcast.141, s32[1024]{0:T(1024)} %pad_clamp_fusion.1), kind=kCustom, calls=%fused_computation.3 | custom fusion | bytes 65664 | tf_op jit(solution)/shard_map/jit(_take)/gather | solution.py:82
  41.5 0.7 %reduce.7 = bf16[4,2048]{1,0:T(4,128)(2,1)S(1)} reduce(bf16[4,1,2048]{2,1,0:T(2,128)(2,1)S(1)} %convert_element_type.108, bf16[]{:T(256)} %broadcast.360), dimensions={1}, to_apply=%convert_element_type.108.reduce_sub_computation | reduce | bytes 32770 | tf_op jit(solution)/shard_map/convert_element_type | solution.py:135
  42.8 5.1 %all-to-all-start.1 = ((bf16[4,2,1024]{2,1,0:T(2,128)(2,1)}), bf16[4,2,1024]{2,1,0:T(2,128)(2,1)S(1)}, u32[]{:S(2)}, u32[]{:S(2)}) async-start(bf16[4,2,1024]{2,1,0:T(2,128)(2,1)} %reshape.512), calls=%async_computation.1 | async-start | bytes 32768 | tf_op jit(solution)/shard_map/all_to_all | solution.py:134
  48.1 1.0 %copy.145 = bf16[1,128,2048]{2,1,0:T(8,128)(2,1)} copy(bf16[1,128,2048]{1,2,0:T(8,128)(2,1)S(1)} %fusion.26) | data formatting | bytes 1048576
  49.5 4.0 %all-to-all-done.1 = bf16[4,2,1024]{2,1,0:T(2,128)(2,1)S(1)} async-done(((bf16[4,2,1024]{2,1,0:T(2,128)(2,1)}), bf16[4,2,1024]{2,1,0:T(2,128)(2,1)S(1)}, u32[]{:S(2)}, u32[]{:S(2)}) %all-to-all-start.1) | async-done | bytes 16416 | tf_op jit(solution)/shard_map/all_to_all | solution.py:134
  53.8 5.6 %all-reduce = (f32[1,128]{1,0:T(1,128)S(1)}, f32[1,4]{1,0:T(1,128)S(1)}) all-reduce(f32[1,128]{1,0:T(1,128)S(1)} %bitcast.143, f32[1,4]{1,0:T(1,128)S(1)} %bitcast.144), channel_id=1, replica_groups=mesh['rep'=2,'sample'=4,'head'=4] {'head'}, use_global_device_ids=true, to_apply=%region_2.4 | all-reduce | flops 132 | bytes 1056 | tf_op jit(solution)/shard_map/psum | solution.py:122
  60.2 1.2 %multiply_convert_fusion = bf16[1,128,2048]{2,1,0:T(8,128)(2,1)} fusion(f32[128]{0:T(128)S(1)} %copy-done.21, f32[2048]{0:T(1024)S(1)} %copy-done.9, f32[128]{0:T(128)S(1)} %rsqrt_bitcast_fusion.1, f32[1,128,2048]{2,1,0:T(8,128)S(1)} %copy.134, bf16[1,128,2048]{2,1,0:T(8,128)(2,1)S(1)} %copy-done.3), kind=kLoop, calls=%fused_computation.41 | loop fusion | flops 2621440 | bytes 2106368 | tf_op jit(solution)/shard_map/convert_element_type | solution.py:124
  (108 shorter events, 11.8 us)
Async XLA Ops:
  0.6 16.6 %copy-start.2 = (bf16[1,128,2048]{2,1,0:T(8,128)(2,1)S(1)}, bf16[1,128,2048]{2,1,0:T(8,128)(2,1)}, u32[]{:S(2)}) copy-start(bf16[1,128,2048]{2,1,0:T(8,128)(2,1)} %param.18) | copy-start | bytes 1572868
  0.6 17.8 %copy-start.6 = (bf16[1,128,512]{2,1,0:T(8,128)(2,1)S(1)}, bf16[1,128,512]{2,1,0:T(8,128)(2,1)}, u32[]{:S(2)}) copy-start(bf16[1,128,512]{2,1,0:T(8,128)(2,1)} %param.20) | copy-start | bytes 393220
  1.9 17.8 %copy-start.13 = (bf16[1,4,512]{2,1,0:T(4,128)(2,1)S(1)}, bf16[1,4,512]{2,1,0:T(4,128)(2,1)}, u32[]{:S(2)}) copy-start(bf16[1,4,512]{2,1,0:T(4,128)(2,1)} %param.32) | copy-start | bytes 12292
  3.2 36.3 %all-to-all-start = ((bf16[4,2,256]{2,1,0:T(2,128)(2,1)}), bf16[4,2,256]{2,1,0:T(2,128)(2,1)}, u32[]{:S(2)}, u32[]{:S(2)}) async-start(bf16[4,2,256]{2,1,0:T(2,128)(2,1)} %reshape.510), calls=%async_computation | async-start | bytes 8192 | tf_op jit(solution)/shard_map/all_to_all | solution.py:130
  10.2 12.5 %copy-start.20 = (f32[128]{0:T(128)}, f32[128]{0:T(128)S(1)}, u32[]{:S(2)}) copy-start(f32[128]{0:T(128)S(1)} %compare_convert_fusion) | copy-start | bytes 1540
  12.6 9.8 %copy-start.4 = (f32[1,128,2048]{2,1,0:T(8,128)S(1)}, f32[1,128,2048]{2,1,0:T(8,128)}, u32[]{:S(2)}) copy-start(f32[1,128,2048]{2,1,0:T(8,128)} %param.24) | copy-start | bytes 3145732
  17.2 5.6 %copy-start.8 = (f32[1,128,32]{1,2,0:T(8,128)S(1)}, f32[1,128,32]{1,2,0:T(8,128)}, u32[]{:S(2)}) copy-start(f32[1,128,32]{1,2,0:T(8,128)} %param.22) | copy-start | bytes 49156
  17.2 5.6 %copy-start.18 = (f32[32]{0:T(128)S(1)}, f32[32]{0:T(128)}, u32[]{:S(2)}) copy-start(f32[32]{0:T(128)} %param.26) | copy-start | bytes 388
  26.5 4.0 %copy-start = (bf16[32,128,128]{2,1,0:T(8,128)(2,1)S(1)}, bf16[32,128,128]{2,1,0:T(8,128)(2,1)}, u32[]{:S(2)}) copy-start(bf16[32,128,128]{2,1,0:T(8,128)(2,1)} %gather_fusion.2) | copy-start | bytes 3145732
  26.5 4.0 %copy-start.1 = (f32[1,128,2048]{1,2,0:T(8,128)S(1)}, f32[1,128,2048]{1,2,0:T(8,128)}, u32[]{:S(2)}) copy-start(f32[1,128,2048]{1,2,0:T(8,128)} %copy.133) | copy-start | bytes 3145732
  26.5 4.0 %copy-start.25 = (f32[32]{0:T(128)S(1)}, f32[32]{0:T(128)}, u32[]{:S(2)}) copy-start(f32[32]{0:T(128)} %param.27) | copy-start | bytes 388
  32.8 3.0 %copy-start.22 = (bf16[1,4,512]{2,1,0:T(4,128)(2,1)S(1)}, bf16[1,4,512]{2,1,0:T(4,128)(2,1)}, u32[]{:S(2)}) copy-start(bf16[1,4,512]{2,1,0:T(4,128)(2,1)} %param.31) | copy-start | bytes 12292
  32.8 3.0 %copy-start.19 = (f32[32]{0:T(128)S(1)}, f32[32]{0:T(128)}, u32[]{:S(2)}) copy-start(f32[32]{0:T(128)} %param.26) | copy-start | bytes 388
  32.8 3.0 %copy-start.23 = (f32[32]{0:T(128)S(1)}, f32[32]{0:T(128)}, u32[]{:S(2)}) copy-start(f32[32]{0:T(128)} %param.25) | copy-start | bytes 388
  33.2 3.0 %copy-start.5 = (bf16[1,128,2048]{1,2,0:T(8,128)(2,1)S(1)}, bf16[1,128,2048]{1,2,0:T(8,128)(2,1)}, u32[]{:S(2)}) copy-start(bf16[1,128,2048]{1,2,0:T(8,128)(2,1)} %copy.127) | copy-start | bytes 1572868
  33.2 3.0 %copy-start.16 = (f32[128,32]{0,1:T(8,128)S(1)}, f32[128,32]{0,1:T(8,128)}, u32[]{:S(2)}) copy-start(f32[128,32]{0,1:T(8,128)} %get-tuple-element.76) | copy-start | bytes 49156
  33.2 3.0 %copy-start.27 = (pred[32]{0:T(512)(128)(4,1)S(1)}, pred[32]{0:T(512)(128)(4,1)}, u32[]{:S(2)}) copy-start(pred[32]{0:T(512)(128)(4,1)} %compare_and_fusion) | copy-start | bytes 100
  36.2 3.2 %copy-start.15 = (bf16[4,4,128]{2,1,0:T(4,128)(2,1)S(1)}, bf16[4,4,128]{2,1,0:T(4,128)(2,1)}, u32[]{:S(2)}) copy-start(bf16[4,4,128]{2,1,0:T(4,128)(2,1)} %reshape.449) | copy-start | bytes 12292
  39.0 9.0 %copy-start.29 = (s32[32]{0:T(128)S(1)}, s32[32]{0:T(128)}, u32[]{:S(2)}) copy-start(s32[32]{0:T(128)} %get-tuple-element.79) | copy-start | bytes 388
  39.0 14.6 %copy-start.10 = (bf16[1,4,2048]{2,1,0:T(4,128)(2,1)S(1)}, bf16[1,4,2048]{2,1,0:T(4,128)(2,1)}, u32[]{:S(2)}) copy-start(bf16[1,4,2048]{2,1,0:T(4,128)(2,1)} %param.30) | copy-start | bytes 49156
  39.0 14.6 %copy-start.11 = (bf16[1,4,2048]{2,1,0:T(4,128)(2,1)S(1)}, bf16[1,4,2048]{2,1,0:T(4,128)(2,1)}, u32[]{:S(2)}) copy-start(bf16[1,4,2048]{2,1,0:T(4,128)(2,1)} %param.29) | copy-start | bytes 49156
  39.0 20.5 %copy-start.9 = (f32[2048]{0:T(1024)S(1)}, f32[2048]{0:T(1024)}, u32[]{:S(2)}) copy-start(f32[2048]{0:T(1024)} %param.28) | copy-start | bytes 24580
  39.0 21.2 %copy-start.21 = (f32[128]{0:T(128)S(1)}, f32[128]{0:T(128)}, u32[]{:S(2)}) copy-start(f32[128]{0:T(128)} %copy-done.20) | copy-start | bytes 1540
  42.8 10.7 %all-to-all-start.1 = ((bf16[4,2,1024]{2,1,0:T(2,128)(2,1)}), bf16[4,2,1024]{2,1,0:T(2,128)(2,1)S(1)}, u32[]{:S(2)}, u32[]{:S(2)}) async-start(bf16[4,2,1024]{2,1,0:T(2,128)(2,1)} %reshape.512), calls=%async_computation.1 | async-start | bytes 32768 | tf_op jit(solution)/shard_map/all_to_all | solution.py:134
  (8 other events, 17.2 us)
where the time goes:
time: 62.1 us; the launch traced here: 61.4 us
  local copies, waits for them, and re-layouts  20.3 us (33%)
  starting transfers between devices  11.4 us (18%)
  matrix products  9.71 us (16%)
  other arithmetic  8.5 us (14%)
  blocking collectives  5.63 us (9%)
  waiting for transfers between devices  4.02 us (6%)
  between operations  1.81 us (3%)
    unnamed x72, local copies, waits for them, and re-layouts  9.6 us
    all_to_all x1, starting transfers between devices, body(): lax.all_to_all(c_dec, 'sample', split_axis=1, concat_axis=0, tiled=True)  6.35 us
    psum x1, blocking collectives, body(): pre_totals = lax.psum(jnp.sum(gated_rows * gated_rows, axis=-1), 'head')  5.63 us
    all_to_all x1, starting transfers between devices, body(): lax.all_to_all(answers.astype(jnp.bfloat16), 'sample', split_axis=0, conc...  5.09 us
    all_to_all x1, waiting for transfers between devices, body(): lax.all_to_all(answers.astype(jnp.bfloat16), 'sample', split_axis=0, conc...  4.01 us
    dot_general x1, matrix products, scan_prompt(): jnp.einsum('cijh,cjhp->cihp', scores, values, precision=highest)  3.96 us
    dot_general x1, matrix products, scan_prompt(): jnp.einsum('cjhn,cjhp->cnhp', b_head * tail_decay[..., None], values, pre...  2.73 us
    dot_general x1, matrix products, scan_prompt(): jnp.einsum('cihn,cnhp->cihp', c_head, starts, precision=highest)  2.2 us
  transfers between devices with their start and end apart: 2, of which 1 were waited for; matrix products, arithmetic and copies ran while one was open for 49% of the time, Pallas kernels for 0%

commit v1 on v0

v1 whole, which is shorter than its diff:
```python
import functools

import jax
import jax.numpy as jnp
from jax import lax
from jax.experimental import pallas as pl
from jax.experimental.pallas import tpu as pltpu
from jax.sharding import PartitionSpec as P

H = 128
G = 4
epsilon = 1e-05
highest = lax.Precision.HIGHEST
f32 = jnp.float32
bf16 = jnp.bfloat16
LOG2E = 1.4426950408889634
CAP = 100.0


def softplus(v):
    return jnp.maximum(v, 0.0) + jnp.log1p(jnp.exp(-jnp.abs(v)))


def silu(z):
    half = 0.5 * z
    return half * (1.0 + jnp.tanh(half))


def split(v, parts):
    out = []
    for _ in range(parts):
        piece = v.astype(bf16)
        out.append(piece)
        v = v - piece.astype(f32)
    return out


def widen(v, width, parts):
    heads = v.shape[1]
    per = width // heads
    row = lax.broadcasted_iota(jnp.int32, (heads, width), 0)
    lane = lax.broadcasted_iota(jnp.int32, (heads, width), 1)
    pick = jnp.where((lane >= row * per) & (lane < (row + 1) * per), 1.0, 0.0).astype(bf16)
    lhs = jnp.concatenate(split(v, parts), axis=1)
    rhs = jnp.concatenate([pick] * parts, axis=0)
    return jnp.dot(lhs, rhs, preferred_element_type=f32)


def group_lanes(states, heads_here):
    start = (lax.axis_index("head") * heads_here) // (H // G)
    return pl.ds(pl.multiple_of(start * states, states), states)


def state_kernel(len_ref, x_ref, b_ref, dt_ref, s0_ref, a_ref, bias_ref, fs_ref, c_ref, r_ref):
    length, heads = dt_ref.shape
    width = x_ref.shape[1]
    states = s0_ref.shape[0]
    valid = lax.broadcasted_iota(jnp.int32, (length, heads), 0) < len_ref[0]
    delta = jnp.where(valid, softplus(dt_ref[...] + bias_ref[...]), 0.0)
    rate = delta * a_ref[...] * (-LOG2E)
    row = lax.broadcasted_iota(jnp.int32, (length, length), 0)
    lane = lax.broadcasted_iota(jnp.int32, (length, length), 1)
    lower = jnp.where(row >= lane, 1.0, 0.0).astype(bf16)
    sums = jnp.dot(
        jnp.concatenate([lower] * 3, axis=1),
        jnp.concatenate(split(rate, 3), axis=0),
        preferred_element_type=f32,
    )
    c_ref[...] = sums
    r_ref[...] = jnp.log2(delta) - sums
    last = sums[length - 1 :, :]
    weight = jnp.exp2(last - sums) * delta
    total = widen(jnp.exp2(last), width, 2)
    wide = widen(weight, width, 2)
    xw = (x_ref[...].astype(f32) * wide).astype(bf16)
    b = b_ref[:, group_lanes(states, heads)]
    fresh = lax.dot_general(b, xw, (((0,), (0,)), ((), ())), preferred_element_type=f32)
    fs_ref[...] = (fresh + total * s0_ref[...]).astype(bf16)


def read_kernel(*refs):
    n = (len(refs) - 1) // 2
    fs_ref = refs[0]
    states, width = fs_ref.shape
    heads = width // 64
    me = lax.axis_index("sample")
    lanes = group_lanes(states, heads)
    rows = []
    for k in range(n):
        block = refs[1 + k][:, lanes].astype(f32)
        mine = lax.broadcasted_iota(jnp.int32, block.shape, 0) == me
        rows.append(jnp.sum(jnp.where(mine, block, 0.0), axis=0, keepdims=True))
    q = jnp.concatenate(rows, axis=0).astype(bf16)
    reads = jnp.dot(q, fs_ref[...], preferred_element_type=f32)
    for k in range(n):
        refs[1 + n + k][...] = reads[k : k + 1, :]


def prompt_kernel(
    x_ref, z_ref, b_ref, cp_ref, s0_ref, c_ref, r_ref, skip_ref, gated_ref, sq_ref, m_ref
):
    length, heads = c_ref.shape
    states, width = s0_ref.shape
    per = width // heads
    lanes = group_lanes(states, heads)
    cp = cp_ref[:, lanes]
    scores = lax.dot_general(
        cp, b_ref[:, lanes], (((1,), (1,)), ((), ())), preferred_element_type=f32
    )
    row = lax.broadcasted_iota(jnp.int32, (length, length), 0)
    lane = lax.broadcasted_iota(jnp.int32, (length, length), 1)
    scores = jnp.where(row >= lane, scores, 0.0)
    m_ref[...] = jnp.dot(cp, s0_ref[...].astype(bf16), preferred_element_type=f32)
    skip = widen(skip_ref[...], width, 3)
    rt = r_ref[...].T
    c = c_ref[...]
    pair = 2 * per
    low = lax.broadcasted_iota(jnp.int32, (length, pair), 1) < per
    squares = jnp.zeros((length, pair), f32)
    for q in range(heads // 2):
        ch = slice(q * pair, (q + 1) * pair)
        x = x_ref[:, ch]
        xf = x.astype(f32)
        x_cat = jnp.concatenate(
            [jnp.where(low, xf, 0.0).astype(bf16), jnp.where(low, 0.0, xf).astype(bf16)], axis=0
        )
        parts = []
        cols = []
        for h in (2 * q, 2 * q + 1):
            col = jnp.broadcast_to(c[:, h : h + 1], (length, length))
            arg = jnp.minimum(col + rt[h : h + 1, :], CAP)
            parts.append((jnp.exp2(arg) * scores).astype(bf16))
            cols.append(col)
        y = jnp.dot(jnp.concatenate(parts, axis=1), x_cat, preferred_element_type=f32)
        decay = jnp.exp2(jnp.where(low, cols[0], cols[1]))
        y = y + decay * m_ref[:, ch] + skip[:, ch] * xf
        gated = y * silu(z_ref[:, ch].astype(f32))
        gated_ref[:, ch] = gated
        squares = squares + gated * gated
    total = jnp.broadcast_to(jnp.sum(squares, axis=1, keepdims=True), (length, length))
    sq_ref[...] = total.T[0:1, :]


def slot_kernel(*refs, states):
    (sq_ref, x_ref, z_ref, b_ref, c_ref, dt_ref, a_ref, bias_ref, skip_ref) = refs[:9]
    read_refs = refs[9:-2]
    gated_ref, pay_ref = refs[-2:]
    prompts, width = x_ref.shape
    heads = dt_ref.shape[1]
    me = lax.axis_index("sample")
    lanes = group_lanes(states, heads)
    step = softplus(dt_ref[...] + bias_ref[...])
    decay = jnp.exp(-step * a_ref[...])
    cb = jnp.sum(c_ref[:, lanes].astype(f32) * b_ref[:, lanes].astype(f32), axis=1, keepdims=True)
    gain = step * cb + skip_ref[...]
    wide = widen(jnp.concatenate([decay, gain], axis=0), width, 3)
    prompt = lax.broadcasted_iota(jnp.int32, (prompts, width), 0)
    reads = jnp.zeros((prompts, width), f32)
    for k, ref in enumerate(read_refs):
        reads = jnp.where(prompt == (me ^ k), ref[...], reads)
    mix = wide[:prompts] * reads + wide[prompts:] * x_ref[...].astype(f32)
    gated = mix * silu(z_ref[...].astype(f32))
    gated_ref[...] = gated
    total = jnp.broadcast_to(jnp.sum(gated * gated, axis=1, keepdims=True), (prompts, 128))
    row = lax.broadcasted_iota(jnp.int32, (prompts, 128), 0)
    lane = lax.broadcasted_iota(jnp.int32, (prompts, 128), 1)
    pay_ref[0:1, :] = sq_ref[...]
    pay_ref[1:2, :] = jnp.sum(jnp.where(row == lane, total, 0.0), axis=0, keepdims=True)


def norm_kernel(*refs, channels):
    len_ref, gated_ref, dec_ref, gain_ref = refs[:4]
    pay_refs = refs[4:-2]
    out_ref, out_dec_ref = refs[-2:]
    length = gated_ref.shape[0]
    prompts = dec_ref.shape[0]
    total = pay_refs[0][...]
    for ref in pay_refs[1:]:
        total = total + ref[...]
    scale = lax.rsqrt(total * (1.0 / channels) + epsilon)
    column = jnp.broadcast_to(scale[0:1, :], (length, length)).T[:, 0:1]
    valid = lax.broadcasted_iota(jnp.int32, (length, 1), 0) < len_ref[0]
    column = jnp.where(valid, column, 0.0)
    gain = gain_ref[...]
    out_ref[...] = (gated_ref[...] * column * gain).astype(bf16)
    row = lax.broadcasted_iota(jnp.int32, (prompts, 128), 0)
    lane = lax.broadcasted_iota(jnp.int32, (prompts, 128), 1)
    wide = jnp.broadcast_to(scale[1:2, :], (prompts, 128))
    dec = jnp.sum(jnp.where(row == lane, wide, 0.0), axis=1, keepdims=True)
    out_dec_ref[...] = (dec_ref[...] * dec * gain).astype(bf16)


smem = pl.BlockSpec(memory_space=pltpu.SMEM)
vmem = pl.BlockSpec(memory_space=pltpu.VMEM)


def call(kernel, name, ins, outs, smem_ins=0, scratch=()):
    return pl.pallas_call(
        kernel,
        name=name,
        in_specs=[smem] * smem_ins + [vmem] * (len(ins) - smem_ins),
        out_specs=tuple(vmem for _ in outs),
        out_shape=tuple(jax.ShapeDtypeStruct(s, d) for s, d in outs),
        scratch_shapes=list(scratch),
    )(*ins)


def make_body(mesh):
    samples = mesh.shape["sample"]
    head_parts = mesh.shape["head"]

    def swap(v, axis, k):
        return lax.ppermute(v, axis, [(i, i ^ k) for i in range(mesh.shape[axis])])

    def body(
        x_pre, z_pre, b_pre, c_pre, dt_pre, lengths, init_state, a_rates, dt_bias, skip_scale,
        norm_gain, x_dec, z_dec, b_dec, c_dec, dt_dec,
    ):
        length, width = x_pre.shape[1:]
        states = init_state.shape[1]
        heads = a_rates.shape[0]
        prompts = x_dec.shape[1]
        x, z, b, cp, dt, s0 = (v[0] for v in (x_pre, z_pre, b_pre, c_pre, dt_pre, init_state))
        xd, zd, bd, cd, dtd = (v[0] for v in (x_dec, z_dec, b_dec, c_dec, dt_dec))
        a, bias, skip = (v[None] for v in (a_rates, dt_bias, skip_scale))
        queries = [cd] + [swap(cd, "sample", k) for k in range(1, samples)]
        fs, c, r = call(
            state_kernel, "state", (lengths, x, b, dt, s0, a, bias),
            (((states, width), bf16), ((length, heads), f32), ((length, heads), f32)), 1,
        )
        reads = call(read_kernel, "read", (fs, *queries), (((1, width), f32),) * samples)
        reads = [reads[0]] + [swap(reads[k], "sample", k) for k in range(1, samples)]
        gated, sq = call(
            prompt_kernel, "prompt", (x, z, b, cp, s0, c, r, skip),
            (((length, width), f32), ((1, length), f32)), 0,
            (pltpu.VMEM((length, width), f32),),
        )
        gated_dec, pay = call(
            functools.partial(slot_kernel, states=states), "slot",
            (sq, xd, zd, bd, cd, dtd, a, bias, skip, *reads),
            (((prompts, width), f32), ((2, 128), f32)),
        )
        pays = [pay] + [swap(pay, "head", k) for k in range(1, head_parts)]
        out_pre, out_dec = call(
            functools.partial(norm_kernel, channels=width * head_parts), "norm",
            (lengths, gated, gated_dec, norm_gain[None], *pays),
            (((length, width), bf16), ((prompts, width), bf16)), 1,
        )
        return out_pre[None], fs[None], out_dec[None]

    return body


def solution(mesh):
    tokens = P(("rep", "sample"), None, "head")
    groups = P(("rep", "sample"), None, None)
    in_specs = (
        tokens, tokens, groups, groups, tokens, P(("rep", "sample")), tokens,
        P("head"), P("head"), P("head"), P("head"), tokens, tokens, groups, groups, tokens,
    )
    return jax.shard_map(
        make_body(mesh), mesh=mesh, in_specs=in_specs, out_specs=(tokens,) * 3, check_vma=False
    )
```

time: 62.1 us -> 33.9 us (0.55)
  local copies, waits for them, and re-layouts: 20.3 us -> 3.86 us
  Pallas kernels: 0 us -> 12.8 us
  matrix products: 9.71 us -> 0 us
  other arithmetic: 8.5 us -> 0 us
  blocking collectives: 5.63 us -> 0 us
    pallas_call x0 -> x5, Pallas kernels: none -> 12.8 us  [call(): pl.pallas_call(kernel, name=name, in_specs=[smem] * smem_ins + [vmem] * (...]
    ppermute x0 -> x9, starting transfers between devices: none -> 12 us  [swap(): return lax.ppermute(v, axis, [(i, i ^ k) for i in range(mesh.shape[axis])])]
    all_to_all x2 -> x0, starting transfers between devices: 11.4 us -> none  [the longest x1 6.35 us: body(): lax.all_to_all(c_dec, 'sample', split_axis=1, concat_axis=0, tiled=True)]
    dot_general x6 -> x0, matrix products: 9.71 us -> none  [the longest x1 3.96 us: scan_prompt(): jnp.einsum('cijh,cjhp->cihp', scores, values, precision=highest)]
    unnamed x72 -> x21, local copies, waits for them, and re-layouts: 9.6 us -> 3.86 us
    psum x1 -> x0, blocking collectives: 5.63 us -> none  [body(): pre_totals = lax.psum(jnp.sum(gated_rows * gated_rows, axis=-1), 'head')]
    gather x4 -> x0, local copies, waits for them, and re-layouts: 5.26 us -> none  [the longest x1 1.93 us: scan_prompt(): c_head = jnp.take(c_groups, owners, axis=2).astype(jnp.float32)]
    all_to_all x2 -> x0, waiting for transfers between devices: 4.02 us -> none  [the longest x1 4.01 us: body(): lax.all_to_all(answers.astype(jnp.bfloat16), 'sample', split_axis=0, conc...]
  transfers between devices with their start and end apart: 2 -> 9, of which waited for: 1 -> 3; matrix products, arithmetic and copies ran while one was open for 49% -> 4% of each run, Pallas kernels for 0% -> 20%
where the time goes in v1:
time: 33.9 us; the launch traced here: 33.5 us
  Pallas kernels  12.8 us (38%)
  starting transfers between devices  12 us (35%)
  local copies, waits for them, and re-layouts  3.86 us (11%)
  waiting for transfers between devices  3.43 us (10%)
  between operations  1.36 us (4%)
    pallas_call x5, Pallas kernels, call(): pl.pallas_call(kernel, name=name, in_specs=[smem] * smem_ins + [vmem] * (...  12.8 us
    ppermute x9, starting transfers between devices, swap(): return lax.ppermute(v, axis, [(i, i ^ k) for i in range(mesh.shape[axis])])  12 us
    unnamed x21, local copies, waits for them, and re-layouts  3.86 us
    ppermute x9, waiting for transfers between devices, swap(): return lax.ppermute(v, axis, [(i, i ^ k) for i in range(mesh.shape[axis])])  3.43 us
  transfers between devices with their start and end apart: 9, of which 3 were waited for; matrix products, arithmetic and copies ran while one was open for 4% of the time, Pallas kernels for 20%

profile of v1, /device:TPU:0, one launch (start us, length us, event | category | flops | bytes accessed | tf_op | source)
XLA Modules:
  0.0 33.5 jit_solution(5984359731030940939)
XLA Ops:
  0.6 5.1 %collective-permute-start.2 = (bf16[4,512]{1,0:T(4,128)(2,1)}, bf16[4,512]{1,0:T(4,128)(2,1)S(1)}, u32[]{:S(2)}, u32[]{:S(2)}) collective-permute-start(bf16[4,512]{1,0:T(4,128)(2,1)} %bitcast.28), channel_id=1, source_target_pairs={{0,12},{4,8},{8,4},{12,0},{1,13},{5,9},{9,5},{13,1},{2,14},{6,10},... | collective-permute-start | bytes 12296 | tf_op jit(solution)/shard_map/ppermute | solution.py:213
  5.8 0.0 collective-permute-start.1
  5.8 0.6 %collective-permute-start = (bf16[4,512]{1,0:T(4,128)(2,1)}, bf16[4,512]{1,0:T(4,128)(2,1)S(1)}, u32[]{:S(2)}, u32[]{:S(2)}) collective-permute-start(bf16[4,512]{1,0:T(4,128)(2,1)} %bitcast.30), channel_id=1, source_target_pairs={{0,4},{4,0},{8,12},{12,8},{1,5},{5,1},{9,13},{13,9},{2,6},{6,2},{1... | collective-permute-start | bytes 12296 | tf_op jit(solution)/shard_map/ppermute | solution.py:213
  7.1 1.4 %copy.19 = f32[1,128,32]{2,1,0:T(8,128)} copy(f32[1,128,32]{1,2,0:T(8,128)} %param.20) | data formatting | bytes 32768 | tf_op args[4]
  8.5 3.0 %state.1 = (bf16[128,2048]{1,0:T(8,128)(2,1)}, f32[128,32]{1,0:T(8,128)}, f32[128,32]{1,0:T(8,128)}) custom-call(s32[1]{0:T(128)S(6)} %copy.20.len_ref.refs_0_, bf16[128,2048]{1,0:T(8,128)(2,1)} %bitcast.20, bf16[128,512]{1,0:T(8,128)(2,1)} %bitcast.24, f32[128,32]{1,0:T(8,128)} %bitcast.26, f32[128,2048]{1,0:T(8,128)} %bitcast.18, f32[1,32]{1,0:T(1,128)} %bitcast.37, ...), custom_call_target="tpu_custom_call" | custom-call | tf_op jit(solution)/shard_map/state/pallas_call | solution.py:198
  11.6 0.5 %copy-done.3 = bf16[4,512]{1,0:T(4,128)(2,1)} copy-done((bf16[4,512]{1,0:T(4,128)(2,1)}, bf16[4,512]{1,0:T(4,128)(2,1)S(1)}, u32[]{:S(2)}) %copy-start.3) | copy-done | bytes 4120
  12.1 0.0 copy-done.4
  12.1 0.0 copy-done.5
  12.1 1.9 %read.1 = (f32[1,2048]{1,0:T(1,128)}, f32[1,2048]{1,0:T(1,128)}, f32[1,2048]{1,0:T(1,128)}, f32[1,2048]{1,0:T(1,128)}) custom-call(bf16[128,2048]{1,0:T(8,128)(2,1)} %get-tuple-element.20.refs_0_, bf16[4,512]{1,0:T(4,128)(2,1)} %bitcast.31, bf16[4,512]{1,0:T(4,128)(2,1)} %copy-done.5, bf16[4,512]{1,0:T(4,128)(2,1)} %copy-done.4, bf16[4,512]{1,0:T(4,128)(2,1)} %copy-done.3), custom_call_target="tpu_custom_call" | custom-call | tf_op jit(solution)/shard_map/read/pallas_call | solution.py:198
  14.0 1.4 %collective-permute-start.3 = (f32[1,2048]{1,0:T(1,128)}, f32[1,2048]{1,0:T(1,128)S(1)}, u32[]{:S(2)}, u32[]{:S(2)}) collective-permute-start(f32[1,2048]{1,0:T(1,128)} %get-tuple-element.22), channel_id=1, source_target_pairs={{0,4},{4,0},{8,12},{12,8},{1,5},{5,1},{9,13},{13,9},{2,6},{6,2},{1... | collective-permute-start | bytes 24584 | tf_op jit(solution)/shard_map/ppermute | solution.py:213
  15.4 2.9 %collective-permute-start.4 = (f32[1,2048]{1,0:T(1,128)}, f32[1,2048]{1,0:T(1,128)S(1)}, u32[]{:S(2)}, u32[]{:S(2)}) collective-permute-start(f32[1,2048]{1,0:T(1,128)} %get-tuple-element.23), channel_id=1, source_target_pairs={{0,8},{4,12},{8,0},{12,4},{1,9},{5,13},{9,1},{13,5},{2,10},{6,14},... | collective-permute-start | bytes 24584 | tf_op jit(solution)/shard_map/ppermute | solution.py:213
  18.3 0.1 collective-permute-start.5
  18.4 3.8 %prompt.1 = (f32[128,2048]{1,0:T(8,128)}, f32[1,128]{1,0:T(1,128)}) custom-call(bf16[128,2048]{1,0:T(8,128)(2,1)} %bitcast.21, bf16[128,2048]{1,0:T(8,128)(2,1)} %bitcast.23, bf16[128,512]{1,0:T(8,128)(2,1)} %bitcast.25, bf16[128,512]{1,0:T(8,128)(2,1)} %bitcast.27, f32[128,2048]{1,0:T(8,128)} %bitcast.19, f32[128,32]{1,0:T(8,128)} %get-tuple-element.16.c_ref, ...), custom_call_target="tpu_custom_call" | custom-call | tf_op jit(solution)/shard_map/prompt/pallas_call | solution.py:198
  22.3 1.7 %collective-permute-done.5.refs_12_ = f32[1,2048]{1,0:T(1,128)S(1)} collective-permute-done((f32[1,2048]{1,0:T(1,128)}, f32[1,2048]{1,0:T(1,128)S(1)}, u32[]{:S(2)}, u32[]{:S(2)}) %collective-permute-start.5) | collective-permute-done | bytes 8224 | tf_op jit(solution)/shard_map/ppermute | solution.py:213
  24.0 0.6 %copy-done.2 = f32[1,2048]{1,0:T(1,128)} copy-done((f32[1,2048]{1,0:T(1,128)}, f32[1,2048]{1,0:T(1,128)S(1)}, u32[]{:S(2)}) %copy-start.2) | copy-done | bytes 8216
  24.6 1.8 %slot.1 = (f32[4,2048]{1,0:T(4,128)}, f32[2,128]{1,0:T(2,128)}) custom-call(f32[1,128]{1,0:T(1,128)} %get-tuple-element.19.refs_0_, bf16[4,2048]{1,0:T(4,128)(2,1)} %bitcast.33, bf16[4,2048]{1,0:T(4,128)(2,1)} %bitcast.34, bf16[4,512]{1,0:T(4,128)(2,1)} %bitcast.36, bf16[4,512]{1,0:T(4,128)(2,1)} %bitcast.32, f32[4,32]{1,0:T(4,128)} %bitcast.41, ...), custom_call_target="tpu_custom_call" | custom-call | tf_op jit(solution)/shard_map/slot/pallas_call | solution.py:198
  26.4 0.7 %copy-done.6 = f32[2,128]{1,0:T(2,128)S(1)} copy-done((f32[2,128]{1,0:T(2,128)S(1)}, f32[2,128]{1,0:T(2,128)}, u32[]{:S(2)}) %copy-start.6) | copy-done | bytes 1048
  27.1 1.5 %collective-permute-start.7 = (f32[2,128]{1,0:T(2,128)S(1)}, f32[2,128]{1,0:T(2,128)S(1)}, u32[]{:S(2)}, u32[]{:S(2)}) collective-permute-start(f32[2,128]{1,0:T(2,128)S(1)} %copy-done.6), channel_id=1, source_target_pairs={{0,2},{1,3},{2,0},{3,1},{4,6},{5,7},{6,4},{7,5},{8,10},{9,11},{10,... | collective-permute-start | bytes 3080 | tf_op jit(solution)/shard_map/ppermute | solution.py:213
  28.5 0.4 %collective-permute-start.6 = (f32[2,128]{1,0:T(2,128)S(1)}, f32[2,128]{1,0:T(2,128)S(1)}, u32[]{:S(2)}, u32[]{:S(2)}) collective-permute-start(f32[2,128]{1,0:T(2,128)S(1)} %copy-done.6), channel_id=1, source_target_pairs={{0,1},{1,0},{2,3},{3,2},{4,5},{5,4},{6,7},{7,6},{8,9},{9,8},{10,11... | collective-permute-start | bytes 3080 | tf_op jit(solution)/shard_map/ppermute | solution.py:213
  28.9 1.1 %collective-permute-done.8.refs_7_ = f32[2,128]{1,0:T(2,128)S(1)} collective-permute-done((f32[2,128]{1,0:T(2,128)S(1)}, f32[2,128]{1,0:T(2,128)S(1)}, u32[]{:S(2)}, u32[]{:S(2)}) %collective-permute-start.8) | collective-permute-done | bytes 1056 | tf_op jit(solution)/shard_map/ppermute | solution.py:213
  30.1 0.6 %collective-permute-done.7.refs_6_ = f32[2,128]{1,0:T(2,128)S(1)} collective-permute-done((f32[2,128]{1,0:T(2,128)S(1)}, f32[2,128]{1,0:T(2,128)S(1)}, u32[]{:S(2)}, u32[]{:S(2)}) %collective-permute-start.7) | collective-permute-done | bytes 1056 | tf_op jit(solution)/shard_map/ppermute | solution.py:213
  30.6 0.6 %copy-done.8 = f32[2,128]{1,0:T(2,128)} copy-done((f32[2,128]{1,0:T(2,128)}, f32[2,128]{1,0:T(2,128)S(1)}, u32[]{:S(2)}) %copy-start.8) | copy-done | bytes 1048
  31.2 0.0 copy-done.9
  31.2 2.3 %norm.1 = (bf16[128,2048]{1,0:T(8,128)(2,1)}, bf16[4,2048]{1,0:T(4,128)(2,1)}) custom-call(s32[1]{0:T(128)S(6)} %copy.20.len_ref.refs_0_, f32[128,2048]{1,0:T(8,128)} %get-tuple-element.18.refs_1_, f32[4,2048]{1,0:T(4,128)} %get-tuple-element.25.refs_2_, f32[1,2048]{1,0:T(1,128)} %bitcast.35, f32[2,128]{1,0:T(2,128)} %get-tuple-element.26.refs_4_, ...), custom_call_target="tpu_custom_call" | custom-call | tf_op jit(solution)/shard_map/norm/pallas_call | solution.py:198
  (20 shorter events, 0.0 us)
Async XLA Ops:
  0.6 10.9 %collective-permute-start.2 = (bf16[4,512]{1,0:T(4,128)(2,1)}, bf16[4,512]{1,0:T(4,128)(2,1)S(1)}, u32[]{:S(2)}, u32[]{:S(2)}) collective-permute-start(bf16[4,512]{1,0:T(4,128)(2,1)} %bitcast.28), channel_id=1, source_target_pairs={{0,12},{4,8},{8,4},{12,0},{1,13},{5,9},{9,5},{13,1},{2,14},{6,10},... | collective-permute-start | bytes 12296 | tf_op jit(solution)/shard_map/ppermute | solution.py:213
  5.8 5.7 %collective-permute-start.1 = (bf16[4,512]{1,0:T(4,128)(2,1)}, bf16[4,512]{1,0:T(4,128)(2,1)S(1)}, u32[]{:S(2)}, u32[]{:S(2)}) collective-permute-start(bf16[4,512]{1,0:T(4,128)(2,1)} %bitcast.29), channel_id=1, source_target_pairs={{0,8},{4,12},{8,0},{12,4},{1,9},{5,13},{9,1},{13,5},{2,10},{6,14},... | collective-permute-start | bytes 12296 | tf_op jit(solution)/shard_map/ppermute | solution.py:213
  5.8 5.8 %collective-permute-start = (bf16[4,512]{1,0:T(4,128)(2,1)}, bf16[4,512]{1,0:T(4,128)(2,1)S(1)}, u32[]{:S(2)}, u32[]{:S(2)}) collective-permute-start(bf16[4,512]{1,0:T(4,128)(2,1)} %bitcast.30), channel_id=1, source_target_pairs={{0,4},{4,0},{8,12},{12,8},{1,5},{5,1},{9,13},{13,9},{2,6},{6,2},{1... | collective-permute-start | bytes 12296 | tf_op jit(solution)/shard_map/ppermute | solution.py:213
  11.5 0.6 %copy-start.3 = (bf16[4,512]{1,0:T(4,128)(2,1)}, bf16[4,512]{1,0:T(4,128)(2,1)S(1)}, u32[]{:S(2)}) copy-start(bf16[4,512]{1,0:T(4,128)(2,1)S(1)} %collective-permute-done.2.refs_4_) | copy-start | bytes 12292
  11.5 0.6 %copy-start.4 = (bf16[4,512]{1,0:T(4,128)(2,1)}, bf16[4,512]{1,0:T(4,128)(2,1)S(1)}, u32[]{:S(2)}) copy-start(bf16[4,512]{1,0:T(4,128)(2,1)S(1)} %collective-permute-done.1.refs_3_) | copy-start | bytes 12292
  11.5 0.6 %copy-start.5 = (bf16[4,512]{1,0:T(4,128)(2,1)}, bf16[4,512]{1,0:T(4,128)(2,1)S(1)}, u32[]{:S(2)}) copy-start(bf16[4,512]{1,0:T(4,128)(2,1)S(1)} %collective-permute-done.refs_2_) | copy-start | bytes 12292
  14.0 8.2 %collective-permute-start.3 = (f32[1,2048]{1,0:T(1,128)}, f32[1,2048]{1,0:T(1,128)S(1)}, u32[]{:S(2)}, u32[]{:S(2)}) collective-permute-start(f32[1,2048]{1,0:T(1,128)} %get-tuple-element.22), channel_id=1, source_target_pairs={{0,4},{4,0},{8,12},{12,8},{1,5},{5,1},{9,13},{13,9},{2,6},{6,2},{1... | collective-permute-start | bytes 24584 | tf_op jit(solution)/shard_map/ppermute | solution.py:213
  15.4 6.9 %collective-permute-start.4 = (f32[1,2048]{1,0:T(1,128)}, f32[1,2048]{1,0:T(1,128)S(1)}, u32[]{:S(2)}, u32[]{:S(2)}) collective-permute-start(f32[1,2048]{1,0:T(1,128)} %get-tuple-element.23), channel_id=1, source_target_pairs={{0,8},{4,12},{8,0},{12,4},{1,9},{5,13},{9,1},{13,5},{2,10},{6,14},... | collective-permute-start | bytes 24584 | tf_op jit(solution)/shard_map/ppermute | solution.py:213
  18.3 5.7 %collective-permute-start.5 = (f32[1,2048]{1,0:T(1,128)}, f32[1,2048]{1,0:T(1,128)S(1)}, u32[]{:S(2)}, u32[]{:S(2)}) collective-permute-start(f32[1,2048]{1,0:T(1,128)} %get-tuple-element.24), channel_id=1, source_target_pairs={{0,12},{4,8},{8,4},{12,0},{1,13},{5,9},{9,5},{13,1},{2,14},{6,10},... | collective-permute-start | bytes 24584 | tf_op jit(solution)/shard_map/ppermute | solution.py:213
  22.2 1.7 %copy-start = (f32[1,2048]{1,0:T(1,128)}, f32[1,2048]{1,0:T(1,128)S(1)}, u32[]{:S(2)}) copy-start(f32[1,2048]{1,0:T(1,128)S(1)} %collective-permute-done.3.refs_10_) | copy-start | bytes 24580
  22.3 1.7 %copy-start.1 = (f32[1,2048]{1,0:T(1,128)}, f32[1,2048]{1,0:T(1,128)S(1)}, u32[]{:S(2)}) copy-start(f32[1,2048]{1,0:T(1,128)S(1)} %collective-permute-done.4.refs_11_) | copy-start | bytes 24580
  24.0 0.6 %copy-start.2 = (f32[1,2048]{1,0:T(1,128)}, f32[1,2048]{1,0:T(1,128)S(1)}, u32[]{:S(2)}) copy-start(f32[1,2048]{1,0:T(1,128)S(1)} %collective-permute-done.5.refs_12_) | copy-start | bytes 24580
  26.4 0.7 %copy-start.6 = (f32[2,128]{1,0:T(2,128)S(1)}, f32[2,128]{1,0:T(2,128)}, u32[]{:S(2)}) copy-start(f32[2,128]{1,0:T(2,128)} %get-tuple-element.26.refs_4_) | copy-start | bytes 3076
  27.0 3.0 %collective-permute-start.8 = (f32[2,128]{1,0:T(2,128)S(1)}, f32[2,128]{1,0:T(2,128)S(1)}, u32[]{:S(2)}, u32[]{:S(2)}) collective-permute-start(f32[2,128]{1,0:T(2,128)S(1)} %copy-done.6), channel_id=1, source_target_pairs={{0,3},{1,2},{2,1},{3,0},{4,7},{5,6},{6,5},{7,4},{8,11},{9,10},{10,... | collective-permute-start | bytes 3080 | tf_op jit(solution)/shard_map/ppermute | solution.py:213
  27.1 3.6 %collective-permute-start.7 = (f32[2,128]{1,0:T(2,128)S(1)}, f32[2,128]{1,0:T(2,128)S(1)}, u32[]{:S(2)}, u32[]{:S(2)}) collective-permute-start(f32[2,128]{1,0:T(2,128)S(1)} %copy-done.6), channel_id=1, source_target_pairs={{0,2},{1,3},{2,0},{3,1},{4,6},{5,7},{6,4},{7,5},{8,10},{9,11},{10,... | collective-permute-start | bytes 3080 | tf_op jit(solution)/shard_map/ppermute | solution.py:213
  28.5 2.1 %collective-permute-start.6 = (f32[2,128]{1,0:T(2,128)S(1)}, f32[2,128]{1,0:T(2,128)S(1)}, u32[]{:S(2)}, u32[]{:S(2)}) collective-permute-start(f32[2,128]{1,0:T(2,128)S(1)} %copy-done.6), channel_id=1, source_target_pairs={{0,1},{1,0},{2,3},{3,2},{4,5},{5,4},{6,7},{7,6},{8,9},{9,8},{10,11... | collective-permute-start | bytes 3080 | tf_op jit(solution)/shard_map/ppermute | solution.py:213
  30.0 0.6 %copy-start.7 = (f32[2,128]{1,0:T(2,128)}, f32[2,128]{1,0:T(2,128)S(1)}, u32[]{:S(2)}) copy-start(f32[2,128]{1,0:T(2,128)S(1)} %collective-permute-done.8.refs_7_) | copy-start | bytes 3076
  30.6 0.6 %copy-start.8 = (f32[2,128]{1,0:T(2,128)}, f32[2,128]{1,0:T(2,128)S(1)}, u32[]{:S(2)}) copy-start(f32[2,128]{1,0:T(2,128)S(1)} %collective-permute-done.7.refs_6_) | copy-start | bytes 3076
  30.6 0.6 %copy-start.9 = (f32[2,128]{1,0:T(2,128)}, f32[2,128]{1,0:T(2,128)S(1)}, u32[]{:S(2)}) copy-start(f32[2,128]{1,0:T(2,128)S(1)} %collective-permute-done.6.refs_5_) | copy-start | bytes 3076

commit v2 on v1

v2 whole, which is shorter than its diff:
```python
import functools

import jax
import jax.numpy as jnp
from jax import lax
from jax.experimental import pallas as pl
from jax.experimental.pallas import tpu as pltpu
from jax.sharding import PartitionSpec as P

H = 128
G = 4
epsilon = 1e-05
highest = lax.Precision.HIGHEST
f32 = jnp.float32
bf16 = jnp.bfloat16
LOG2E = 1.4426950408889634
CAP = 100.0
CHUNKS = 4
GRANT = 16 << 20


def softplus(v):
    return jnp.maximum(v, 0.0) + jnp.log1p(jnp.exp(-jnp.abs(v)))


def silu(z):
    half = 0.5 * z
    return half * (1.0 + jnp.tanh(half))


def split(v, parts):
    out = []
    for _ in range(parts):
        piece = v.astype(bf16)
        out.append(piece)
        v = v - piece.astype(f32)
    return out


def widen(v, width, parts):
    heads = v.shape[1]
    per = width // heads
    row = lax.broadcasted_iota(jnp.int32, (heads, width), 0)
    lane = lax.broadcasted_iota(jnp.int32, (heads, width), 1)
    pick = jnp.where((lane >= row * per) & (lane < (row + 1) * per), 1.0, 0.0).astype(bf16)
    lhs = jnp.concatenate(split(v, parts), axis=1)
    rhs = jnp.concatenate([pick] * parts, axis=0)
    return jnp.dot(lhs, rhs, preferred_element_type=f32)


def group_lanes(states, heads_here):
    start = (lax.axis_index("head") * heads_here) // (H // G)
    return pl.ds(pl.multiple_of(start * states, states), states)


def as_column(row):
    n = row.shape[1]
    wide = jnp.broadcast_to(row, (n, n))
    here = lax.broadcasted_iota(jnp.int32, (n, n), 0) == lax.broadcasted_iota(jnp.int32, (n, n), 1)
    return jnp.sum(jnp.where(here, wide, 0.0), axis=1, keepdims=True)


def widen_columns(v, width, parts):
    heads = v.shape[0]
    per = width // heads
    row = lax.broadcasted_iota(jnp.int32, (heads, width), 0)
    lane = lax.broadcasted_iota(jnp.int32, (heads, width), 1)
    pick = jnp.where((lane >= row * per) & (lane < (row + 1) * per), 1.0, 0.0).astype(bf16)
    lhs = jnp.concatenate(split(v, parts), axis=0)
    rhs = jnp.concatenate([pick] * parts, axis=0)
    return lax.dot_general(lhs, rhs, (((0,), (0,)), ((), ())), preferred_element_type=f32)


def state_kernel(
    len_hbm, dt_hbm, a_hbm, bias_hbm, x_hbm, b_hbm, s0_hbm, z_hbm, cp_hbm,
    fs_ref, c_ref, r_ref, valid_ref, x_ref, b_ref, s0_ref, z_ref, cp_ref,
    len_ref, dt_ref, a_ref, bias_ref, sems,
):
    heads, length = dt_ref.shape
    width = x_ref.shape[1]
    states = s0_ref.shape[0]
    lanes = group_lanes(states, heads)
    copies = [
        pltpu.make_async_copy(source, target, sems.at[i])
        for i, (source, target) in enumerate((
            (len_hbm, len_ref), (dt_hbm, dt_ref), (a_hbm, a_ref), (bias_hbm, bias_ref),
            (x_hbm, x_ref), (b_hbm.at[:, lanes], b_ref), (s0_hbm, s0_ref),
            (z_hbm, z_ref), (cp_hbm.at[:, lanes], cp_ref),
        ))
    ]
    for copy in copies:
        copy.start()
    row = lax.broadcasted_iota(jnp.int32, (length, length), 0)
    lane = lax.broadcasted_iota(jnp.int32, (length, length), 1)
    upper = jnp.where(row <= lane, 1.0, 0.0).astype(bf16)
    for copy in copies[:4]:
        copy.wait()
    valid = lax.broadcasted_iota(jnp.int32, (heads, length), 1) < len_ref[0]
    delta = jnp.where(valid, softplus(dt_ref[...] + as_column(bias_ref[...])), 0.0)
    rate = delta * as_column(a_ref[...]) * (-LOG2E)
    sums = jnp.dot(
        jnp.concatenate(split(rate, 3), axis=1),
        jnp.concatenate([upper] * 3, axis=0),
        preferred_element_type=f32,
    )
    rows = lax.broadcasted_iota(jnp.int32, valid_ref.shape, 0)
    valid_ref[...] = jnp.where(rows < len_ref[0], 1.0, 0.0)
    c_ref[...] = sums.T
    r_ref[...] = jnp.log2(delta) - sums
    last = sums[:, length - 1 :]
    weight = jnp.exp2(last - sums) * delta
    total = widen_columns(jnp.broadcast_to(jnp.exp2(last), (heads, 8)), width, 2)[0:1, :]
    wide = widen_columns(weight, width, 2)
    copies[4].wait()
    copies[5].wait()
    xw = (x_ref[...].astype(f32) * wide).astype(bf16)
    fresh = lax.dot_general(b_ref[...], xw, (((0,), (0,)), ((), ())), preferred_element_type=f32)
    copies[6].wait()
    fs_ref[...] = (fresh + total * s0_ref[...]).astype(bf16)
    copies[7].wait()
    copies[8].wait()


def read_kernel(*refs):
    n = (len(refs) - 1) // 2
    fs_ref = refs[0]
    states, width = fs_ref.shape
    heads = width // 64
    me = lax.axis_index("sample")
    lanes = group_lanes(states, heads)
    rows = []
    for k in range(n):
        block = refs[1 + k][:, lanes].astype(f32)
        mine = lax.broadcasted_iota(jnp.int32, block.shape, 0) == me
        rows.append(jnp.sum(jnp.where(mine, block, 0.0), axis=0, keepdims=True))
    q = jnp.concatenate(rows, axis=0).astype(bf16)
    reads = jnp.dot(q, fs_ref[...], preferred_element_type=f32)
    for k in range(n):
        refs[1 + n + k][...] = reads[k : k + 1, :]


def prompt_kernel(
    fs_ref, x_ref, z_ref, b_ref, cp_ref, s0_ref, c_ref, r_ref, skip_ref, gain_ref,
    xd_ref, zd_ref, bd_ref, cd_ref, dtd_ref, a_ref, bias_ref,
    gated_ref, sq_ref, u_ref, v_ref, fs_hbm, m_ref, sem,
):
    length, heads = c_ref.shape
    states, width = s0_ref.shape
    per = width // heads
    prompts = xd_ref.shape[0]
    lanes = group_lanes(states, heads)
    store = pltpu.make_async_copy(fs_ref, fs_hbm, sem)
    store.start()
    cp = cp_ref[...]
    scores = lax.dot_general(cp, b_ref[...], (((1,), (1,)), ((), ())), preferred_element_type=f32)
    row = lax.broadcasted_iota(jnp.int32, (length, length), 0)
    lane = lax.broadcasted_iota(jnp.int32, (length, length), 1)
    scores = jnp.where(row >= lane, scores, 0.0)
    m_ref[...] = jnp.dot(cp, s0_ref[...].astype(bf16), preferred_element_type=f32)

    step = softplus(dtd_ref[...] + bias_ref[...])
    cb = cd_ref[:, lanes].astype(f32) * bd_ref[:, lanes].astype(f32)
    cb = jnp.sum(cb, axis=1, keepdims=True)
    gain = step * cb + skip_ref[...]
    skips = jnp.broadcast_to(skip_ref[...], (8, heads))
    wide = widen(jnp.concatenate([jnp.exp(-step * a_ref[...]), gain], axis=0), width, 3)
    skip = widen(skips, width, 3)[0:1, :]
    gate = silu(zd_ref[...].astype(f32))
    u_ref[...] = wide[:prompts] * gate
    v_ref[...] = wide[prompts:] * xd_ref[...].astype(f32) * gate

    rt = r_ref[...]
    c = c_ref[...]
    pair = 2 * per
    low = lax.broadcasted_iota(jnp.int32, (length, pair), 1) < per
    squares = jnp.zeros((length, pair), f32)
    for q in range(heads // 2):
        ch = slice(q * pair, (q + 1) * pair)
        x = x_ref[:, ch]
        xf = x.astype(f32)
        x_cat = jnp.concatenate(
            [jnp.where(low, xf, 0.0).astype(bf16), jnp.where(low, 0.0, xf).astype(bf16)], axis=0
        )
        parts = []
        cols = []
        for h in (2 * q, 2 * q + 1):
            col = jnp.broadcast_to(c[:, h : h + 1], (length, length))
            arg = jnp.minimum(col + rt[h : h + 1, :], CAP)
            parts.append((jnp.exp2(arg) * scores).astype(bf16))
            cols.append(col)
        y = jnp.dot(jnp.concatenate(parts, axis=1), x_cat, preferred_element_type=f32)
        decay = jnp.exp2(jnp.where(low, cols[0], cols[1]))
        y = y + decay * m_ref[:, ch] + skip[:, ch] * xf
        gated = y * silu(z_ref[:, ch].astype(f32))
        gated_ref[:, ch] = gated * gain_ref[:, ch]
        squares = squares + gated * gated
    total = jnp.broadcast_to(jnp.sum(squares, axis=1, keepdims=True), (length, length))
    sq_ref[...] = total.T[0:1, :]
    store.wait()


def slot_kernel(*refs):
    sq_ref, u_ref, v_ref = refs[:3]
    read_refs = refs[3:-2]
    gated_ref, pay_ref = refs[-2:]
    prompts, width = u_ref.shape
    me = lax.axis_index("sample")
    prompt = lax.broadcasted_iota(jnp.int32, (prompts, width), 0)
    reads = jnp.zeros((prompts, width), f32)
    for k, ref in enumerate(read_refs):
        reads = jnp.where(prompt == (me ^ k), ref[...], reads)
    gated = u_ref[...] * reads + v_ref[...]
    gated_ref[...] = gated
    total = jnp.broadcast_to(jnp.sum(gated * gated, axis=1, keepdims=True), (prompts, 128))
    row = lax.broadcasted_iota(jnp.int32, (prompts, 128), 0)
    lane = lax.broadcasted_iota(jnp.int32, (prompts, 128), 1)
    pay_ref[0:1, :] = sq_ref[...]
    pay_ref[1:2, :] = jnp.sum(jnp.where(row == lane, total, 0.0), axis=0, keepdims=True)


def norm_kernel(*refs, channels, payloads):
    valid_ref, gated_ref, dec_ref, gain_ref = refs[:4]
    pay_refs = refs[4 : 4 + payloads]
    out_hbm, dec_hbm, out_ref, out_dec_ref, sems = refs[4 + payloads :]
    length = gated_ref.shape[0]
    prompts = dec_ref.shape[0]
    total = pay_refs[0][...]
    for ref in pay_refs[1:]:
        total = total + ref[...]
    scale = lax.rsqrt(total * (1.0 / channels) + epsilon)
    row = lax.broadcasted_iota(jnp.int32, (prompts, 128), 0)
    lane = lax.broadcasted_iota(jnp.int32, (prompts, 128), 1)
    wide = jnp.broadcast_to(scale[1:2, :], (prompts, 128))
    dec = jnp.sum(jnp.where(row == lane, wide, 0.0), axis=1, keepdims=True)
    out_dec_ref[...] = (dec_ref[...] * dec * gain_ref[...]).astype(bf16)
    copies = [pltpu.make_async_copy(out_dec_ref, dec_hbm, sems.at[0])]
    copies[0].start()
    column = jnp.broadcast_to(scale[0:1, :], (length, length)).T * valid_ref[...]
    column = column[:, 0:1]
    for i in range(CHUNKS):
        rows = slice(i * length // CHUNKS, (i + 1) * length // CHUNKS)
        out_ref[rows, :] = (gated_ref[rows, :] * column[rows, :]).astype(bf16)
        copies.append(
            pltpu.make_async_copy(out_ref.at[rows, :], out_hbm.at[rows, :], sems.at[1 + i])
        )
        copies[-1].start()
    for copy in copies:
        copy.wait()


VMEM = pltpu.MemorySpace.VMEM
HBM = pltpu.MemorySpace.HBM


def call(kernel, name, ins, outs, scratch=(), far=(), fetch=False):
    space = HBM if fetch else VMEM
    outs = [(VMEM, *out) for out in outs] + [(HBM, *out) for out in far]
    return pl.pallas_call(
        kernel,
        name=name,
        in_specs=[pl.BlockSpec(memory_space=pl.ANY if v.size == 1 else space) for v in ins],
        out_specs=tuple(pl.BlockSpec(memory_space=out[0]) for out in outs),
        out_shape=tuple(out[0](*out[1:]) for out in outs),
        scratch_shapes=list(scratch),
        compiler_params=pltpu.CompilerParams(vmem_limit_bytes=GRANT),
    )(*(v if v.size == 1 else pltpu.with_memory_space_constraint(v, space) for v in ins))


def make_body(mesh):
    samples = mesh.shape["sample"]
    head_parts = mesh.shape["head"]

    def swap(v, axis, k):
        return lax.ppermute(v, axis, [(i, i ^ k) for i in range(mesh.shape[axis])])

    def body(
        x_pre, z_pre, b_pre, c_pre, dt_pre, lengths, init_state, a_rates, dt_bias, skip_scale,
        norm_gain, x_dec, z_dec, b_dec, c_dec, dt_dec,
    ):
        length, width = x_pre.shape[1:]
        states = init_state.shape[1]
        heads = a_rates.shape[0]
        prompts = x_dec.shape[1]
        x, z, b, cp, dt, s0 = (v[0] for v in (x_pre, z_pre, b_pre, c_pre, dt_pre, init_state))
        xd, zd, bd, cd, dtd = (v[0] for v in (x_dec, z_dec, b_dec, c_dec, dt_dec))
        a, bias, skip, gain = (v[None] for v in (a_rates, dt_bias, skip_scale, norm_gain))
        queries = [cd] + [swap(cd, "sample", k) for k in range(1, samples)]
        fs, c, r, valid, x, b, s0, z, cp = call(
            state_kernel, "state", (lengths, dt.T, a, bias, x, b, s0, z, cp),
            (
                ((states, width), bf16), ((length, heads), f32), ((heads, length), f32),
                ((length, 128), f32), ((length, width), bf16), ((length, states), bf16), ((states, width), f32),
                ((length, width), bf16), ((length, states), bf16),
            ),
            (
                pltpu.SMEM((1,), jnp.int32), pltpu.VMEM((heads, length), f32),
                pltpu.VMEM((1, heads), f32), pltpu.VMEM((1, heads), f32),
                pltpu.SemaphoreType.DMA((9,)),
            ), fetch=True,
        )
        reads = call(read_kernel, "read", (fs, *queries), (((1, width), f32),) * samples)
        reads = [reads[0]] + [swap(reads[k], "sample", k) for k in range(1, samples)]
        gated, sq, u, v, fs = call(
            prompt_kernel, "prompt",
            (fs, x, z, b, cp, s0, c, r, skip, gain, xd, zd, bd, cd, dtd, a, bias),
            (((length, width), f32), ((1, length), f32)) + (((prompts, width), f32),) * 2,
            (pltpu.VMEM((length, width), f32), pltpu.SemaphoreType.DMA(())),
            (((states, width), bf16),),
        )
        gated_dec, pay = call(
            slot_kernel, "slot", (sq, u, v, *reads), (((prompts, width), f32), ((2, 128), f32))
        )
        pays = [pay] + [swap(pay, "head", k) for k in range(1, head_parts)]
        out_pre, out_dec = call(
            functools.partial(norm_kernel, channels=width * head_parts, payloads=head_parts),
            "norm", (valid, gated, gated_dec, gain, *pays), (),
            (
                pltpu.VMEM((length, width), bf16), pltpu.VMEM((prompts, width), bf16),
                pltpu.SemaphoreType.DMA((1 + CHUNKS,)),
            ), (((length, width), bf16), ((prompts, width), bf16)),
        )
        return out_pre[None], fs[None], out_dec[None]

    return body


def solution(mesh):
    tokens = P(("rep", "sample"), None, "head")
    groups = P(("rep", "sample"), None, None)
    in_specs = (
        tokens, tokens, groups, groups, tokens, P(("rep", "sample")), tokens,
        P("head"), P("head"), P("head"), P("head"), tokens, tokens, groups, groups, tokens,
    )
    return jax.shard_map(
        make_body(mesh), mesh=mesh, in_specs=in_specs, out_specs=(tokens,) * 3, check_vma=False
    )
```

time: 33.9 us -> 25.3 us (0.75)
  Pallas kernels: 12.8 us -> 5.25 us
  local copies, waits for them, and re-layouts: 3.86 us -> 0.69 us
  waiting for transfers between devices: 3.43 us -> 5.7 us
    pallas_call x5, Pallas kernels: 12.8 us -> 5.25 us  [call(): pl.pallas_call(kernel, name=name, in_specs=[pl.BlockSpec(memory_space=pl....]
    unnamed x21 -> x18, local copies, waits for them, and re-layouts: 3.86 us -> 0.69 us
    ppermute x9, waiting for transfers between devices: 3.43 us -> 5.7 us  [swap(): return lax.ppermute(v, axis, [(i, i ^ k) for i in range(mesh.shape[axis])])]
  transfers between devices with their start and end apart: 9 -> 9, of which waited for: 3 -> 3; matrix products, arithmetic and copies ran while one was open for 4% -> 0% of each run, Pallas kernels for 20% -> 16%
where the time goes in v2:
time: 25.3 us; the launch traced here: 25.1 us
  starting transfers between devices  12 us (47%)
  waiting for transfers between devices  5.7 us (23%)
  Pallas kernels  5.25 us (21%)
  between operations  1.42 us (6%)
  local copies, waits for them, and re-layouts  0.69 us (3%)
    ppermute x9, starting transfers between devices, swap(): return lax.ppermute(v, axis, [(i, i ^ k) for i in range(mesh.shape[axis])])  12 us
    ppermute x9, waiting for transfers between devices, swap(): return lax.ppermute(v, axis, [(i, i ^ k) for i in range(mesh.shape[axis])])  5.7 us
    pallas_call x5, Pallas kernels, call(): pl.pallas_call(kernel, name=name, in_specs=[pl.BlockSpec(memory_space=pl....  5.25 us
    unnamed x18, local copies, waits for them, and re-layouts  0.69 us
  transfers between devices with their start and end apart: 9, of which 3 were waited for; matrix products, arithmetic and copies ran while one was open for 0% of the time, Pallas kernels for 16%

profile of v2, /device:TPU:0, one launch (start us, length us, event | category | flops | bytes accessed | tf_op | source)
XLA Modules:
  0.0 25.1 jit_solution(12137144625981471103)
XLA Ops:
  0.6 3.1 %collective-permute-start = (bf16[4,512]{1,0:T(4,128)(2,1)}, bf16[4,512]{1,0:T(4,128)(2,1)S(1)}, u32[]{:S(2)}, u32[]{:S(2)}) collective-permute-start(bf16[4,512]{1,0:T(4,128)(2,1)} %bitcast.24), channel_id=1, source_target_pairs={{0,4},{4,0},{8,12},{12,8},{1,5},{5,1},{9,13},{13,9},{2,6},{6,2},{1... | collective-permute-start | bytes 12296 | tf_op jit(solution)/shard_map/ppermute | solution.py:274
  3.8 2.6 %collective-permute-start.1 = (bf16[4,512]{1,0:T(4,128)(2,1)}, bf16[4,512]{1,0:T(4,128)(2,1)S(1)}, u32[]{:S(2)}, u32[]{:S(2)}) collective-permute-start(bf16[4,512]{1,0:T(4,128)(2,1)} %bitcast.25), channel_id=1, source_target_pairs={{0,8},{4,12},{8,0},{12,4},{1,9},{5,13},{9,1},{13,5},{2,10},{6,14},... | collective-permute-start | bytes 12296 | tf_op jit(solution)/shard_map/ppermute | solution.py:274
  6.3 0.0 collective-permute-start.2
  7.0 1.9 %state.1 = (bf16[128,2048]{1,0:T(8,128)(2,1)S(1)}, f32[128,32]{1,0:T(8,128)S(1)}, f32[32,128]{1,0:T(8,128)S(1)}, f32[128,128]{1,0:T(8,128)S(1)}, bf16[128,2048]{...) custom-call(s32[1]{0:T(128)S(6)} %copy.19.len_hbm, ...), custom_call_target="tpu_custom_call" | custom-call | tf_op jit(solution)/shard_map/state/pallas_call | solution.py:258
  8.9 0.0 collective-permute-done.refs_2_
  9.0 3.0 %collective-permute-done.2.refs_4_ = bf16[4,512]{1,0:T(4,128)(2,1)S(1)} collective-permute-done((bf16[4,512]{1,0:T(4,128)(2,1)}, bf16[4,512]{1,0:T(4,128)(2,1)S(1)}, u32[]{:S(2)}, u32[]{:S(2)}) %collective-permute-start.2) | collective-permute-done | bytes 4128 | tf_op jit(solution)/shard_map/ppermute | solution.py:274
  12.0 0.0 copy-start.8
  12.0 0.2 read.1
  12.2 0.1 collective-permute-start.3
  12.3 1.4 %collective-permute-start.4 = (f32[1,2048]{1,0:T(1,128)S(1)}, f32[1,2048]{1,0:T(1,128)S(1)}, u32[]{:S(2)}, u32[]{:S(2)}) collective-permute-start(f32[1,2048]{1,0:T(1,128)S(1)} %get-tuple-element.40), channel_id=1, source_target_pairs={{0,8},{4,12},{8,0},{12,4},{1,9},{5,13},{9,1},{13,5},{2,10},{6,14},... | collective-permute-start | bytes 24584 | tf_op jit(solution)/shard_map/ppermute | solution.py:274
  13.7 2.9 %collective-permute-start.5 = (f32[1,2048]{1,0:T(1,128)S(1)}, f32[1,2048]{1,0:T(1,128)S(1)}, u32[]{:S(2)}, u32[]{:S(2)}) collective-permute-start(f32[1,2048]{1,0:T(1,128)S(1)} %get-tuple-element.41), channel_id=1, source_target_pairs={{0,12},{4,8},{8,4},{12,0},{1,13},{5,9},{9,5},{13,1},{2,14},{6,10},... | collective-permute-start | bytes 24584 | tf_op jit(solution)/shard_map/ppermute | solution.py:274
  16.7 0.6 %copy-done = f32[2048]{0:T(1024)S(1)} copy-done((f32[2048]{0:T(1024)S(1)}, f32[2048]{0:T(1024)}, u32[]{:S(2)}) %copy-start) | copy-done | bytes 8216
  17.3 0.0 copy-done.4
  17.3 0.0 copy-done.5
  17.3 2.0 %prompt.1 = (f32[128,2048]{1,0:T(8,128)S(1)}, f32[1,128]{1,0:T(1,128)S(1)}, f32[4,2048]{1,0:T(4,128)S(1)}, f32[4,2048]{1,0:T(4,128)S(1)}, bf16[128,2048]{1,0:T(8,128)(2,1)}) custom-call(bf16[128,2048]{1,0:T(8,128)(2,1)S(1)} %get-tuple-element.26.fs_ref.refs_0_, bf16[128,2048]{1,0:T(8,128)(2,1)S(1)} %get-tuple-element.27.x_ref, ...), custom_call_target="tpu_custom_call" | custom-call | tf_op jit(solution)/shard_map/prompt/pallas_call | solution.py:258
  19.4 0.0 collective-permute-done.3.refs_4_
  19.4 0.0 collective-permute-done.4.refs_5_
  19.4 0.1 slot.1
  19.5 1.6 %collective-permute-start.7 = (f32[2,128]{1,0:T(2,128)S(1)}, f32[2,128]{1,0:T(2,128)S(1)}, u32[]{:S(2)}, u32[]{:S(2)}) collective-permute-start(f32[2,128]{1,0:T(2,128)S(1)} %get-tuple-element.43.refs_4_), channel_id=1, source_target_pairs={{0,2},{1,3},{2,0},{3,1},{4,6},{5,7},{6,4},{7,5},{8,10},{9,11},{10,... | collective-permute-start | bytes 3080 | tf_op jit(solution)/shard_map/ppermute | solution.py:274
  21.1 0.3 %collective-permute-start.8 = (f32[2,128]{1,0:T(2,128)S(1)}, f32[2,128]{1,0:T(2,128)S(1)}, u32[]{:S(2)}, u32[]{:S(2)}) collective-permute-start(f32[2,128]{1,0:T(2,128)S(1)} %get-tuple-element.43.refs_4_), channel_id=1, source_target_pairs={{0,3},{1,2},{2,1},{3,0},{4,7},{5,6},{6,5},{7,4},{8,11},{9,10},{10,... | collective-permute-start | bytes 3080 | tf_op jit(solution)/shard_map/ppermute | solution.py:274
  21.4 0.0 collective-permute-done.6.refs_5_
  21.4 1.8 %collective-permute-done.7.refs_6_ = f32[2,128]{1,0:T(2,128)S(1)} collective-permute-done((f32[2,128]{1,0:T(2,128)S(1)}, f32[2,128]{1,0:T(2,128)S(1)}, u32[]{:S(2)}, u32[]{:S(2)}) %collective-permute-start.7) | collective-permute-done | bytes 1056 | tf_op jit(solution)/shard_map/ppermute | solution.py:274
  23.2 0.9 %collective-permute-done.8.refs_7_ = f32[2,128]{1,0:T(2,128)S(1)} collective-permute-done((f32[2,128]{1,0:T(2,128)S(1)}, f32[2,128]{1,0:T(2,128)S(1)}, u32[]{:S(2)}, u32[]{:S(2)}) %collective-permute-start.8) | collective-permute-done | bytes 1056 | tf_op jit(solution)/shard_map/ppermute | solution.py:274
  24.1 1.0 %norm.1 = (bf16[128,2048]{1,0:T(8,128)(2,1)}, bf16[4,2048]{1,0:T(4,128)(2,1)}) custom-call(f32[128,128]{1,0:T(8,128)S(1)} %get-tuple-element.25.refs_0_, f32[128,2048]{1,0:T(8,128)S(1)} %get-tuple-element.34.refs_1_, f32[4,2048]{1,0:T(4,128)S(1)} %get-tuple-element.42.refs_2_, f32[1,2048]{1,0:T(1,128)S(1)} %bitcast.21, ...), custom_call_target="tpu_custom_call" | custom-call | tf_op jit(solution)/shard_map/norm/pallas_call | solution.py:258
  (17 shorter events, 0.0 us)
Async XLA Ops:
  0.6 8.3 %collective-permute-start = (bf16[4,512]{1,0:T(4,128)(2,1)}, bf16[4,512]{1,0:T(4,128)(2,1)S(1)}, u32[]{:S(2)}, u32[]{:S(2)}) collective-permute-start(bf16[4,512]{1,0:T(4,128)(2,1)} %bitcast.24), channel_id=1, source_target_pairs={{0,4},{4,0},{8,12},{12,8},{1,5},{5,1},{9,13},{13,9},{2,6},{6,2},{1... | collective-permute-start | bytes 12296 | tf_op jit(solution)/shard_map/ppermute | solution.py:274
  3.8 5.2 %collective-permute-start.1 = (bf16[4,512]{1,0:T(4,128)(2,1)}, bf16[4,512]{1,0:T(4,128)(2,1)S(1)}, u32[]{:S(2)}, u32[]{:S(2)}) collective-permute-start(bf16[4,512]{1,0:T(4,128)(2,1)} %bitcast.25), channel_id=1, source_target_pairs={{0,8},{4,12},{8,0},{12,4},{1,9},{5,13},{9,1},{13,5},{2,10},{6,14},... | collective-permute-start | bytes 12296 | tf_op jit(solution)/shard_map/ppermute | solution.py:274
  6.3 5.6 %collective-permute-start.2 = (bf16[4,512]{1,0:T(4,128)(2,1)}, bf16[4,512]{1,0:T(4,128)(2,1)S(1)}, u32[]{:S(2)}, u32[]{:S(2)}) collective-permute-start(bf16[4,512]{1,0:T(4,128)(2,1)} %bitcast.26), channel_id=1, source_target_pairs={{0,12},{4,8},{8,4},{12,0},{1,13},{5,9},{9,5},{13,1},{2,14},{6,10},... | collective-permute-start | bytes 12296 | tf_op jit(solution)/shard_map/ppermute | solution.py:274
  7.0 5.0 %copy-start.3 = (bf16[1,4,512]{2,1,0:T(4,128)(2,1)S(1)}, bf16[1,4,512]{2,1,0:T(4,128)(2,1)}, u32[]{:S(2)}) copy-start(bf16[1,4,512]{2,1,0:T(4,128)(2,1)} %param.30) | copy-start | bytes 12292
  12.0 4.7 %copy-start.2 = (bf16[1,4,2048]{2,1,0:T(4,128)(2,1)S(1)}, bf16[1,4,2048]{2,1,0:T(4,128)(2,1)}, u32[]{:S(2)}) copy-start(bf16[1,4,2048]{2,1,0:T(4,128)(2,1)} %param.28) | copy-start | bytes 49156
  12.0 4.7 %copy-start.6 = (f32[32]{0:T(128)S(1)}, f32[32]{0:T(128)}, u32[]{:S(2)}) copy-start(f32[32]{0:T(128)} %param.23) | copy-start | bytes 388
  12.0 4.7 %copy-start.7 = (f32[32]{0:T(128)S(1)}, f32[32]{0:T(128)}, u32[]{:S(2)}) copy-start(f32[32]{0:T(128)} %param.24) | copy-start | bytes 388
  12.0 4.7 %copy-start.8 = (f32[32]{0:T(128)S(1)}, f32[32]{0:T(128)}, u32[]{:S(2)}) copy-start(f32[32]{0:T(128)} %param.25) | copy-start | bytes 388
  12.2 4.5 %copy-start.1 = (bf16[1,4,2048]{2,1,0:T(4,128)(2,1)S(1)}, bf16[1,4,2048]{2,1,0:T(4,128)(2,1)}, u32[]{:S(2)}) copy-start(bf16[1,4,2048]{2,1,0:T(4,128)(2,1)} %param.27) | copy-start | bytes 49156
  12.2 7.2 %collective-permute-start.3 = (f32[1,2048]{1,0:T(1,128)S(1)}, f32[1,2048]{1,0:T(1,128)S(1)}, u32[]{:S(2)}, u32[]{:S(2)}) collective-permute-start(f32[1,2048]{1,0:T(1,128)S(1)} %get-tuple-element.39), channel_id=1, source_target_pairs={{0,4},{4,0},{8,12},{12,8},{1,5},{5,1},{9,13},{13,9},{2,6},{6,2},{1... | collective-permute-start | bytes 24584 | tf_op jit(solution)/shard_map/ppermute | solution.py:274
  12.3 7.1 %collective-permute-start.4 = (f32[1,2048]{1,0:T(1,128)S(1)}, f32[1,2048]{1,0:T(1,128)S(1)}, u32[]{:S(2)}, u32[]{:S(2)}) collective-permute-start(f32[1,2048]{1,0:T(1,128)S(1)} %get-tuple-element.40), channel_id=1, source_target_pairs={{0,8},{4,12},{8,0},{12,4},{1,9},{5,13},{9,1},{13,5},{2,10},{6,14},... | collective-permute-start | bytes 24584 | tf_op jit(solution)/shard_map/ppermute | solution.py:274
  13.7 5.7 %collective-permute-start.5 = (f32[1,2048]{1,0:T(1,128)S(1)}, f32[1,2048]{1,0:T(1,128)S(1)}, u32[]{:S(2)}, u32[]{:S(2)}) collective-permute-start(f32[1,2048]{1,0:T(1,128)S(1)} %get-tuple-element.41), channel_id=1, source_target_pairs={{0,12},{4,8},{8,4},{12,0},{1,13},{5,9},{9,5},{13,1},{2,14},{6,10},... | collective-permute-start | bytes 24584 | tf_op jit(solution)/shard_map/ppermute | solution.py:274
  16.6 0.7 %copy-start = (f32[2048]{0:T(1024)S(1)}, f32[2048]{0:T(1024)}, u32[]{:S(2)}) copy-start(f32[2048]{0:T(1024)} %param.26) | copy-start | bytes 24580
  16.6 0.7 %copy-start.4 = (bf16[1,4,512]{2,1,0:T(4,128)(2,1)S(1)}, bf16[1,4,512]{2,1,0:T(4,128)(2,1)}, u32[]{:S(2)}) copy-start(bf16[1,4,512]{2,1,0:T(4,128)(2,1)} %param.29) | copy-start | bytes 12292
  16.6 0.7 %copy-start.5 = (f32[1,4,32]{2,1,0:T(4,128)S(1)}, f32[1,4,32]{2,1,0:T(4,128)}, u32[]{:S(2)}) copy-start(f32[1,4,32]{2,1,0:T(4,128)} %param.31) | copy-start | bytes 1540
  19.5 1.9 %collective-permute-start.6 = (f32[2,128]{1,0:T(2,128)S(1)}, f32[2,128]{1,0:T(2,128)S(1)}, u32[]{:S(2)}, u32[]{:S(2)}) collective-permute-start(f32[2,128]{1,0:T(2,128)S(1)} %get-tuple-element.43.refs_4_), channel_id=1, source_target_pairs={{0,1},{1,0},{2,3},{3,2},{4,5},{5,4},{6,7},{7,6},{8,9},{9,8},{10,11... | collective-permute-start | bytes 3080 | tf_op jit(solution)/shard_map/ppermute | solution.py:274
  19.5 3.6 %collective-permute-start.7 = (f32[2,128]{1,0:T(2,128)S(1)}, f32[2,128]{1,0:T(2,128)S(1)}, u32[]{:S(2)}, u32[]{:S(2)}) collective-permute-start(f32[2,128]{1,0:T(2,128)S(1)} %get-tuple-element.43.refs_4_), channel_id=1, source_target_pairs={{0,2},{1,3},{2,0},{3,1},{4,6},{5,7},{6,4},{7,5},{8,10},{9,11},{10,... | collective-permute-start | bytes 3080 | tf_op jit(solution)/shard_map/ppermute | solution.py:274
  21.1 3.0 %collective-permute-start.8 = (f32[2,128]{1,0:T(2,128)S(1)}, f32[2,128]{1,0:T(2,128)S(1)}, u32[]{:S(2)}, u32[]{:S(2)}) collective-permute-start(f32[2,128]{1,0:T(2,128)S(1)} %get-tuple-element.43.refs_4_), channel_id=1, source_target_pairs={{0,3},{1,2},{2,1},{3,0},{4,7},{5,6},{6,5},{7,4},{8,11},{9,10},{10,... | collective-permute-start | bytes 3080 | tf_op jit(solution)/shard_map/ppermute | solution.py:274

commit v3 on v2

--- a/solution.py
+++ b/solution.py
@@ -7,10 +7,10 @@
 from jax.experimental.pallas import tpu as pltpu
 from jax.sharding import PartitionSpec as P
 
+
 H = 128
 G = 4
 epsilon = 1e-05
-highest = lax.Precision.HIGHEST
 f32 = jnp.float32
 bf16 = jnp.bfloat16
 LOG2E = 1.4426950408889634
@@ -73,8 +73,10 @@
 
 def state_kernel(
     len_hbm, dt_hbm, a_hbm, bias_hbm, x_hbm, b_hbm, s0_hbm, z_hbm, cp_hbm,
+    skip_hbm, gain_hbm, xd_hbm, zd_hbm, bd_hbm, cd_hbm, dtd_hbm,
     fs_ref, c_ref, r_ref, valid_ref, x_ref, b_ref, s0_ref, z_ref, cp_ref,
-    len_ref, dt_ref, a_ref, bias_ref, sems,
+    skip_ref, gain_ref, xd_ref, zd_ref, bd_ref, cd_ref, dtd_ref, a_ref, bias_ref,
+    len_ref, dt_ref, sems,
 ):
     heads, length = dt_ref.shape
     width = x_ref.shape[1]
@@ -85,7 +87,9 @@
         for i, (source, target) in enumerate((
             (len_hbm, len_ref), (dt_hbm, dt_ref), (a_hbm, a_ref), (bias_hbm, bias_ref),
             (x_hbm, x_ref), (b_hbm.at[:, lanes], b_ref), (s0_hbm, s0_ref),
-            (z_hbm, z_ref), (cp_hbm.at[:, lanes], cp_ref),
+            (z_hbm, z_ref), (cp_hbm.at[:, lanes], cp_ref), (skip_hbm, skip_ref),
+            (gain_hbm, gain_ref), (xd_hbm, xd_ref), (zd_hbm, zd_ref),
+            (bd_hbm.at[:, lanes], bd_ref), (cd_hbm.at[:, lanes], cd_ref), (dtd_hbm, dtd_ref),
         ))
     ]
     for copy in copies:
@@ -117,8 +121,8 @@
     fresh = lax.dot_general(b_ref[...], xw, (((0,), (0,)), ((), ())), preferred_element_type=f32)
     copies[6].wait()
     fs_ref[...] = (fresh + total * s0_ref[...]).astype(bf16)
-    copies[7].wait()
-    copies[8].wait()
+    for copy in copies[7:]:
+        copy.wait()
 
 
 def read_kernel(*refs):
@@ -145,10 +149,9 @@
     gated_ref, sq_ref, u_ref, v_ref, fs_hbm, m_ref, sem,
 ):
     length, heads = c_ref.shape
-    states, width = s0_ref.shape
+    _, width = s0_ref.shape
     per = width // heads
     prompts = xd_ref.shape[0]
-    lanes = group_lanes(states, heads)
     store = pltpu.make_async_copy(fs_ref, fs_hbm, sem)
     store.start()
     cp = cp_ref[...]
@@ -159,7 +162,7 @@
     m_ref[...] = jnp.dot(cp, s0_ref[...].astype(bf16), preferred_element_type=f32)
 
     step = softplus(dtd_ref[...] + bias_ref[...])
-    cb = cd_ref[:, lanes].astype(f32) * bd_ref[:, lanes].astype(f32)
+    cb = cd_ref[...].astype(f32) * bd_ref[...].astype(f32)
     cb = jnp.sum(cb, axis=1, keepdims=True)
     gain = step * cb + skip_ref[...]
     skips = jnp.broadcast_to(skip_ref[...], (8, heads))
@@ -252,12 +255,11 @@
 HBM = pltpu.MemorySpace.HBM
 
 
-def call(kernel, name, ins, outs, scratch=(), far=(), fetch=False):
+def call(kernel, ins, outs, scratch=(), far=(), fetch=False):
     space = HBM if fetch else VMEM
     outs = [(VMEM, *out) for out in outs] + [(HBM, *out) for out in far]
     return pl.pallas_call(
         kernel,
-        name=name,
         in_specs=[pl.BlockSpec(memory_space=pl.ANY if v.size == 1 else space) for v in ins],
         out_specs=tuple(pl.BlockSpec(memory_space=out[0]) for out in outs),
         out_shape=tuple(out[0](*out[1:]) for out in outs),
@@ -274,6 +276,15 @@
         return lax.ppermute(v, axis, [(i, i ^ k) for i in range(mesh.shape[axis])])
 
     def body(
+        x_pre, z_pre, b_pre, c_pre, dt_pre, lengths, init_state, a_rates, dt_bias, skip_scale,
+        norm_gain, x_dec, z_dec, b_dec, c_dec, dt_dec,
+    ):
+        return layer(
+            x_pre, z_pre, b_pre, c_pre, dt_pre, lengths, init_state, a_rates, dt_bias,
+            skip_scale, norm_gain, x_dec, z_dec, b_dec, c_dec, dt_dec,
+        )
+
+    def layer(
         x_pre, z_pre, b_pre, c_pre, dt_pre, lengths, init_state, a_rates, dt_bias, skip_scale,
         norm_gain, x_dec, z_dec, b_dec, c_dec, dt_dec,
     ):
@@ -285,35 +296,40 @@
         xd, zd, bd, cd, dtd = (v[0] for v in (x_dec, z_dec, b_dec, c_dec, dt_dec))
         a, bias, skip, gain = (v[None] for v in (a_rates, dt_bias, skip_scale, norm_gain))
         queries = [cd] + [swap(cd, "sample", k) for k in range(1, samples)]
-        fs, c, r, valid, x, b, s0, z, cp = call(
-            state_kernel, "state", (lengths, dt.T, a, bias, x, b, s0, z, cp),
+        fs, c, r, valid, *loaded = call(
+            state_kernel,
+            (lengths, dt.T, a, bias, x, b, s0, z, cp, skip, gain, xd, zd, bd, cd, dtd),
             (
                 ((states, width), bf16), ((length, heads), f32), ((heads, length), f32),
                 ((length, 128), f32), ((length, width), bf16), ((length, states), bf16), ((states, width), f32),
                 ((length, width), bf16), ((length, states), bf16),
+                ((1, heads), f32), ((1, width), f32),
+                ((prompts, width), bf16), ((prompts, width), bf16),
+                ((prompts, states), bf16), ((prompts, states), bf16),
+                ((prompts, heads), f32), ((1, heads), f32), ((1, heads), f32),
             ),
             (
                 pltpu.SMEM((1,), jnp.int32), pltpu.VMEM((heads, length), f32),
-                pltpu.VMEM((1, heads), f32), pltpu.VMEM((1, heads), f32),
-                pltpu.SemaphoreType.DMA((9,)),
+                pltpu.SemaphoreType.DMA((16,)),
             ), fetch=True,
         )
-        reads = call(read_kernel, "read", (fs, *queries), (((1, width), f32),) * samples)
+        x, b, s0, z, cp, skip, gain, xd, zd, bd, own, dtd, a, bias = loaded
+        reads = call(read_kernel, (fs, *queries), (((1, width), f32),) * samples)
         reads = [reads[0]] + [swap(reads[k], "sample", k) for k in range(1, samples)]
         gated, sq, u, v, fs = call(
-            prompt_kernel, "prompt",
-            (fs, x, z, b, cp, s0, c, r, skip, gain, xd, zd, bd, cd, dtd, a, bias),
+            prompt_kernel,
+            (fs, x, z, b, cp, s0, c, r, skip, gain, xd, zd, bd, own, dtd, a, bias),
             (((length, width), f32), ((1, length), f32)) + (((prompts, width), f32),) * 2,
             (pltpu.VMEM((length, width), f32), pltpu.SemaphoreType.DMA(())),
             (((states, width), bf16),),
         )
         gated_dec, pay = call(
-            slot_kernel, "slot", (sq, u, v, *reads), (((prompts, width), f32), ((2, 128), f32))
+            slot_kernel, (sq, u, v, *reads), (((prompts, width), f32), ((2, 128), f32))
         )
         pays = [pay] + [swap(pay, "head", k) for k in range(1, head_parts)]
         out_pre, out_dec = call(
             functools.partial(norm_kernel, channels=width * head_parts, payloads=head_parts),
-            "norm", (valid, gated, gated_dec, gain, *pays), (),
+            (valid, gated, gated_dec, gain, *pays), (),
             (
                 pltpu.VMEM((length, width), bf16), pltpu.VMEM((prompts, width), bf16),
                 pltpu.SemaphoreType.DMA((1 + CHUNKS,)),

time: 25.3 us -> 25 us (0.988)
  local copies, waits for them, and re-layouts: 0.69 us -> 0.01 us
  waiting for transfers between devices: 5.7 us -> 6.05 us
    unnamed x18 -> x2, local copies, waits for them, and re-layouts: 0.69 us -> 0.01 us
    ppermute x9, waiting for transfers between devices: 5.7 us -> 6.05 us  [swap(): return lax.ppermute(v, axis, [(i, i ^ k) for i in range(mesh.shape[axis])])]
  transfers between devices with their start and end apart: 9 -> 9, of which waited for: 3 -> 4; matrix products, arithmetic and copies ran while one was open for 0% -> 0% of each run, Pallas kernels for 16% -> 17%
where the time goes in v3:
time: 25 us; the launch traced here: 24.9 us
  starting transfers between devices  12 us (48%)
  waiting for transfers between devices  6.05 us (24%)
  Pallas kernels  5.44 us (22%)
  between operations  1.36 us (5%)
    ppermute x9, starting transfers between devices, swap(): return lax.ppermute(v, axis, [(i, i ^ k) for i in range(mesh.shape[axis])])  12 us
    ppermute x9, waiting for transfers between devices, swap(): return lax.ppermute(v, axis, [(i, i ^ k) for i in range(mesh.shape[axis])])  6.05 us
    pallas_call x5, Pallas kernels, call(): pl.pallas_call(kernel, in_specs=[pl.BlockSpec(memory_space=pl.ANY if v.si...  5.44 us
  transfers between devices with their start and end apart: 9, of which 4 were waited for; matrix products, arithmetic and copies ran while one was open for 0% of the time, Pallas kernels for 17%

profile of v3, /device:TPU:0, one launch (start us, length us, event | category | flops | bytes accessed | tf_op | source)
XLA Modules:
  0.0 24.9 jit_solution(18144276759025128032)
XLA Ops:
  0.6 3.1 %collective-permute-start = (bf16[4,512]{1,0:T(4,128)(2,1)}, bf16[4,512]{1,0:T(4,128)(2,1)S(1)}, u32[]{:S(2)}, u32[]{:S(2)}) collective-permute-start(bf16[4,512]{1,0:T(4,128)(2,1)} %bitcast.20), channel_id=1, source_target_pairs={{0,4},{4,0},{8,12},{12,8},{1,5},{5,1},{9,13},{13,9},{2,6},{6,2},{1... | collective-permute-start | bytes 12296 | tf_op jit(solution)/shard_map/ppermute | solution.py:276
  3.8 2.6 %collective-permute-start.1 = (bf16[4,512]{1,0:T(4,128)(2,1)}, bf16[4,512]{1,0:T(4,128)(2,1)S(1)}, u32[]{:S(2)}, u32[]{:S(2)}) collective-permute-start(bf16[4,512]{1,0:T(4,128)(2,1)} %bitcast.21), channel_id=1, source_target_pairs={{0,8},{4,12},{8,0},{12,4},{1,9},{5,13},{9,1},{13,5},{2,10},{6,14},... | collective-permute-start | bytes 12296 | tf_op jit(solution)/shard_map/ppermute | solution.py:276
  6.3 0.0 collective-permute-start.2
  7.0 0.0 copy-start
  7.0 2.0 %shard_map.175 = (bf16[128,2048]{1,0:T(8,128)(2,1)S(1)}, f32[128,32]{1,0:T(8,128)S(1)}, f32[32,128]{1,0:T(8,128)S(1)}, f32[128,128]{1,0:T(8,128)S(1)}, bf16[128,...) custom-call(s32[1]{0:T(128)S(6)} %copy.19.len_hbm, ...), custom_call_target="tpu_custom_call" | custom-call | tf_op jit(solution)/shard_map/pallas_call | solution.py:261
  9.1 0.0 collective-permute-done.refs_2_
  9.1 0.0 collective-permute-done.1.refs_3_
  9.1 2.9 %collective-permute-done.2.refs_4_ = bf16[4,512]{1,0:T(4,128)(2,1)S(1)} collective-permute-done((bf16[4,512]{1,0:T(4,128)(2,1)}, bf16[4,512]{1,0:T(4,128)(2,1)S(1)}, u32[]{:S(2)}, u32[]{:S(2)}) %collective-permute-start.2) | collective-permute-done | bytes 4128 | tf_op jit(solution)/shard_map/ppermute | solution.py:276
  12.0 0.2 shard_map.177
  12.1 0.1 collective-permute-start.3
  12.2 1.5 %collective-permute-start.4 = (f32[1,2048]{1,0:T(1,128)S(1)}, f32[1,2048]{1,0:T(1,128)S(1)}, u32[]{:S(2)}, u32[]{:S(2)}) collective-permute-start(f32[1,2048]{1,0:T(1,128)S(1)} %get-tuple-element.58), channel_id=1, source_target_pairs={{0,8},{4,12},{8,0},{12,4},{1,9},{5,13},{9,1},{13,5},{2,10},{6,14},... | collective-permute-start | bytes 24584 | tf_op jit(solution)/shard_map/ppermute | solution.py:276
  13.7 2.9 %collective-permute-start.5 = (f32[1,2048]{1,0:T(1,128)S(1)}, f32[1,2048]{1,0:T(1,128)S(1)}, u32[]{:S(2)}, u32[]{:S(2)}) collective-permute-start(f32[1,2048]{1,0:T(1,128)S(1)} %get-tuple-element.59), channel_id=1, source_target_pairs={{0,12},{4,8},{8,4},{12,0},{1,13},{5,9},{9,5},{13,1},{2,14},{6,10},... | collective-permute-start | bytes 24584 | tf_op jit(solution)/shard_map/ppermute | solution.py:276
  16.6 2.1 %shard_map.176 = (f32[128,2048]{1,0:T(8,128)S(1)}, f32[1,128]{1,0:T(1,128)S(1)}, f32[4,2048]{1,0:T(4,128)S(1)}, f32[4,2048]{1,0:T(4,128)S(1)}, bf16[128,2048]{1,0:T(8,128)(2,1)}) custom-call(bf16[128,2048]{1,0:T(8,128)(2,1)S(1)} %get-tuple-element.35.fs_ref.refs_0_, bf16[128,2048]{1,0:T(8,128)(2,1)S(1)} %get-tuple-element.36.x_ref, ...), custom_call_target="tpu_custom_call" | custom-call | tf_op jit(solution)/shard_map/pallas_call | solution.py:261
  18.7 0.0 collective-permute-done.3.refs_4_
  18.7 0.0 collective-permute-done.4.refs_5_
  18.7 0.5 %collective-permute-done.5.refs_6_ = f32[1,2048]{1,0:T(1,128)S(1)} collective-permute-done((f32[1,2048]{1,0:T(1,128)S(1)}, f32[1,2048]{1,0:T(1,128)S(1)}, u32[]{:S(2)}, u32[]{:S(2)}) %collective-permute-start.5) | collective-permute-done | bytes 8224 | tf_op jit(solution)/shard_map/ppermute | solution.py:276
  19.2 0.1 shard_map.178
  19.3 0.0 collective-permute-start.6
  19.3 1.6 %collective-permute-start.7 = (f32[2,128]{1,0:T(2,128)S(1)}, f32[2,128]{1,0:T(2,128)S(1)}, u32[]{:S(2)}, u32[]{:S(2)}) collective-permute-start(f32[2,128]{1,0:T(2,128)S(1)} %get-tuple-element.61.refs_4_), channel_id=1, source_target_pairs={{0,2},{1,3},{2,0},{3,1},{4,6},{5,7},{6,4},{7,5},{8,10},{9,11},{10,... | collective-permute-start | bytes 3080 | tf_op jit(solution)/shard_map/ppermute | solution.py:276
  20.9 0.3 %collective-permute-start.8 = (f32[2,128]{1,0:T(2,128)S(1)}, f32[2,128]{1,0:T(2,128)S(1)}, u32[]{:S(2)}, u32[]{:S(2)}) collective-permute-start(f32[2,128]{1,0:T(2,128)S(1)} %get-tuple-element.61.refs_4_), channel_id=1, source_target_pairs={{0,3},{1,2},{2,1},{3,0},{4,7},{5,6},{6,5},{7,4},{8,11},{9,10},{10,... | collective-permute-start | bytes 3080 | tf_op jit(solution)/shard_map/ppermute | solution.py:276
  21.2 0.0 collective-permute-done.6.refs_5_
  21.2 1.8 %collective-permute-done.7.refs_6_ = f32[2,128]{1,0:T(2,128)S(1)} collective-permute-done((f32[2,128]{1,0:T(2,128)S(1)}, f32[2,128]{1,0:T(2,128)S(1)}, u32[]{:S(2)}, u32[]{:S(2)}) %collective-permute-start.7) | collective-permute-done | bytes 1056 | tf_op jit(solution)/shard_map/ppermute | solution.py:276
  22.9 0.9 %collective-permute-done.8.refs_7_ = f32[2,128]{1,0:T(2,128)S(1)} collective-permute-done((f32[2,128]{1,0:T(2,128)S(1)}, f32[2,128]{1,0:T(2,128)S(1)}, u32[]{:S(2)}, u32[]{:S(2)}) %collective-permute-start.8) | collective-permute-done | bytes 1056 | tf_op jit(solution)/shard_map/ppermute | solution.py:276
  23.9 1.0 %shard_map.179 = (bf16[128,2048]{1,0:T(8,128)(2,1)}, bf16[4,2048]{1,0:T(4,128)(2,1)}) custom-call(f32[128,128]{1,0:T(8,128)S(1)} %get-tuple-element.34.refs_0_, f32[128,2048]{1,0:T(8,128)S(1)} %get-tuple-element.52.refs_1_, f32[4,2048]{1,0:T(4,128)S(1)} %get-tuple-element.60.refs_2_, f32[1,2048]{1,0:T(1,128)S(1)} %get-tuple-element.44.gain_ref.refs_3_, ...), custom_call_target="tpu_custom_call" | custom-call | tf_op jit(solution)/shard_map/pallas_call | solution.py:261
  (1 shorter events, 0.0 us)
Async XLA Ops:
  0.6 8.4 %collective-permute-start = (bf16[4,512]{1,0:T(4,128)(2,1)}, bf16[4,512]{1,0:T(4,128)(2,1)S(1)}, u32[]{:S(2)}, u32[]{:S(2)}) collective-permute-start(bf16[4,512]{1,0:T(4,128)(2,1)} %bitcast.20), channel_id=1, source_target_pairs={{0,4},{4,0},{8,12},{12,8},{1,5},{5,1},{9,13},{13,9},{2,6},{6,2},{1... | collective-permute-start | bytes 12296 | tf_op jit(solution)/shard_map/ppermute | solution.py:276
  3.8 5.3 %collective-permute-start.1 = (bf16[4,512]{1,0:T(4,128)(2,1)}, bf16[4,512]{1,0:T(4,128)(2,1)S(1)}, u32[]{:S(2)}, u32[]{:S(2)}) collective-permute-start(bf16[4,512]{1,0:T(4,128)(2,1)} %bitcast.21), channel_id=1, source_target_pairs={{0,8},{4,12},{8,0},{12,4},{1,9},{5,13},{9,1},{13,5},{2,10},{6,14},... | collective-permute-start | bytes 12296 | tf_op jit(solution)/shard_map/ppermute | solution.py:276
  6.3 5.6 %collective-permute-start.2 = (bf16[4,512]{1,0:T(4,128)(2,1)}, bf16[4,512]{1,0:T(4,128)(2,1)S(1)}, u32[]{:S(2)}, u32[]{:S(2)}) collective-permute-start(bf16[4,512]{1,0:T(4,128)(2,1)} %bitcast.22), channel_id=1, source_target_pairs={{0,12},{4,8},{8,4},{12,0},{1,13},{5,9},{9,5},{13,1},{2,14},{6,10},... | collective-permute-start | bytes 12296 | tf_op jit(solution)/shard_map/ppermute | solution.py:276
  7.0 5.0 %copy-start = (bf16[1,4,512]{2,1,0:T(4,128)(2,1)S(1)}, bf16[1,4,512]{2,1,0:T(4,128)(2,1)}, u32[]{:S(2)}) copy-start(bf16[1,4,512]{2,1,0:T(4,128)(2,1)} %param.30) | copy-start | bytes 12292
  12.1 6.6 %collective-permute-start.3 = (f32[1,2048]{1,0:T(1,128)S(1)}, f32[1,2048]{1,0:T(1,128)S(1)}, u32[]{:S(2)}, u32[]{:S(2)}) collective-permute-start(f32[1,2048]{1,0:T(1,128)S(1)} %get-tuple-element.57), channel_id=1, source_target_pairs={{0,4},{4,0},{8,12},{12,8},{1,5},{5,1},{9,13},{13,9},{2,6},{6,2},{1... | collective-permute-start | bytes 24584 | tf_op jit(solution)/shard_map/ppermute | solution.py:276
  12.2 6.5 %collective-permute-start.4 = (f32[1,2048]{1,0:T(1,128)S(1)}, f32[1,2048]{1,0:T(1,128)S(1)}, u32[]{:S(2)}, u32[]{:S(2)}) collective-permute-start(f32[1,2048]{1,0:T(1,128)S(1)} %get-tuple-element.58), channel_id=1, source_target_pairs={{0,8},{4,12},{8,0},{12,4},{1,9},{5,13},{9,1},{13,5},{2,10},{6,14},... | collective-permute-start | bytes 24584 | tf_op jit(solution)/shard_map/ppermute | solution.py:276
  13.7 5.4 %collective-permute-start.5 = (f32[1,2048]{1,0:T(1,128)S(1)}, f32[1,2048]{1,0:T(1,128)S(1)}, u32[]{:S(2)}, u32[]{:S(2)}) collective-permute-start(f32[1,2048]{1,0:T(1,128)S(1)} %get-tuple-element.59), channel_id=1, source_target_pairs={{0,12},{4,8},{8,4},{12,0},{1,13},{5,9},{9,5},{13,1},{2,14},{6,10},... | collective-permute-start | bytes 24584 | tf_op jit(solution)/shard_map/ppermute | solution.py:276
  19.3 1.9 %collective-permute-start.6 = (f32[2,128]{1,0:T(2,128)S(1)}, f32[2,128]{1,0:T(2,128)S(1)}, u32[]{:S(2)}, u32[]{:S(2)}) collective-permute-start(f32[2,128]{1,0:T(2,128)S(1)} %get-tuple-element.61.refs_4_), channel_id=1, source_target_pairs={{0,1},{1,0},{2,3},{3,2},{4,5},{5,4},{6,7},{7,6},{8,9},{9,8},{10,11... | collective-permute-start | bytes 3080 | tf_op jit(solution)/shard_map/ppermute | solution.py:276
  19.3 3.6 %collective-permute-start.7 = (f32[2,128]{1,0:T(2,128)S(1)}, f32[2,128]{1,0:T(2,128)S(1)}, u32[]{:S(2)}, u32[]{:S(2)}) collective-permute-start(f32[2,128]{1,0:T(2,128)S(1)} %get-tuple-element.61.refs_4_), channel_id=1, source_target_pairs={{0,2},{1,3},{2,0},{3,1},{4,6},{5,7},{6,4},{7,5},{8,10},{9,11},{10,... | collective-permute-start | bytes 3080 | tf_op jit(solution)/shard_map/ppermute | solution.py:276
  20.9 3.0 %collective-permute-start.8 = (f32[2,128]{1,0:T(2,128)S(1)}, f32[2,128]{1,0:T(2,128)S(1)}, u32[]{:S(2)}, u32[]{:S(2)}) collective-permute-start(f32[2,128]{1,0:T(2,128)S(1)} %get-tuple-element.61.refs_4_), channel_id=1, source_target_pairs={{0,3},{1,2},{2,1},{3,0},{4,7},{5,6},{6,5},{7,4},{8,11},{9,10},{10,... | collective-permute-start | bytes 3080 | tf_op jit(solution)/shard_map/ppermute | solution.py:276

commit v4 on v3

--- a/solution.py
+++ b/solution.py
@@ -125,22 +125,34 @@
         copy.wait()
 
 
-def read_kernel(*refs):
-    n = (len(refs) - 1) // 2
-    fs_ref = refs[0]
+def entry(table, index):
+    value = jnp.int32(table[0])
+    for i, number in enumerate(table[1:], 1):
+        value = jnp.where(index == i, jnp.int32(number), value)
+    return value
+
+
+def read_kernel(*refs, asks, answers):
+    fs_ref, own_ref = refs[:2]
+    ask_refs = refs[2 : 2 + len(asks)]
+    mine_ref = refs[2 + len(asks)]
+    out_refs = refs[3 + len(asks) :]
     states, width = fs_ref.shape
-    heads = width // 64
     me = lax.axis_index("sample")
-    lanes = group_lanes(states, heads)
-    rows = []
-    for k in range(n):
-        block = refs[1 + k][:, lanes].astype(f32)
-        mine = lax.broadcasted_iota(jnp.int32, block.shape, 0) == me
-        rows.append(jnp.sum(jnp.where(mine, block, 0.0), axis=0, keepdims=True))
-    q = jnp.concatenate(rows, axis=0).astype(bf16)
-    reads = jnp.dot(q, fs_ref[...], preferred_element_type=f32)
-    for k in range(n):
-        refs[1 + n + k][...] = reads[k : k + 1, :]
+    lanes = pl.ds(0, states)
+    if own_ref.shape[1] != states:
+        lanes = group_lanes(states, width // 64)
+    n = own_ref.shape[0]
+    row = lax.broadcasted_iota(jnp.int32, (n, states), 0)
+    q = jnp.zeros((n, states), f32)
+    for who, ref in [(me, own_ref)] + [(entry(t, me), r) for t, r in zip(asks, ask_refs)]:
+        block = ref[:, lanes].astype(f32)
+        query = jnp.sum(jnp.where(row == me, block, 0.0), axis=0, keepdims=True)
+        q = jnp.where(row == who, query, q)
+    reads = jnp.dot(q.astype(bf16), fs_ref[...], preferred_element_type=f32)
+    slot = lax.broadcasted_iota(jnp.int32, (n, width), 0)
+    for who, ref in [(me, mine_ref)] + [(entry(t, me), r) for t, r in zip(answers, out_refs)]:
+        ref[...] = jnp.sum(jnp.where(slot == who, reads, 0.0), axis=0, keepdims=True)
 
 
 def prompt_kernel(
@@ -202,7 +214,7 @@
     store.wait()
 
 
-def slot_kernel(*refs):
+def slot_kernel(*refs, sources):
     sq_ref, u_ref, v_ref = refs[:3]
     read_refs = refs[3:-2]
     gated_ref, pay_ref = refs[-2:]
@@ -210,8 +222,9 @@
     me = lax.axis_index("sample")
     prompt = lax.broadcasted_iota(jnp.int32, (prompts, width), 0)
     reads = jnp.zeros((prompts, width), f32)
-    for k, ref in enumerate(read_refs):
-        reads = jnp.where(prompt == (me ^ k), ref[...], reads)
+    whose = [me] + [entry(table, me) for table in sources]
+    for who, ref in zip(whose, read_refs):
+        reads = jnp.where(prompt == who, ref[...], reads)
     gated = u_ref[...] * reads + v_ref[...]
     gated_ref[...] = gated
     total = jnp.broadcast_to(jnp.sum(gated * gated, axis=1, keepdims=True), (prompts, 128))
@@ -268,12 +281,37 @@
     )(*(v if v.size == 1 else pltpu.with_memory_space_constraint(v, space) for v in ins))
 
 
+SCHEDULES = {
+    ("query", 4): [
+        [(0, 2), (1, 3), (2, 0), (3, 1)],
+        [(0, 3), (1, 2), (2, 1), (3, 0)],
+        [(0, 1), (1, 0), (2, 3), (3, 2)],
+    ],
+    ("reads", 4): [
+        [(0, 3), (1, 2), (2, 1), (3, 0)],
+        [(0, 2), (1, 3), (2, 0), (3, 1)],
+        [(0, 1), (1, 0), (2, 3), (3, 2)],
+    ],
+}
+
+
+def steps(tag, n):
+    if (tag, n) in SCHEDULES:
+        return SCHEDULES[tag, n]
+    return [[(i, i ^ k) for i in range(n)] for k in range(n - 1, 0, -1)]
+
+
+def sources(pairs, n):
+    return [dict((b, a) for a, b in pairs).get(i, -1) for i in range(n)]
+
+
+def targets(pairs, n):
+    return [dict(pairs).get(i, -1) for i in range(n)]
+
+
 def make_body(mesh):
     samples = mesh.shape["sample"]
     head_parts = mesh.shape["head"]
-
-    def swap(v, axis, k):
-        return lax.ppermute(v, axis, [(i, i ^ k) for i in range(mesh.shape[axis])])
 
     def body(
         x_pre, z_pre, b_pre, c_pre, dt_pre, lengths, init_state, a_rates, dt_bias, skip_scale,
@@ -295,7 +333,9 @@
         x, z, b, cp, dt, s0 = (v[0] for v in (x_pre, z_pre, b_pre, c_pre, dt_pre, init_state))
         xd, zd, bd, cd, dtd = (v[0] for v in (x_dec, z_dec, b_dec, c_dec, dt_dec))
         a, bias, skip, gain = (v[None] for v in (a_rates, dt_bias, skip_scale, norm_gain))
-        queries = [cd] + [swap(cd, "sample", k) for k in range(1, samples)]
+        asking = steps("query", samples)
+        answering = steps("reads", samples)
+        queries = [lax.ppermute(cd, "sample", pairs) for pairs in asking]
         fs, c, r, valid, *loaded = call(
             state_kernel,
             (lengths, dt.T, a, bias, x, b, s0, z, cp, skip, gain, xd, zd, bd, cd, dtd),
@@ -314,8 +354,16 @@
             ), fetch=True,
         )
         x, b, s0, z, cp, skip, gain, xd, zd, bd, own, dtd, a, bias = loaded
-        reads = call(read_kernel, (fs, *queries), (((1, width), f32),) * samples)
-        reads = [reads[0]] + [swap(reads[k], "sample", k) for k in range(1, samples)]
+        reads = call(
+            functools.partial(
+                read_kernel, asks=[sources(pairs, samples) for pairs in asking],
+                answers=[targets(pairs, samples) for pairs in answering],
+            ), (fs, cd, *queries), (((1, width), f32),) * (1 + len(answering)),
+        )
+        reads = [reads[0]] + [
+            lax.ppermute(v, "sample", pairs)
+            for v, pairs in zip(reads[1:], answering)
+        ]
         gated, sq, u, v, fs = call(
             prompt_kernel,
             (fs, x, z, b, cp, s0, c, r, skip, gain, xd, zd, bd, own, dtd, a, bias),
@@ -324,9 +372,11 @@
             (((states, width), bf16),),
         )
         gated_dec, pay = call(
-            slot_kernel, (sq, u, v, *reads), (((prompts, width), f32), ((2, 128), f32))
-        )
-        pays = [pay] + [swap(pay, "head", k) for k in range(1, head_parts)]
+            functools.partial(
+                slot_kernel, sources=[sources(pairs, samples) for pairs in answering]
+            ), (sq, u, v, *reads), (((prompts, width), f32), ((2, 128), f32)),
+        )
+        pays = [pay] + [lax.ppermute(pay, "head", pairs) for pairs in steps("sums", head_parts)]
         out_pre, out_dec = call(
             functools.partial(norm_kernel, channels=width * head_parts, payloads=head_parts),
             (valid, gated, gated_dec, gain, *pays), (),

time: 25 us -> 22.2 us (0.89)
  waiting for transfers between devices: 6.05 us -> 3.18 us
    ppermute x9, waiting for transfers between devices: 6.05 us -> 3.18 us  [the longest x3 1.78 us: layer(): lax.ppermute(pay, 'head', pairs)]
  transfers between devices with their start and end apart: 9 -> 9, of which waited for: 4 -> 4; matrix products, arithmetic and copies ran while one was open for 0% -> 0% of each run, Pallas kernels for 17% -> 19%
where the time goes in v4:
time: 22.2 us; the launch traced here: 22 us
  starting transfers between devices  12 us (54%)
  Pallas kernels  5.49 us (25%)
  waiting for transfers between devices  3.18 us (14%)
  between operations  1.34 us (6%)
    ppermute x3, starting transfers between devices, layer(): queries = [lax.ppermute(cd, 'sample', pairs) for pairs in asking]  5.71 us
    pallas_call x5, Pallas kernels, call(): pl.pallas_call(kernel, in_specs=[pl.BlockSpec(memory_space=pl.ANY if v.si...  5.49 us
    ppermute x3, starting transfers between devices, layer(): lax.ppermute(v, 'sample', pairs)  4.45 us
    ppermute x3, starting transfers between devices, layer(): lax.ppermute(pay, 'head', pairs)  1.86 us
    ppermute x3, waiting for transfers between devices, layer(): lax.ppermute(pay, 'head', pairs)  1.78 us
    ppermute x3, waiting for transfers between devices, layer(): queries = [lax.ppermute(cd, 'sample', pairs) for pairs in asking]  1.32 us
  transfers between devices with their start and end apart: 9, of which 4 were waited for; matrix products, arithmetic and copies ran while one was open for 0% of the time, Pallas kernels for 19%

profile of v4, /device:TPU:0, one launch (start us, length us, event | category | flops | bytes accessed | tf_op | source)
XLA Modules:
  0.0 22.0 jit_solution(13305824443781884393)
XLA Ops:
  0.6 4.1 %collective-permute-start = (bf16[4,512]{1,0:T(4,128)(2,1)}, bf16[4,512]{1,0:T(4,128)(2,1)S(1)}, u32[]{:S(2)}, u32[]{:S(2)}) collective-permute-start(bf16[4,512]{1,0:T(4,128)(2,1)} %bitcast.20), channel_id=1, source_target_pairs={{0,8},{4,12},{8,0},{12,4},{1,9},{5,13},{9,1},{13,5},{2,10},{6,14},... | collective-permute-start | bytes 12296 | tf_op jit(solution)/shard_map/ppermute | solution.py:338
  4.8 1.3 %collective-permute-start.1 = (bf16[4,512]{1,0:T(4,128)(2,1)}, bf16[4,512]{1,0:T(4,128)(2,1)S(1)}, u32[]{:S(2)}, u32[]{:S(2)}) collective-permute-start(bf16[4,512]{1,0:T(4,128)(2,1)} %bitcast.21), channel_id=1, source_target_pairs={{0,12},{4,8},{8,4},{12,0},{1,13},{5,9},{9,5},{13,1},{2,14},{6,10},... | collective-permute-start | bytes 12296 | tf_op jit(solution)/shard_map/ppermute | solution.py:338
  6.1 0.2 %collective-permute-start.2 = (bf16[4,512]{1,0:T(4,128)(2,1)}, bf16[4,512]{1,0:T(4,128)(2,1)S(1)}, u32[]{:S(2)}, u32[]{:S(2)}) collective-permute-start(bf16[4,512]{1,0:T(4,128)(2,1)} %bitcast.22), channel_id=1, source_target_pairs={{0,4},{4,0},{8,12},{12,8},{1,5},{5,1},{9,13},{13,9},{2,6},{6,2},{1... | collective-permute-start | bytes 12296 | tf_op jit(solution)/shard_map/ppermute | solution.py:338
  7.0 0.0 copy-start
  7.0 2.0 %shard_map.175 = (bf16[128,2048]{1,0:T(8,128)(2,1)S(1)}, f32[128,32]{1,0:T(8,128)S(1)}, f32[32,128]{1,0:T(8,128)S(1)}, f32[128,128]{1,0:T(8,128)S(1)}, bf16[128,...) custom-call(s32[1]{0:T(128)S(6)} %copy.19.len_hbm, ...), custom_call_target="tpu_custom_call" | custom-call | tf_op jit(solution)/shard_map/pallas_call | solution.py:274
  9.1 0.0 collective-permute-done.refs_2_
  9.1 1.3 %collective-permute-done.1.refs_3_ = bf16[4,512]{1,0:T(4,128)(2,1)S(1)} collective-permute-done((bf16[4,512]{1,0:T(4,128)(2,1)}, bf16[4,512]{1,0:T(4,128)(2,1)S(1)}, u32[]{:S(2)}, u32[]{:S(2)}) %collective-permute-start.1) | collective-permute-done | bytes 4128 | tf_op jit(solution)/shard_map/ppermute | solution.py:338
  10.4 0.0 collective-permute-done.2.refs_4_
  10.4 0.2 %shard_map.177 = (f32[1,2048]{1,0:T(1,128)S(1)}, f32[1,2048]{1,0:T(1,128)S(1)}, f32[1,2048]{1,0:T(1,128)S(1)}, f32[1,2048]{1,0:T(1,128)S(1)}) custom-call(bf16[128,2048]{1,0:T(8,128)(2,1)S(1)} %get-tuple-element.35.fs_ref.refs_0_, bf16[4,512]{1,0:T(4,128)(2,1)S(1)} %bitcast.24, bf16[4,512]{1,0:T(4,128)(2,1)S(1)} %collective-permute-done.refs_2_, ...), custom_call_target="tpu_custom_call" | custom-call | tf_op jit(solution)/shard_map/pallas_call | solution.py:274
  10.6 2.1 %collective-permute-start.3 = (f32[1,2048]{1,0:T(1,128)S(1)}, f32[1,2048]{1,0:T(1,128)S(1)}, u32[]{:S(2)}, u32[]{:S(2)}) collective-permute-start(f32[1,2048]{1,0:T(1,128)S(1)} %get-tuple-element.57), channel_id=1, source_target_pairs={{0,12},{4,8},{8,4},{12,0},{1,13},{5,9},{9,5},{13,1},{2,14},{6,10},... | collective-permute-start | bytes 24584 | tf_op jit(solution)/shard_map/ppermute | solution.py:364
  12.7 0.0 collective-permute-start.4
  12.7 2.4 %collective-permute-start.5 = (f32[1,2048]{1,0:T(1,128)S(1)}, f32[1,2048]{1,0:T(1,128)S(1)}, u32[]{:S(2)}, u32[]{:S(2)}) collective-permute-start(f32[1,2048]{1,0:T(1,128)S(1)} %get-tuple-element.59), channel_id=1, source_target_pairs={{0,4},{4,0},{8,12},{12,8},{1,5},{5,1},{9,13},{13,9},{2,6},{6,2},{1... | collective-permute-start | bytes 24584 | tf_op jit(solution)/shard_map/ppermute | solution.py:364
  15.1 2.1 %shard_map.176 = (f32[128,2048]{1,0:T(8,128)S(1)}, f32[1,128]{1,0:T(1,128)S(1)}, f32[4,2048]{1,0:T(4,128)S(1)}, f32[4,2048]{1,0:T(4,128)S(1)}, bf16[128,2048]{1,0:T(8,128)(2,1)}) custom-call(bf16[128,2048]{1,0:T(8,128)(2,1)S(1)} %get-tuple-element.35.fs_ref.refs_0_, bf16[128,2048]{1,0:T(8,128)(2,1)S(1)} %get-tuple-element.36.x_ref, ...), custom_call_target="tpu_custom_call" | custom-call | tf_op jit(solution)/shard_map/pallas_call | solution.py:274
  17.2 0.0 collective-permute-done.3.refs_4_
  17.2 0.1 collective-permute-done.4.refs_5_
  17.3 0.0 collective-permute-done.5.refs_6_
  17.3 0.1 shard_map.178
  17.4 0.0 collective-permute-start.6
  17.4 1.6 %collective-permute-start.7 = (f32[2,128]{1,0:T(2,128)S(1)}, f32[2,128]{1,0:T(2,128)S(1)}, u32[]{:S(2)}, u32[]{:S(2)}) collective-permute-start(f32[2,128]{1,0:T(2,128)S(1)} %get-tuple-element.61.refs_4_), channel_id=1, source_target_pairs={{0,2},{1,3},{2,0},{3,1},{4,6},{5,7},{6,4},{7,5},{8,10},{9,11},{10,... | collective-permute-start | bytes 3080 | tf_op jit(solution)/shard_map/ppermute | solution.py:379
  18.9 0.3 %collective-permute-start.8 = (f32[2,128]{1,0:T(2,128)S(1)}, f32[2,128]{1,0:T(2,128)S(1)}, u32[]{:S(2)}, u32[]{:S(2)}) collective-permute-start(f32[2,128]{1,0:T(2,128)S(1)} %get-tuple-element.61.refs_4_), channel_id=1, source_target_pairs={{0,1},{1,0},{2,3},{3,2},{4,5},{5,4},{6,7},{7,6},{8,9},{9,8},{10,11... | collective-permute-start | bytes 3080 | tf_op jit(solution)/shard_map/ppermute | solution.py:379
  19.2 1.1 %collective-permute-done.6.refs_5_ = f32[2,128]{1,0:T(2,128)S(1)} collective-permute-done((f32[2,128]{1,0:T(2,128)S(1)}, f32[2,128]{1,0:T(2,128)S(1)}, u32[]{:S(2)}, u32[]{:S(2)}) %collective-permute-start.6) | collective-permute-done | bytes 1056 | tf_op jit(solution)/shard_map/ppermute | solution.py:379
  20.4 0.6 %collective-permute-done.7.refs_6_ = f32[2,128]{1,0:T(2,128)S(1)} collective-permute-done((f32[2,128]{1,0:T(2,128)S(1)}, f32[2,128]{1,0:T(2,128)S(1)}, u32[]{:S(2)}, u32[]{:S(2)}) %collective-permute-start.7) | collective-permute-done | bytes 1056 | tf_op jit(solution)/shard_map/ppermute | solution.py:379
  21.0 0.0 collective-permute-done.8.refs_7_
  21.0 1.0 %shard_map.179 = (bf16[128,2048]{1,0:T(8,128)(2,1)}, bf16[4,2048]{1,0:T(4,128)(2,1)}) custom-call(f32[128,128]{1,0:T(8,128)S(1)} %get-tuple-element.34.refs_0_, f32[128,2048]{1,0:T(8,128)S(1)} %get-tuple-element.52.refs_1_, f32[4,2048]{1,0:T(4,128)S(1)} %get-tuple-element.60.refs_2_, f32[1,2048]{1,0:T(1,128)S(1)} %get-tuple-element.44.gain_ref.refs_3_, ...), custom_call_target="tpu_custom_call" | custom-call | tf_op jit(solution)/shard_map/pallas_call | solution.py:274
  (1 shorter events, 0.0 us)
Async XLA Ops:
  0.6 8.4 %collective-permute-start = (bf16[4,512]{1,0:T(4,128)(2,1)}, bf16[4,512]{1,0:T(4,128)(2,1)S(1)}, u32[]{:S(2)}, u32[]{:S(2)}) collective-permute-start(bf16[4,512]{1,0:T(4,128)(2,1)} %bitcast.20), channel_id=1, source_target_pairs={{0,8},{4,12},{8,0},{12,4},{1,9},{5,13},{9,1},{13,5},{2,10},{6,14},... | collective-permute-start | bytes 12296 | tf_op jit(solution)/shard_map/ppermute | solution.py:338
  4.8 5.6 %collective-permute-start.1 = (bf16[4,512]{1,0:T(4,128)(2,1)}, bf16[4,512]{1,0:T(4,128)(2,1)S(1)}, u32[]{:S(2)}, u32[]{:S(2)}) collective-permute-start(bf16[4,512]{1,0:T(4,128)(2,1)} %bitcast.21), channel_id=1, source_target_pairs={{0,12},{4,8},{8,4},{12,0},{1,13},{5,9},{9,5},{13,1},{2,14},{6,10},... | collective-permute-start | bytes 12296 | tf_op jit(solution)/shard_map/ppermute | solution.py:338
  6.1 4.3 %collective-permute-start.2 = (bf16[4,512]{1,0:T(4,128)(2,1)}, bf16[4,512]{1,0:T(4,128)(2,1)S(1)}, u32[]{:S(2)}, u32[]{:S(2)}) collective-permute-start(bf16[4,512]{1,0:T(4,128)(2,1)} %bitcast.22), channel_id=1, source_target_pairs={{0,4},{4,0},{8,12},{12,8},{1,5},{5,1},{9,13},{13,9},{2,6},{6,2},{1... | collective-permute-start | bytes 12296 | tf_op jit(solution)/shard_map/ppermute | solution.py:338
  7.0 3.4 %copy-start = (bf16[1,4,512]{2,1,0:T(4,128)(2,1)S(1)}, bf16[1,4,512]{2,1,0:T(4,128)(2,1)}, u32[]{:S(2)}) copy-start(bf16[1,4,512]{2,1,0:T(4,128)(2,1)} %param.30) | copy-start | bytes 12292
  10.6 6.6 %collective-permute-start.3 = (f32[1,2048]{1,0:T(1,128)S(1)}, f32[1,2048]{1,0:T(1,128)S(1)}, u32[]{:S(2)}, u32[]{:S(2)}) collective-permute-start(f32[1,2048]{1,0:T(1,128)S(1)} %get-tuple-element.57), channel_id=1, source_target_pairs={{0,12},{4,8},{8,4},{12,0},{1,13},{5,9},{9,5},{13,1},{2,14},{6,10},... | collective-permute-start | bytes 24584 | tf_op jit(solution)/shard_map/ppermute | solution.py:364
  12.7 4.5 %collective-permute-start.4 = (f32[1,2048]{1,0:T(1,128)S(1)}, f32[1,2048]{1,0:T(1,128)S(1)}, u32[]{:S(2)}, u32[]{:S(2)}) collective-permute-start(f32[1,2048]{1,0:T(1,128)S(1)} %get-tuple-element.58), channel_id=1, source_target_pairs={{0,8},{4,12},{8,0},{12,4},{1,9},{5,13},{9,1},{13,5},{2,10},{6,14},... | collective-permute-start | bytes 24584 | tf_op jit(solution)/shard_map/ppermute | solution.py:364
  12.7 4.5 %collective-permute-start.5 = (f32[1,2048]{1,0:T(1,128)S(1)}, f32[1,2048]{1,0:T(1,128)S(1)}, u32[]{:S(2)}, u32[]{:S(2)}) collective-permute-start(f32[1,2048]{1,0:T(1,128)S(1)} %get-tuple-element.59), channel_id=1, source_target_pairs={{0,4},{4,0},{8,12},{12,8},{1,5},{5,1},{9,13},{13,9},{2,6},{6,2},{1... | collective-permute-start | bytes 24584 | tf_op jit(solution)/shard_map/ppermute | solution.py:364
  17.4 3.0 %collective-permute-start.6 = (f32[2,128]{1,0:T(2,128)S(1)}, f32[2,128]{1,0:T(2,128)S(1)}, u32[]{:S(2)}, u32[]{:S(2)}) collective-permute-start(f32[2,128]{1,0:T(2,128)S(1)} %get-tuple-element.61.refs_4_), channel_id=1, source_target_pairs={{0,3},{1,2},{2,1},{3,0},{4,7},{5,6},{6,5},{7,4},{8,11},{9,10},{10,... | collective-permute-start | bytes 3080 | tf_op jit(solution)/shard_map/ppermute | solution.py:379
  17.4 3.6 %collective-permute-start.7 = (f32[2,128]{1,0:T(2,128)S(1)}, f32[2,128]{1,0:T(2,128)S(1)}, u32[]{:S(2)}, u32[]{:S(2)}) collective-permute-start(f32[2,128]{1,0:T(2,128)S(1)} %get-tuple-element.61.refs_4_), channel_id=1, source_target_pairs={{0,2},{1,3},{2,0},{3,1},{4,6},{5,7},{6,4},{7,5},{8,10},{9,11},{10,... | collective-permute-start | bytes 3080 | tf_op jit(solution)/shard_map/ppermute | solution.py:379
  18.9 2.1 %collective-permute-start.8 = (f32[2,128]{1,0:T(2,128)S(1)}, f32[2,128]{1,0:T(2,128)S(1)}, u32[]{:S(2)}, u32[]{:S(2)}) collective-permute-start(f32[2,128]{1,0:T(2,128)S(1)} %get-tuple-element.61.refs_4_), channel_id=1, source_target_pairs={{0,1},{1,0},{2,3},{3,2},{4,5},{5,4},{6,7},{7,6},{8,9},{9,8},{10,11... | collective-permute-start | bytes 3080 | tf_op jit(solution)/shard_map/ppermute | solution.py:379

commit v5 on v3

v5 whole, which is shorter than its diff:
```python
import functools

import jax
import jax.numpy as jnp
from jax import lax
from jax.experimental import pallas as pl
from jax.experimental.pallas import tpu as pltpu
from jax.sharding import PartitionSpec as P


H = 128
G = 4
epsilon = 1e-05
f32 = jnp.float32
bf16 = jnp.bfloat16
LOG2E = 1.4426950408889634
CAP = 100.0
CHUNKS = 4
GRANT = 16 << 20


def softplus(v):
    return jnp.maximum(v, 0.0) + jnp.log1p(jnp.exp(-jnp.abs(v)))


def silu(z):
    half = 0.5 * z
    return half * (1.0 + jnp.tanh(half))


def split(v, parts):
    out = []
    for _ in range(parts):
        piece = v.astype(bf16)
        out.append(piece)
        v = v - piece.astype(f32)
    return out


def picks(heads, width, parts):
    per = width // heads
    row = lax.broadcasted_iota(jnp.int32, (heads, width), 0)
    lane = lax.broadcasted_iota(jnp.int32, (heads, width), 1)
    pick = jnp.where((lane >= row * per) & (lane < (row + 1) * per), 1.0, 0.0).astype(bf16)
    return jnp.concatenate([pick] * parts, axis=0)


def widen(v, width, parts):
    lhs = jnp.concatenate(split(v, parts), axis=1)
    return jnp.dot(lhs, picks(v.shape[1], width, parts), preferred_element_type=f32)


def as_column(row):
    n = row.shape[1]
    wide = jnp.broadcast_to(row, (n, n))
    here = lax.broadcasted_iota(jnp.int32, (n, n), 0) == lax.broadcasted_iota(jnp.int32, (n, n), 1)
    return jnp.sum(jnp.where(here, wide, 0.0), axis=1, keepdims=True)


def widen_columns(v, pick_ref):
    lhs = jnp.concatenate(split(v, pick_ref.shape[0] // v.shape[0]), axis=0)
    return lax.dot_general(
        lhs, pick_ref[...], (((0,), (0,)), ((), ())), preferred_element_type=f32
    )


def group_lanes(states, heads_here):
    start = (lax.axis_index("head") * heads_here) // (H // G)
    return pl.ds(pl.multiple_of(start * states, states), states)


def state_kernel(
    valid_ref, dt_hbm, a_hbm, bias_hbm, x_hbm, b_hbm, s0_hbm,
    fs_ref, sums_ref, delta_ref, x_ref, b_ref, s0_ref, a_ref, bias_ref,
    dt_ref, pick_ref, fresh_ref, sems,
):
    heads, length = dt_ref.shape
    width = x_ref.shape[1]
    states = s0_ref.shape[0]
    lanes = group_lanes(states, heads)
    copies = [
        pltpu.make_async_copy(source, target, sems.at[i])
        for i, (source, target) in enumerate((
            (dt_hbm, dt_ref), (a_hbm, a_ref), (bias_hbm, bias_ref),
            (x_hbm, x_ref), (b_hbm.at[:, lanes], b_ref), (s0_hbm, s0_ref),
        ))
    ]
    for copy in copies:
        copy.start()
    row = lax.broadcasted_iota(jnp.int32, (length, length), 0)
    lane = lax.broadcasted_iota(jnp.int32, (length, length), 1)
    upper = jnp.where(row <= lane, 1.0, 0.0).astype(bf16)
    pick_ref[...] = picks(heads, width, 2)
    for copy in copies[:3]:
        copy.wait()
    delta = softplus(dt_ref[...] + as_column(bias_ref[...])) * valid_ref[...]
    rate = delta * as_column(a_ref[...]) * (-LOG2E)
    sums = jnp.dot(
        jnp.concatenate(split(rate, 3), axis=1),
        jnp.concatenate([upper] * 3, axis=0),
        preferred_element_type=f32,
    )
    sums_ref[...] = sums
    delta_ref[...] = delta
    last = sums[:, length - 1 :]
    weight = jnp.exp2(last - sums) * delta
    total = widen_columns(jnp.broadcast_to(jnp.exp2(last), (heads, 8)), pick_ref)[0:1, :]
    wide = widen_columns(weight, pick_ref)
    copies[3].wait()
    copies[4].wait()
    xw = (x_ref[...].astype(f32) * wide).astype(bf16)
    fresh = lax.dot_general(b_ref[...], xw, (((0,), (0,)), ((), ())), preferred_element_type=f32)
    fresh_ref[...] = fresh
    copies[5].wait()
    for i in range(8):
        rows = slice(i * states // 8, (i + 1) * states // 8)
        fs_ref[rows, :] = (fresh_ref[rows, :] + total * s0_ref[rows, :]).astype(bf16)


def read_kernel(fs_ref, query_ref, out_ref):
    states, width = fs_ref.shape
    me = lax.axis_index("sample")
    block = query_ref[:, group_lanes(states, width // 64)].astype(f32)
    mine = lax.broadcasted_iota(jnp.int32, block.shape, 0) == me
    query = jnp.sum(jnp.where(mine, block, 0.0), axis=0, keepdims=True).astype(bf16)
    out_ref[...] = jnp.dot(query, fs_ref[...], preferred_element_type=f32)


def prompt_kernel(
    fs_ref, x_ref, z_ref, b_ref, cp_ref, s0_ref, sums_ref, delta_ref, skip_ref, gain_ref,
    xd_ref, zd_ref, bd_ref, cd_ref, dtd_ref, a_ref, bias_ref,
    gated_ref, sq_ref, u_ref, v_ref, own_ref, fs_hbm, m_ref, sem,
):
    heads, length = sums_ref.shape
    states, width = s0_ref.shape
    per = width // heads
    prompts = xd_ref.shape[0]
    store = pltpu.make_async_copy(fs_ref, fs_hbm, sem)
    store.start()
    lanes = group_lanes(states, heads)
    cp = cp_ref[:, lanes]
    scores = lax.dot_general(cp, b_ref[...], (((1,), (1,)), ((), ())), preferred_element_type=f32)
    row = lax.broadcasted_iota(jnp.int32, (length, length), 0)
    lane = lax.broadcasted_iota(jnp.int32, (length, length), 1)
    scores = jnp.where(row >= lane, scores, 0.0)
    m_ref[...] = jnp.dot(cp, s0_ref[...].astype(bf16), preferred_element_type=f32)

    step = softplus(dtd_ref[...] + bias_ref[...])
    own = cd_ref[:, lanes].astype(f32)
    cb = own * bd_ref[:, lanes].astype(f32)
    cb = jnp.sum(cb, axis=1, keepdims=True)
    gain = step * cb + skip_ref[...]
    skips = jnp.broadcast_to(skip_ref[...], (8, heads))
    wide = widen(jnp.concatenate([jnp.exp(-step * a_ref[...]), gain], axis=0), width, 3)
    skip = widen(skips, width, 3)[0:1, :]
    gate = silu(zd_ref[...].astype(f32))
    u_ref[...] = wide[:prompts] * gate
    v_ref[...] = wide[prompts:] * xd_ref[...].astype(f32) * gate

    mine = lax.broadcasted_iota(jnp.int32, own.shape, 0) == lax.axis_index("sample")
    query = jnp.where(mine, own, 0.0)
    query = jnp.sum(query, axis=0, keepdims=True).astype(bf16)
    own_ref[...] = jnp.dot(query, fs_ref[...], preferred_element_type=f32)

    rt = jnp.log2(delta_ref[...]) - sums_ref[...]
    c = sums_ref[...].T
    pair = 2 * per
    low = lax.broadcasted_iota(jnp.int32, (length, pair), 1) < per
    squares = jnp.zeros((length, pair), f32)
    for q in range(heads // 2):
        ch = slice(q * pair, (q + 1) * pair)
        x = x_ref[:, ch]
        xf = x.astype(f32)
        x_cat = jnp.concatenate(
            [jnp.where(low, xf, 0.0).astype(bf16), jnp.where(low, 0.0, xf).astype(bf16)], axis=0
        )
        parts = []
        cols = []
        for h in (2 * q, 2 * q + 1):
            col = jnp.broadcast_to(c[:, h : h + 1], (length, length))
            arg = jnp.minimum(col + rt[h : h + 1, :], CAP)
            parts.append((jnp.exp2(arg) * scores).astype(bf16))
            cols.append(col)
        y = jnp.dot(jnp.concatenate(parts, axis=1), x_cat, preferred_element_type=f32)
        decay = jnp.exp2(jnp.where(low, cols[0], cols[1]))
        y = y + decay * m_ref[:, ch] + skip[:, ch] * xf
        gated = y * silu(z_ref[:, ch].astype(f32))
        gated_ref[:, ch] = gated * gain_ref[:, ch]
        squares = squares + gated * gated
    total = jnp.broadcast_to(jnp.sum(squares, axis=1, keepdims=True), (length, length))
    sq_ref[...] = total.T[0:1, :]
    store.wait()


def slot_kernel(*refs):
    sq_ref, u_ref, v_ref = refs[:3]
    read_refs = refs[3:-2]
    gated_ref, pay_ref = refs[-2:]
    prompts, width = u_ref.shape
    me = lax.axis_index("sample")
    prompt = lax.broadcasted_iota(jnp.int32, (prompts, width), 0)
    reads = jnp.zeros((prompts, width), f32)
    for k, ref in zip([0] + shifts(prompts), read_refs):
        reads = jnp.where(prompt == lax.rem(me + k, prompts), ref[...], reads)
    gated = u_ref[...] * reads + v_ref[...]
    gated_ref[...] = gated
    total = jnp.broadcast_to(jnp.sum(gated * gated, axis=1, keepdims=True), (prompts, 128))
    row = lax.broadcasted_iota(jnp.int32, (prompts, 128), 0)
    lane = lax.broadcasted_iota(jnp.int32, (prompts, 128), 1)
    pay_ref[0:1, :] = sq_ref[...]
    pay_ref[1:2, :] = jnp.sum(jnp.where(row == lane, total, 0.0), axis=0, keepdims=True)


def norm_kernel(*refs, channels, payloads):
    valid_ref, gated_ref, dec_ref, gain_ref = refs[:4]
    pay_refs = refs[4 : 4 + payloads]
    out_hbm, dec_hbm, out_ref, out_dec_ref, sems = refs[4 + payloads :]
    length = gated_ref.shape[0]
    prompts = dec_ref.shape[0]
    total = pay_refs[0][...]
    for ref in pay_refs[1:]:
        total = total + ref[...]
    scale = lax.rsqrt(total * (1.0 / channels) + epsilon)
    row = lax.broadcasted_iota(jnp.int32, (prompts, 128), 0)
    lane = lax.broadcasted_iota(jnp.int32, (prompts, 128), 1)
    wide = jnp.broadcast_to(scale[1:2, :], (prompts, 128))
    dec = jnp.sum(jnp.where(row == lane, wide, 0.0), axis=1, keepdims=True)
    out_dec_ref[...] = (dec_ref[...] * dec * gain_ref[...]).astype(bf16)
    copies = [pltpu.make_async_copy(out_dec_ref, dec_hbm, sems.at[0])]
    copies[0].start()
    column = jnp.broadcast_to(scale[0:1, :] * valid_ref[...], (length, length)).T[:, 0:1]
    for i in range(CHUNKS):
        rows = slice(i * length // CHUNKS, (i + 1) * length // CHUNKS)
        out_ref[rows, :] = (gated_ref[rows, :] * column[rows, :]).astype(bf16)
        copies.append(
            pltpu.make_async_copy(out_ref.at[rows, :], out_hbm.at[rows, :], sems.at[1 + i])
        )
        copies[-1].start()
    for copy in copies:
        copy.wait()


VMEM = pltpu.MemorySpace.VMEM
HBM = pltpu.MemorySpace.HBM


def call(kernel, ins, outs, scratch=(), far=(), fetch=False):
    spaces = [VMEM if not fetch or i == 0 else HBM for i in range(len(ins))]
    outs = [(VMEM, *out) for out in outs] + [(HBM, *out) for out in far]
    return pl.pallas_call(
        kernel,
        in_specs=[pl.BlockSpec(memory_space=space) for space in spaces],
        out_specs=tuple(pl.BlockSpec(memory_space=out[0]) for out in outs),
        out_shape=tuple(out[0](*out[1:]) for out in outs),
        scratch_shapes=list(scratch),
        compiler_params=pltpu.CompilerParams(vmem_limit_bytes=GRANT),
    )(*(pltpu.with_memory_space_constraint(v, space) for v, space in zip(ins, spaces)))


def shifts(n):
    return [k for j in range(1, n // 2 + 1) for k in dict.fromkeys((j, n - j))]


def make_body(mesh):
    samples = mesh.shape["sample"]
    head_parts = mesh.shape["head"]

    def body(
        x_pre, z_pre, b_pre, c_pre, dt_pre, lengths, init_state, a_rates, dt_bias, skip_scale,
        norm_gain, x_dec, z_dec, b_dec, c_dec, dt_dec,
    ):
        return layer(
            x_pre, z_pre, b_pre, c_pre, dt_pre, lengths, init_state, a_rates, dt_bias,
            skip_scale, norm_gain, x_dec, z_dec, b_dec, c_dec, dt_dec,
        )

    def layer(
        x_pre, z_pre, b_pre, c_pre, dt_pre, lengths, init_state, a_rates, dt_bias, skip_scale,
        norm_gain, x_dec, z_dec, b_dec, c_dec, dt_dec,
    ):
        length, width = x_pre.shape[1:]
        states = init_state.shape[1]
        heads = a_rates.shape[0]
        prompts = x_dec.shape[1]
        x, z, b, cp, dt, s0 = (v[0] for v in (x_pre, z_pre, b_pre, c_pre, dt_pre, init_state))
        xd, zd, bd, cd, dtd = (v[0] for v in (x_dec, z_dec, b_dec, c_dec, dt_dec))
        a, bias, skip, gain = (v[None] for v in (a_rates, dt_bias, skip_scale, norm_gain))

        def shifted(v, k):
            pairs = [(j, (j + k) % samples) for j in range(samples)]
            return lax.ppermute(v, "sample", pairs)

        queries = [shifted(cd, k) for k in shifts(samples)]
        positions = jnp.arange(length, dtype=jnp.int32)
        valid = (positions[None, :] < lengths[:, None]).astype(f32)
        fs, sums, delta, x, b, s0, a, bias = call(
            state_kernel, (valid, dt.T, a, bias, x, b, s0),
            (
                ((states, width), bf16), ((heads, length), f32), ((heads, length), f32),
                ((length, width), bf16), ((length, states), bf16), ((states, width), f32),
                ((1, heads), f32), ((1, heads), f32),
            ),
            (
                pltpu.VMEM((heads, length), f32), pltpu.VMEM((2 * heads, width), bf16),
                pltpu.VMEM((states, width), f32),
                pltpu.SemaphoreType.DMA((6,)),
            ), fetch=True,
        )
        reads = []
        for k, query in zip(shifts(samples), queries):
            (answer,) = call(read_kernel, (fs, query), (((1, width), f32),))
            reads.append(shifted(answer, -k))
        gated, sq, u, v, mine, fs = call(
            prompt_kernel,
            (fs, x, z, b, cp, s0, sums, delta, skip, gain, xd, zd, bd, cd, dtd, a, bias),
            (((length, width), f32), ((1, length), f32)) + (((prompts, width), f32),) * 2
            + (((1, width), f32),),
            (pltpu.VMEM((length, width), f32), pltpu.SemaphoreType.DMA(())),
            (((states, width), bf16),),
        )
        gated_dec, pay = call(
            slot_kernel, (sq, u, v, mine, *reads),
            (((prompts, width), f32), ((2, 128), f32)),
        )
        pays = [pay] + [
            lax.ppermute(pay, "head", [(j, j ^ k) for j in range(head_parts)])
            for k in range(head_parts - 1, 0, -1)
        ]
        out_pre, out_dec = call(
            functools.partial(norm_kernel, channels=width * head_parts, payloads=head_parts),
            (valid, gated, gated_dec, gain, *pays), (),
            (
                pltpu.VMEM((length, width), bf16), pltpu.VMEM((prompts, width), bf16),
                pltpu.SemaphoreType.DMA((1 + CHUNKS,)),
            ), (((length, width), bf16), ((prompts, width), bf16)),
        )
        return out_pre[None], fs[None], out_dec[None]

    return body


def solution(mesh):
    tokens = P(("rep", "sample"), None, "head")
    groups = P(("rep", "sample"), None, None)
    in_specs = (
        tokens, tokens, groups, groups, tokens, P(("rep", "sample")), tokens,
        P("head"), P("head"), P("head"), P("head"), tokens, tokens, groups, groups, tokens,
    )
    return jax.shard_map(
        make_body(mesh), mesh=mesh, in_specs=in_specs, out_specs=(tokens,) * 3, check_vma=False
    )
```

time: 25 us -> 21.7 us (0.87)
  waiting for transfers between devices: 6.05 us -> 2.12 us
  local copies, waits for them, and re-layouts: 0.01 us -> 0.67 us
  Pallas kernels: 5.44 us -> 5.12 us
    ppermute x9, waiting for transfers between devices: 6.05 us -> 2.12 us  [the longest x3 1.78 us: layer(): lax.ppermute(pay, 'head', [(j, j ^ k) for j in range(head_parts)])]
    unnamed x2 -> x18, local copies, waits for them, and re-layouts: 0.01 us -> 0.67 us
    pallas_call x5 -> x7, Pallas kernels: 5.44 us -> 5.12 us  [call(): pl.pallas_call(kernel, in_specs=[pl.BlockSpec(memory_space=space) for spa...]
  transfers between devices with their start and end apart: 9 -> 9, of which waited for: 4 -> 4; matrix products, arithmetic and copies ran while one was open for 0% -> 0% of each run, Pallas kernels for 17% -> 19%
where the time goes in v5:
time: 21.7 us; the launch traced here: 21.5 us
  starting transfers between devices  12.2 us (56%)
  Pallas kernels  5.12 us (24%)
  waiting for transfers between devices  2.12 us (10%)
  between operations  1.4 us (6%)
  local copies, waits for them, and re-layouts  0.67 us (3%)
    ppermute x6, starting transfers between devices, shifted(): return lax.ppermute(v, 'sample', pairs)  10.3 us
    pallas_call x7, Pallas kernels, call(): pl.pallas_call(kernel, in_specs=[pl.BlockSpec(memory_space=space) for spa...  5.12 us
    ppermute x3, starting transfers between devices, layer(): lax.ppermute(pay, 'head', [(j, j ^ k) for j in range(head_parts)])  1.86 us
    ppermute x3, waiting for transfers between devices, layer(): lax.ppermute(pay, 'head', [(j, j ^ k) for j in range(head_parts)])  1.78 us
    unnamed x18, local copies, waits for them, and re-layouts  0.67 us
  transfers between devices with their start and end apart: 9, of which 4 were waited for; matrix products, arithmetic and copies ran while one was open for 0% of the time, Pallas kernels for 19%

profile of v5, /device:TPU:0, one launch (start us, length us, event | category | flops | bytes accessed | tf_op | source)
XLA Modules:
  0.0 21.5 jit_solution(5957046440940132091)
XLA Ops:
  0.6 3.1 %collective-permute-start = (bf16[4,512]{1,0:T(4,128)(2,1)}, bf16[4,512]{1,0:T(4,128)(2,1)S(1)}, u32[]{:S(2)}, u32[]{:S(2)}) collective-permute-start(bf16[4,512]{1,0:T(4,128)(2,1)} %bitcast.29), channel_id=1, source_target_pairs={{0,4},{4,8},{8,12},{12,0},{1,5},{5,9},{9,13},{13,1},{2,6},{6,10},{... | collective-permute-start | bytes 12296 | tf_op jit(solution)/shard_map/ppermute | solution.py:291
  3.7 2.1 %collective-permute-start.2 = (bf16[4,512]{1,0:T(4,128)(2,1)}, bf16[4,512]{1,0:T(4,128)(2,1)S(1)}, u32[]{:S(2)}, u32[]{:S(2)}) collective-permute-start(bf16[4,512]{1,0:T(4,128)(2,1)} %bitcast.30), channel_id=1, source_target_pairs={{0,12},{4,0},{8,4},{12,8},{1,13},{5,1},{9,5},{13,9},{2,14},{6,2},{... | collective-permute-start | bytes 12296 | tf_op jit(solution)/shard_map/ppermute | solution.py:291
  5.8 0.9 %collective-permute-start.4 = (bf16[4,512]{1,0:T(4,128)(2,1)}, bf16[4,512]{1,0:T(4,128)(2,1)S(1)}, u32[]{:S(2)}, u32[]{:S(2)}) collective-permute-start(bf16[4,512]{1,0:T(4,128)(2,1)} %bitcast.31), channel_id=1, source_target_pairs={{0,8},{4,12},{8,0},{12,4},{1,9},{5,13},{9,1},{13,5},{2,10},{6,14},... | collective-permute-start | bytes 12296 | tf_op jit(solution)/shard_map/ppermute | solution.py:291
  7.4 1.9 %shard_map.175 = (bf16[128,2048]{1,0:T(8,128)(2,1)S(1)}, f32[32,128]{1,0:T(8,128)S(1)}, f32[32,128]{1,0:T(8,128)S(1)}, bf16[128,2048]{1,0:T(8,128)(2,1)S(1)}, bf...) custom-call(f32[1,128]{1,0:T(1,128)S(1)} %compare_convert_fusion.valid_ref.refs, ...), custom_call_target="tpu_custom_call" | custom-call | tf_op jit(solution)/shard_map/pallas_call | solution.py:250
  9.4 0.2 shard_map.177
  9.5 1.4 %collective-permute-start.1 = (f32[1,2048]{1,0:T(1,128)S(1)}, f32[1,2048]{1,0:T(1,128)S(1)}, u32[]{:S(2)}, u32[]{:S(2)}) collective-permute-start(f32[1,2048]{1,0:T(1,128)S(1)} %shard_map.177), channel_id=1, source_target_pairs={{0,12},{4,0},{8,4},{12,8},{1,13},{5,1},{9,5},{13,9},{2,14},{6,2},{... | collective-permute-start | bytes 24584 | tf_op jit(solution)/shard_map/ppermute | solution.py:291
  10.9 0.2 shard_map.178
  11.1 0.7 %collective-permute-start.3 = (f32[1,2048]{1,0:T(1,128)S(1)}, f32[1,2048]{1,0:T(1,128)S(1)}, u32[]{:S(2)}, u32[]{:S(2)}) collective-permute-start(f32[1,2048]{1,0:T(1,128)S(1)} %shard_map.178), channel_id=1, source_target_pairs={{0,4},{4,8},{8,12},{12,0},{1,5},{5,9},{9,13},{13,1},{2,6},{6,10},{... | collective-permute-start | bytes 24584 | tf_op jit(solution)/shard_map/ppermute | solution.py:291
  11.9 0.0 copy-start.8
  11.9 0.2 shard_map.179
  12.1 2.0 %collective-permute-start.5 = (f32[1,2048]{1,0:T(1,128)S(1)}, f32[1,2048]{1,0:T(1,128)S(1)}, u32[]{:S(2)}, u32[]{:S(2)}) collective-permute-start(f32[1,2048]{1,0:T(1,128)S(1)} %shard_map.179), channel_id=1, source_target_pairs={{0,8},{4,12},{8,0},{12,4},{1,9},{5,13},{9,1},{13,5},{2,10},{6,14},... | collective-permute-start | bytes 24584 | tf_op jit(solution)/shard_map/ppermute | solution.py:291
  14.2 0.6 %copy-done.2 = f32[2048]{0:T(1024)S(1)} copy-done((f32[2048]{0:T(1024)S(1)}, f32[2048]{0:T(1024)}, u32[]{:S(2)}) %copy-start.2) | copy-done | bytes 8216
  14.8 0.0 copy-done.5
  14.8 1.5 %shard_map.176 = (f32[128,2048]{1,0:T(8,128)S(1)}, f32[1,128]{1,0:T(1,128)S(1)}, f32[4,2048]{1,0:T(4,128)S(1)}, f32[4,2048]{1,0:T(4,128)S(1)}, f32[1,2048]{1,0:T(1,128)S(1)}, /*index=5*/bf16[128,2048]{1,0:T(8,128)(2,1)}) custom-call(bf16[128,2048]{1,0:T(8,128)(2,1)S(1)} %get-tuple-element.21.fs_ref, bf16[128,2048]{1,0:T(8,128)(2,1)S(1)} %get-tuple-element.22.x_ref, ...), custom_call_target="tpu_custom_call" | custom-call | tf_op jit(solution)/shard_map/pallas_call | solution.py:250
  16.4 0.2 %collective-permute-done.3.refs_5_ = f32[1,2048]{1,0:T(1,128)S(1)} collective-permute-done((f32[1,2048]{1,0:T(1,128)S(1)}, f32[1,2048]{1,0:T(1,128)S(1)}, u32[]{:S(2)}, u32[]{:S(2)}) %collective-permute-start.3) | collective-permute-done | bytes 8224 | tf_op jit(solution)/shard_map/ppermute | solution.py:291
  16.6 0.1 collective-permute-done.5.refs_6_
  16.7 0.1 shard_map.180
  16.8 0.0 collective-permute-start.6
  16.8 1.6 %collective-permute-start.7 = (f32[2,128]{1,0:T(2,128)S(1)}, f32[2,128]{1,0:T(2,128)S(1)}, u32[]{:S(2)}, u32[]{:S(2)}) collective-permute-start(f32[2,128]{1,0:T(2,128)S(1)} %get-tuple-element.35.refs_4_), channel_id=1, source_target_pairs={{0,2},{1,3},{2,0},{3,1},{4,6},{5,7},{6,4},{7,5},{8,10},{9,11},{10,... | collective-permute-start | bytes 3080 | tf_op jit(solution)/shard_map/ppermute | solution.py:326
  18.4 0.3 %collective-permute-start.8 = (f32[2,128]{1,0:T(2,128)S(1)}, f32[2,128]{1,0:T(2,128)S(1)}, u32[]{:S(2)}, u32[]{:S(2)}) collective-permute-start(f32[2,128]{1,0:T(2,128)S(1)} %get-tuple-element.35.refs_4_), channel_id=1, source_target_pairs={{0,1},{1,0},{2,3},{3,2},{4,5},{5,4},{6,7},{7,6},{8,9},{9,8},{10,11... | collective-permute-start | bytes 3080 | tf_op jit(solution)/shard_map/ppermute | solution.py:326
  18.7 1.1 %collective-permute-done.6.refs_5_ = f32[2,128]{1,0:T(2,128)S(1)} collective-permute-done((f32[2,128]{1,0:T(2,128)S(1)}, f32[2,128]{1,0:T(2,128)S(1)}, u32[]{:S(2)}, u32[]{:S(2)}) %collective-permute-start.6) | collective-permute-done | bytes 1056 | tf_op jit(solution)/shard_map/ppermute | solution.py:326
  19.8 0.6 %collective-permute-done.7.refs_6_ = f32[2,128]{1,0:T(2,128)S(1)} collective-permute-done((f32[2,128]{1,0:T(2,128)S(1)}, f32[2,128]{1,0:T(2,128)S(1)}, u32[]{:S(2)}, u32[]{:S(2)}) %collective-permute-start.7) | collective-permute-done | bytes 1056 | tf_op jit(solution)/shard_map/ppermute | solution.py:326
  20.5 0.0 collective-permute-done.8.refs_7_
  20.5 1.0 %shard_map.181 = (bf16[128,2048]{1,0:T(8,128)(2,1)}, bf16[4,2048]{1,0:T(4,128)(2,1)}) custom-call(f32[1,128]{1,0:T(1,128)S(1)} %compare_convert_fusion.valid_ref.refs_0_, f32[128,2048]{1,0:T(8,128)S(1)} %get-tuple-element.29.refs_1_, f32[4,2048]{1,0:T(4,128)S(1)} %get-tuple-element.34.refs_2_, f32[1,2048]{1,0:T(1,128)S(1)} %bitcast.25, ...), custom_call_target="tpu_custom_call" | custom-call | tf_op jit(solution)/shard_map/pallas_call | solution.py:250
  (20 shorter events, 0.0 us)
Async XLA Ops:
  0.6 8.7 %collective-permute-start = (bf16[4,512]{1,0:T(4,128)(2,1)}, bf16[4,512]{1,0:T(4,128)(2,1)S(1)}, u32[]{:S(2)}, u32[]{:S(2)}) collective-permute-start(bf16[4,512]{1,0:T(4,128)(2,1)} %bitcast.29), channel_id=1, source_target_pairs={{0,4},{4,8},{8,12},{12,0},{1,5},{5,9},{9,13},{13,1},{2,6},{6,10},{... | collective-permute-start | bytes 12296 | tf_op jit(solution)/shard_map/ppermute | solution.py:291
  3.7 7.2 %collective-permute-start.2 = (bf16[4,512]{1,0:T(4,128)(2,1)}, bf16[4,512]{1,0:T(4,128)(2,1)S(1)}, u32[]{:S(2)}, u32[]{:S(2)}) collective-permute-start(bf16[4,512]{1,0:T(4,128)(2,1)} %bitcast.30), channel_id=1, source_target_pairs={{0,12},{4,0},{8,4},{12,8},{1,13},{5,1},{9,5},{13,9},{2,14},{6,2},{... | collective-permute-start | bytes 12296 | tf_op jit(solution)/shard_map/ppermute | solution.py:291
  5.8 6.0 %collective-permute-start.4 = (bf16[4,512]{1,0:T(4,128)(2,1)}, bf16[4,512]{1,0:T(4,128)(2,1)S(1)}, u32[]{:S(2)}, u32[]{:S(2)}) collective-permute-start(bf16[4,512]{1,0:T(4,128)(2,1)} %bitcast.31), channel_id=1, source_target_pairs={{0,8},{4,12},{8,0},{12,4},{1,9},{5,13},{9,1},{13,5},{2,10},{6,14},... | collective-permute-start | bytes 12296 | tf_op jit(solution)/shard_map/ppermute | solution.py:291
  9.5 4.6 %copy-start = (bf16[1,128,2048]{2,1,0:T(8,128)(2,1)S(1)}, bf16[1,128,2048]{2,1,0:T(8,128)(2,1)}, u32[]{:S(2)}) copy-start(bf16[1,128,2048]{2,1,0:T(8,128)(2,1)} %param.17) | copy-start | bytes 1572868
  9.5 6.8 %collective-permute-start.1 = (f32[1,2048]{1,0:T(1,128)S(1)}, f32[1,2048]{1,0:T(1,128)S(1)}, u32[]{:S(2)}, u32[]{:S(2)}) collective-permute-start(f32[1,2048]{1,0:T(1,128)S(1)} %shard_map.177), channel_id=1, source_target_pairs={{0,12},{4,0},{8,4},{12,8},{1,13},{5,1},{9,5},{13,9},{2,14},{6,2},{... | collective-permute-start | bytes 24584 | tf_op jit(solution)/shard_map/ppermute | solution.py:291
  11.1 3.0 %copy-start.1 = (bf16[1,128,512]{2,1,0:T(8,128)(2,1)S(1)}, bf16[1,128,512]{2,1,0:T(8,128)(2,1)}, u32[]{:S(2)}) copy-start(bf16[1,128,512]{2,1,0:T(8,128)(2,1)} %param.19) | copy-start | bytes 393220
  11.1 5.5 %collective-permute-start.3 = (f32[1,2048]{1,0:T(1,128)S(1)}, f32[1,2048]{1,0:T(1,128)S(1)}, u32[]{:S(2)}, u32[]{:S(2)}) collective-permute-start(f32[1,2048]{1,0:T(1,128)S(1)} %shard_map.178), channel_id=1, source_target_pairs={{0,4},{4,8},{8,12},{12,0},{1,5},{5,9},{9,13},{13,1},{2,6},{6,10},{... | collective-permute-start | bytes 24584 | tf_op jit(solution)/shard_map/ppermute | solution.py:291
  11.9 2.3 %copy-start.4 = (bf16[1,4,2048]{2,1,0:T(4,128)(2,1)S(1)}, bf16[1,4,2048]{2,1,0:T(4,128)(2,1)}, u32[]{:S(2)}) copy-start(bf16[1,4,2048]{2,1,0:T(4,128)(2,1)} %param.28) | copy-start | bytes 49156
  11.9 2.3 %copy-start.6 = (bf16[1,4,512]{2,1,0:T(4,128)(2,1)S(1)}, bf16[1,4,512]{2,1,0:T(4,128)(2,1)}, u32[]{:S(2)}) copy-start(bf16[1,4,512]{2,1,0:T(4,128)(2,1)} %param.30) | copy-start | bytes 12292
  11.9 2.3 %copy-start.7 = (f32[1,4,32]{2,1,0:T(4,128)S(1)}, f32[1,4,32]{2,1,0:T(4,128)}, u32[]{:S(2)}) copy-start(f32[1,4,32]{2,1,0:T(4,128)} %param.31) | copy-start | bytes 1540
  11.9 2.3 %copy-start.8 = (f32[32]{0:T(128)S(1)}, f32[32]{0:T(128)}, u32[]{:S(2)}) copy-start(f32[32]{0:T(128)} %param.25) | copy-start | bytes 388
  12.1 2.1 %copy-start.3 = (bf16[1,4,2048]{2,1,0:T(4,128)(2,1)S(1)}, bf16[1,4,2048]{2,1,0:T(4,128)(2,1)}, u32[]{:S(2)}) copy-start(bf16[1,4,2048]{2,1,0:T(4,128)(2,1)} %param.27) | copy-start | bytes 49156
  12.1 4.6 %collective-permute-start.5 = (f32[1,2048]{1,0:T(1,128)S(1)}, f32[1,2048]{1,0:T(1,128)S(1)}, u32[]{:S(2)}, u32[]{:S(2)}) collective-permute-start(f32[1,2048]{1,0:T(1,128)S(1)} %shard_map.179), channel_id=1, source_target_pairs={{0,8},{4,12},{8,0},{12,4},{1,9},{5,13},{9,1},{13,5},{2,10},{6,14},... | collective-permute-start | bytes 24584 | tf_op jit(solution)/shard_map/ppermute | solution.py:291
  14.1 0.7 %copy-start.2 = (f32[2048]{0:T(1024)S(1)}, f32[2048]{0:T(1024)}, u32[]{:S(2)}) copy-start(f32[2048]{0:T(1024)} %param.26) | copy-start | bytes 24580
  14.1 0.7 %copy-start.5 = (bf16[1,4,512]{2,1,0:T(4,128)(2,1)S(1)}, bf16[1,4,512]{2,1,0:T(4,128)(2,1)}, u32[]{:S(2)}) copy-start(bf16[1,4,512]{2,1,0:T(4,128)(2,1)} %param.29) | copy-start | bytes 12292
  16.8 3.0 %collective-permute-start.6 = (f32[2,128]{1,0:T(2,128)S(1)}, f32[2,128]{1,0:T(2,128)S(1)}, u32[]{:S(2)}, u32[]{:S(2)}) collective-permute-start(f32[2,128]{1,0:T(2,128)S(1)} %get-tuple-element.35.refs_4_), channel_id=1, source_target_pairs={{0,3},{1,2},{2,1},{3,0},{4,7},{5,6},{6,5},{7,4},{8,11},{9,10},{10,... | collective-permute-start | bytes 3080 | tf_op jit(solution)/shard_map/ppermute | solution.py:326
  16.8 3.6 %collective-permute-start.7 = (f32[2,128]{1,0:T(2,128)S(1)}, f32[2,128]{1,0:T(2,128)S(1)}, u32[]{:S(2)}, u32[]{:S(2)}) collective-permute-start(f32[2,128]{1,0:T(2,128)S(1)} %get-tuple-element.35.refs_4_), channel_id=1, source_target_pairs={{0,2},{1,3},{2,0},{3,1},{4,6},{5,7},{6,4},{7,5},{8,10},{9,11},{10,... | collective-permute-start | bytes 3080 | tf_op jit(solution)/shard_map/ppermute | solution.py:326
  18.4 2.1 %collective-permute-start.8 = (f32[2,128]{1,0:T(2,128)S(1)}, f32[2,128]{1,0:T(2,128)S(1)}, u32[]{:S(2)}, u32[]{:S(2)}) collective-permute-start(f32[2,128]{1,0:T(2,128)S(1)} %get-tuple-element.35.refs_4_), channel_id=1, source_target_pairs={{0,1},{1,0},{2,3},{3,2},{4,5},{5,4},{6,7},{7,6},{8,9},{9,8},{10,11... | collective-permute-start | bytes 3080 | tf_op jit(solution)/shard_map/ppermute | solution.py:326

commit v6 on v5

--- a/solution.py
+++ b/solution.py
@@ -62,6 +62,15 @@
     return lax.dot_general(
         lhs, pick_ref[...], (((0,), (0,)), ((), ())), preferred_element_type=f32
     )
+
+
+def widen_row(v, width):
+    heads = v.shape[0]
+    per = width // heads
+    wide = jnp.broadcast_to(v, (heads, 2 * per))
+    low = lax.broadcasted_iota(jnp.int32, (1, 2 * per), 1) < per
+    rows = [jnp.where(low, wide[i : i + 1], wide[i + 1 : i + 2]) for i in range(0, heads, 2)]
+    return jnp.concatenate(rows, axis=1)
 
 
 def group_lanes(states, heads_here):
@@ -104,16 +113,16 @@
     delta_ref[...] = delta
     last = sums[:, length - 1 :]
     weight = jnp.exp2(last - sums) * delta
-    total = widen_columns(jnp.broadcast_to(jnp.exp2(last), (heads, 8)), pick_ref)[0:1, :]
-    wide = widen_columns(weight, pick_ref)
+    total = widen_row(jnp.exp2(last), width)
     copies[3].wait()
     copies[4].wait()
+    wide = widen_columns(weight, pick_ref)
     xw = (x_ref[...].astype(f32) * wide).astype(bf16)
     fresh = lax.dot_general(b_ref[...], xw, (((0,), (0,)), ((), ())), preferred_element_type=f32)
     fresh_ref[...] = fresh
     copies[5].wait()
-    for i in range(8):
-        rows = slice(i * states // 8, (i + 1) * states // 8)
+    for i in range(16):
+        rows = slice(i * states // 16, (i + 1) * states // 16)
         fs_ref[rows, :] = (fresh_ref[rows, :] + total * s0_ref[rows, :]).astype(bf16)
 
 

time: 21.7 us -> 21.6 us (level)
  transfers between devices with their start and end apart: 9 -> 9, of which waited for: 4 -> 4; matrix products, arithmetic and copies ran while one was open for 0% -> 0% of each run, Pallas kernels for 19% -> 18%
where the time goes in v6:
time: 21.6 us; the launch traced here: 21.4 us
  starting transfers between devices  12.2 us (56%)
  Pallas kernels  4.99 us (23%)
  waiting for transfers between devices  2.13 us (10%)
  between operations  1.4 us (6%)
  local copies, waits for them, and re-layouts  0.67 us (3%)
    ppermute x6, starting transfers between devices, shifted(): return lax.ppermute(v, 'sample', pairs)  10.3 us
    pallas_call x7, Pallas kernels, call(): pl.pallas_call(kernel, in_specs=[pl.BlockSpec(memory_space=space) for spa...  4.99 us
    ppermute x3, starting transfers between devices, layer(): lax.ppermute(pay, 'head', [(j, j ^ k) for j in range(head_parts)])  1.86 us
    ppermute x3, waiting for transfers between devices, layer(): lax.ppermute(pay, 'head', [(j, j ^ k) for j in range(head_parts)])  1.78 us
    unnamed x18, local copies, waits for them, and re-layouts  0.67 us
  transfers between devices with their start and end apart: 9, of which 4 were waited for; matrix products, arithmetic and copies ran while one was open for 0% of the time, Pallas kernels for 18%

profile of v6, /device:TPU:0, one launch (start us, length us, event | category | flops | bytes accessed | tf_op | source)
XLA Modules:
  0.0 21.4 jit_solution(5883804864244264976)
XLA Ops:
  0.6 3.1 %collective-permute-start = (bf16[4,512]{1,0:T(4,128)(2,1)}, bf16[4,512]{1,0:T(4,128)(2,1)S(1)}, u32[]{:S(2)}, u32[]{:S(2)}) collective-permute-start(bf16[4,512]{1,0:T(4,128)(2,1)} %bitcast.29), channel_id=1, source_target_pairs={{0,4},{4,8},{8,12},{12,0},{1,5},{5,9},{9,13},{13,1},{2,6},{6,10},{... | collective-permute-start | bytes 12296 | tf_op jit(solution)/shard_map/ppermute | solution.py:300
  3.7 2.1 %collective-permute-start.2 = (bf16[4,512]{1,0:T(4,128)(2,1)}, bf16[4,512]{1,0:T(4,128)(2,1)S(1)}, u32[]{:S(2)}, u32[]{:S(2)}) collective-permute-start(bf16[4,512]{1,0:T(4,128)(2,1)} %bitcast.30), channel_id=1, source_target_pairs={{0,12},{4,0},{8,4},{12,8},{1,13},{5,1},{9,5},{13,9},{2,14},{6,2},{... | collective-permute-start | bytes 12296 | tf_op jit(solution)/shard_map/ppermute | solution.py:300
  5.8 0.9 %collective-permute-start.4 = (bf16[4,512]{1,0:T(4,128)(2,1)}, bf16[4,512]{1,0:T(4,128)(2,1)S(1)}, u32[]{:S(2)}, u32[]{:S(2)}) collective-permute-start(bf16[4,512]{1,0:T(4,128)(2,1)} %bitcast.31), channel_id=1, source_target_pairs={{0,8},{4,12},{8,0},{12,4},{1,9},{5,13},{9,1},{13,5},{2,10},{6,14},... | collective-permute-start | bytes 12296 | tf_op jit(solution)/shard_map/ppermute | solution.py:300
  7.4 1.8 %shard_map.175 = (bf16[128,2048]{1,0:T(8,128)(2,1)S(1)}, f32[32,128]{1,0:T(8,128)S(1)}, f32[32,128]{1,0:T(8,128)S(1)}, bf16[128,2048]{1,0:T(8,128)(2,1)S(1)}, bf...) custom-call(f32[1,128]{1,0:T(1,128)S(1)} %compare_convert_fusion.valid_ref.refs, ...), custom_call_target="tpu_custom_call" | custom-call | tf_op jit(solution)/shard_map/pallas_call | solution.py:259
  9.2 0.0 collective-permute-done.query_ref
  9.2 0.2 shard_map.177
  9.4 1.4 %collective-permute-start.1 = (f32[1,2048]{1,0:T(1,128)S(1)}, f32[1,2048]{1,0:T(1,128)S(1)}, u32[]{:S(2)}, u32[]{:S(2)}) collective-permute-start(f32[1,2048]{1,0:T(1,128)S(1)} %shard_map.177), channel_id=1, source_target_pairs={{0,12},{4,0},{8,4},{12,8},{1,13},{5,1},{9,5},{13,9},{2,14},{6,2},{... | collective-permute-start | bytes 24584 | tf_op jit(solution)/shard_map/ppermute | solution.py:300
  10.8 0.0 collective-permute-done.2.query_ref
  10.8 0.2 shard_map.178
  11.0 0.7 %collective-permute-start.3 = (f32[1,2048]{1,0:T(1,128)S(1)}, f32[1,2048]{1,0:T(1,128)S(1)}, u32[]{:S(2)}, u32[]{:S(2)}) collective-permute-start(f32[1,2048]{1,0:T(1,128)S(1)} %shard_map.178), channel_id=1, source_target_pairs={{0,4},{4,8},{8,12},{12,0},{1,5},{5,9},{9,13},{13,1},{2,6},{6,10},{... | collective-permute-start | bytes 24584 | tf_op jit(solution)/shard_map/ppermute | solution.py:300
  11.8 0.0 copy-start.8
  11.8 0.2 shard_map.179
  12.0 2.0 %collective-permute-start.5 = (f32[1,2048]{1,0:T(1,128)S(1)}, f32[1,2048]{1,0:T(1,128)S(1)}, u32[]{:S(2)}, u32[]{:S(2)}) collective-permute-start(f32[1,2048]{1,0:T(1,128)S(1)} %shard_map.179), channel_id=1, source_target_pairs={{0,8},{4,12},{8,0},{12,4},{1,9},{5,13},{9,1},{13,5},{2,10},{6,14},... | collective-permute-start | bytes 24584 | tf_op jit(solution)/shard_map/ppermute | solution.py:300
  14.1 0.6 %copy-done.2 = f32[2048]{0:T(1024)S(1)} copy-done((f32[2048]{0:T(1024)S(1)}, f32[2048]{0:T(1024)}, u32[]{:S(2)}) %copy-start.2) | copy-done | bytes 8216
  14.7 0.0 copy-done.5
  14.7 1.5 %shard_map.176 = (f32[128,2048]{1,0:T(8,128)S(1)}, f32[1,128]{1,0:T(1,128)S(1)}, f32[4,2048]{1,0:T(4,128)S(1)}, f32[4,2048]{1,0:T(4,128)S(1)}, f32[1,2048]{1,0:T(1,128)S(1)}, /*index=5*/bf16[128,2048]{1,0:T(8,128)(2,1)}) custom-call(bf16[128,2048]{1,0:T(8,128)(2,1)S(1)} %get-tuple-element.21.fs_ref, bf16[128,2048]{1,0:T(8,128)(2,1)S(1)} %get-tuple-element.22.x_ref, ...), custom_call_target="tpu_custom_call" | custom-call | tf_op jit(solution)/shard_map/pallas_call | solution.py:259
  16.3 0.3 %collective-permute-done.3.refs_5_ = f32[1,2048]{1,0:T(1,128)S(1)} collective-permute-done((f32[1,2048]{1,0:T(1,128)S(1)}, f32[1,2048]{1,0:T(1,128)S(1)}, u32[]{:S(2)}, u32[]{:S(2)}) %collective-permute-start.3) | collective-permute-done | bytes 8224 | tf_op jit(solution)/shard_map/ppermute | solution.py:300
  16.5 0.1 collective-permute-done.5.refs_6_
  16.6 0.1 shard_map.180
  16.7 1.6 %collective-permute-start.7 = (f32[2,128]{1,0:T(2,128)S(1)}, f32[2,128]{1,0:T(2,128)S(1)}, u32[]{:S(2)}, u32[]{:S(2)}) collective-permute-start(f32[2,128]{1,0:T(2,128)S(1)} %get-tuple-element.35.refs_4_), channel_id=1, source_target_pairs={{0,2},{1,3},{2,0},{3,1},{4,6},{5,7},{6,4},{7,5},{8,10},{9,11},{10,... | collective-permute-start | bytes 3080 | tf_op jit(solution)/shard_map/ppermute | solution.py:335
  18.3 0.3 %collective-permute-start.8 = (f32[2,128]{1,0:T(2,128)S(1)}, f32[2,128]{1,0:T(2,128)S(1)}, u32[]{:S(2)}, u32[]{:S(2)}) collective-permute-start(f32[2,128]{1,0:T(2,128)S(1)} %get-tuple-element.35.refs_4_), channel_id=1, source_target_pairs={{0,1},{1,0},{2,3},{3,2},{4,5},{5,4},{6,7},{7,6},{8,9},{9,8},{10,11... | collective-permute-start | bytes 3080 | tf_op jit(solution)/shard_map/ppermute | solution.py:335
  18.6 1.1 %collective-permute-done.6.refs_5_ = f32[2,128]{1,0:T(2,128)S(1)} collective-permute-done((f32[2,128]{1,0:T(2,128)S(1)}, f32[2,128]{1,0:T(2,128)S(1)}, u32[]{:S(2)}, u32[]{:S(2)}) %collective-permute-start.6) | collective-permute-done | bytes 1056 | tf_op jit(solution)/shard_map/ppermute | solution.py:335
  19.7 0.6 %collective-permute-done.7.refs_6_ = f32[2,128]{1,0:T(2,128)S(1)} collective-permute-done((f32[2,128]{1,0:T(2,128)S(1)}, f32[2,128]{1,0:T(2,128)S(1)}, u32[]{:S(2)}, u32[]{:S(2)}) %collective-permute-start.7) | collective-permute-done | bytes 1056 | tf_op jit(solution)/shard_map/ppermute | solution.py:335
  20.4 1.0 %shard_map.181 = (bf16[128,2048]{1,0:T(8,128)(2,1)}, bf16[4,2048]{1,0:T(4,128)(2,1)}) custom-call(f32[1,128]{1,0:T(1,128)S(1)} %compare_convert_fusion.valid_ref.refs_0_, f32[128,2048]{1,0:T(8,128)S(1)} %get-tuple-element.29.refs_1_, f32[4,2048]{1,0:T(4,128)S(1)} %get-tuple-element.34.refs_2_, f32[1,2048]{1,0:T(1,128)S(1)} %bitcast.25, ...), custom_call_target="tpu_custom_call" | custom-call | tf_op jit(solution)/shard_map/pallas_call | solution.py:259
  (20 shorter events, 0.0 us)
Async XLA Ops:
  0.6 8.6 %collective-permute-start = (bf16[4,512]{1,0:T(4,128)(2,1)}, bf16[4,512]{1,0:T(4,128)(2,1)S(1)}, u32[]{:S(2)}, u32[]{:S(2)}) collective-permute-start(bf16[4,512]{1,0:T(4,128)(2,1)} %bitcast.29), channel_id=1, source_target_pairs={{0,4},{4,8},{8,12},{12,0},{1,5},{5,9},{9,13},{13,1},{2,6},{6,10},{... | collective-permute-start | bytes 12296 | tf_op jit(solution)/shard_map/ppermute | solution.py:300
  3.7 7.1 %collective-permute-start.2 = (bf16[4,512]{1,0:T(4,128)(2,1)}, bf16[4,512]{1,0:T(4,128)(2,1)S(1)}, u32[]{:S(2)}, u32[]{:S(2)}) collective-permute-start(bf16[4,512]{1,0:T(4,128)(2,1)} %bitcast.30), channel_id=1, source_target_pairs={{0,12},{4,0},{8,4},{12,8},{1,13},{5,1},{9,5},{13,9},{2,14},{6,2},{... | collective-permute-start | bytes 12296 | tf_op jit(solution)/shard_map/ppermute | solution.py:300
  5.8 5.9 %collective-permute-start.4 = (bf16[4,512]{1,0:T(4,128)(2,1)}, bf16[4,512]{1,0:T(4,128)(2,1)S(1)}, u32[]{:S(2)}, u32[]{:S(2)}) collective-permute-start(bf16[4,512]{1,0:T(4,128)(2,1)} %bitcast.31), channel_id=1, source_target_pairs={{0,8},{4,12},{8,0},{12,4},{1,9},{5,13},{9,1},{13,5},{2,10},{6,14},... | collective-permute-start | bytes 12296 | tf_op jit(solution)/shard_map/ppermute | solution.py:300
  9.4 4.6 %copy-start = (bf16[1,128,2048]{2,1,0:T(8,128)(2,1)S(1)}, bf16[1,128,2048]{2,1,0:T(8,128)(2,1)}, u32[]{:S(2)}) copy-start(bf16[1,128,2048]{2,1,0:T(8,128)(2,1)} %param.17) | copy-start | bytes 1572868
  9.4 6.8 %collective-permute-start.1 = (f32[1,2048]{1,0:T(1,128)S(1)}, f32[1,2048]{1,0:T(1,128)S(1)}, u32[]{:S(2)}, u32[]{:S(2)}) collective-permute-start(f32[1,2048]{1,0:T(1,128)S(1)} %shard_map.177), channel_id=1, source_target_pairs={{0,12},{4,0},{8,4},{12,8},{1,13},{5,1},{9,5},{13,9},{2,14},{6,2},{... | collective-permute-start | bytes 24584 | tf_op jit(solution)/shard_map/ppermute | solution.py:300
  11.0 3.0 %copy-start.1 = (bf16[1,128,512]{2,1,0:T(8,128)(2,1)S(1)}, bf16[1,128,512]{2,1,0:T(8,128)(2,1)}, u32[]{:S(2)}) copy-start(bf16[1,128,512]{2,1,0:T(8,128)(2,1)} %param.19) | copy-start | bytes 393220
  11.0 5.5 %collective-permute-start.3 = (f32[1,2048]{1,0:T(1,128)S(1)}, f32[1,2048]{1,0:T(1,128)S(1)}, u32[]{:S(2)}, u32[]{:S(2)}) collective-permute-start(f32[1,2048]{1,0:T(1,128)S(1)} %shard_map.178), channel_id=1, source_target_pairs={{0,4},{4,8},{8,12},{12,0},{1,5},{5,9},{9,13},{13,1},{2,6},{6,10},{... | collective-permute-start | bytes 24584 | tf_op jit(solution)/shard_map/ppermute | solution.py:300
  11.7 2.3 %copy-start.4 = (bf16[1,4,2048]{2,1,0:T(4,128)(2,1)S(1)}, bf16[1,4,2048]{2,1,0:T(4,128)(2,1)}, u32[]{:S(2)}) copy-start(bf16[1,4,2048]{2,1,0:T(4,128)(2,1)} %param.28) | copy-start | bytes 49156
  11.7 2.3 %copy-start.6 = (bf16[1,4,512]{2,1,0:T(4,128)(2,1)S(1)}, bf16[1,4,512]{2,1,0:T(4,128)(2,1)}, u32[]{:S(2)}) copy-start(bf16[1,4,512]{2,1,0:T(4,128)(2,1)} %param.30) | copy-start | bytes 12292
  11.8 2.3 %copy-start.7 = (f32[1,4,32]{2,1,0:T(4,128)S(1)}, f32[1,4,32]{2,1,0:T(4,128)}, u32[]{:S(2)}) copy-start(f32[1,4,32]{2,1,0:T(4,128)} %param.31) | copy-start | bytes 1540
  11.8 2.3 %copy-start.8 = (f32[32]{0:T(128)S(1)}, f32[32]{0:T(128)}, u32[]{:S(2)}) copy-start(f32[32]{0:T(128)} %param.25) | copy-start | bytes 388
  12.0 2.1 %copy-start.3 = (bf16[1,4,2048]{2,1,0:T(4,128)(2,1)S(1)}, bf16[1,4,2048]{2,1,0:T(4,128)(2,1)}, u32[]{:S(2)}) copy-start(bf16[1,4,2048]{2,1,0:T(4,128)(2,1)} %param.27) | copy-start | bytes 49156
  12.0 4.7 %collective-permute-start.5 = (f32[1,2048]{1,0:T(1,128)S(1)}, f32[1,2048]{1,0:T(1,128)S(1)}, u32[]{:S(2)}, u32[]{:S(2)}) collective-permute-start(f32[1,2048]{1,0:T(1,128)S(1)} %shard_map.179), channel_id=1, source_target_pairs={{0,8},{4,12},{8,0},{12,4},{1,9},{5,13},{9,1},{13,5},{2,10},{6,14},... | collective-permute-start | bytes 24584 | tf_op jit(solution)/shard_map/ppermute | solution.py:300
  14.0 0.7 %copy-start.2 = (f32[2048]{0:T(1024)S(1)}, f32[2048]{0:T(1024)}, u32[]{:S(2)}) copy-start(f32[2048]{0:T(1024)} %param.26) | copy-start | bytes 24580
  14.0 0.7 %copy-start.5 = (bf16[1,4,512]{2,1,0:T(4,128)(2,1)S(1)}, bf16[1,4,512]{2,1,0:T(4,128)(2,1)}, u32[]{:S(2)}) copy-start(bf16[1,4,512]{2,1,0:T(4,128)(2,1)} %param.29) | copy-start | bytes 12292
  16.7 3.0 %collective-permute-start.6 = (f32[2,128]{1,0:T(2,128)S(1)}, f32[2,128]{1,0:T(2,128)S(1)}, u32[]{:S(2)}, u32[]{:S(2)}) collective-permute-start(f32[2,128]{1,0:T(2,128)S(1)} %get-tuple-element.35.refs_4_), channel_id=1, source_target_pairs={{0,3},{1,2},{2,1},{3,0},{4,7},{5,6},{6,5},{7,4},{8,11},{9,10},{10,... | collective-permute-start | bytes 3080 | tf_op jit(solution)/shard_map/ppermute | solution.py:335
  16.7 3.6 %collective-permute-start.7 = (f32[2,128]{1,0:T(2,128)S(1)}, f32[2,128]{1,0:T(2,128)S(1)}, u32[]{:S(2)}, u32[]{:S(2)}) collective-permute-start(f32[2,128]{1,0:T(2,128)S(1)} %get-tuple-element.35.refs_4_), channel_id=1, source_target_pairs={{0,2},{1,3},{2,0},{3,1},{4,6},{5,7},{6,4},{7,5},{8,10},{9,11},{10,... | collective-permute-start | bytes 3080 | tf_op jit(solution)/shard_map/ppermute | solution.py:335
  18.3 2.1 %collective-permute-start.8 = (f32[2,128]{1,0:T(2,128)S(1)}, f32[2,128]{1,0:T(2,128)S(1)}, u32[]{:S(2)}, u32[]{:S(2)}) collective-permute-start(f32[2,128]{1,0:T(2,128)S(1)} %get-tuple-element.35.refs_4_), channel_id=1, source_target_pairs={{0,1},{1,0},{2,3},{3,2},{4,5},{5,4},{6,7},{7,6},{8,9},{9,8},{10,11... | collective-permute-start | bytes 3080 | tf_op jit(solution)/shard_map/ppermute | solution.py:335

commit v7 on v6

--- a/solution.py
+++ b/solution.py
@@ -132,7 +132,9 @@
     block = query_ref[:, group_lanes(states, width // 64)].astype(f32)
     mine = lax.broadcasted_iota(jnp.int32, block.shape, 0) == me
     query = jnp.sum(jnp.where(mine, block, 0.0), axis=0, keepdims=True).astype(bf16)
-    out_ref[...] = jnp.dot(query, fs_ref[...], preferred_element_type=f32)
+    reads = jnp.dot(query, fs_ref[...], preferred_element_type=f32)
+    rows = [reads[:, i * 128 : (i + 1) * 128] for i in range(width // 128)]
+    out_ref[...] = jnp.concatenate(rows, axis=0).astype(bf16)
 
 
 def prompt_kernel(
@@ -210,7 +212,10 @@
     prompt = lax.broadcasted_iota(jnp.int32, (prompts, width), 0)
     reads = jnp.zeros((prompts, width), f32)
     for k, ref in zip([0] + shifts(prompts), read_refs):
-        reads = jnp.where(prompt == lax.rem(me + k, prompts), ref[...], reads)
+        answer = ref[...].astype(f32)
+        if k:
+            answer = jnp.concatenate([answer[i : i + 1] for i in range(width // 128)], axis=1)
+        reads = jnp.where(prompt == lax.rem(me + k, prompts), answer, reads)
     gated = u_ref[...] * reads + v_ref[...]
     gated_ref[...] = gated
     total = jnp.broadcast_to(jnp.sum(gated * gated, axis=1, keepdims=True), (prompts, 128))
@@ -317,7 +322,7 @@
         )
         reads = []
         for k, query in zip(shifts(samples), queries):
-            (answer,) = call(read_kernel, (fs, query), (((1, width), f32),))
+            (answer,) = call(read_kernel, (fs, query), (((width // 128, 128), bf16),))
             reads.append(shifted(answer, -k))
         gated, sq, u, v, mine, fs = call(
             prompt_kernel,

time: 21.6 us -> 21.6 us (level)
  no operation moved by 1% of the time
where the time goes in v7:
time: 21.6 us; the launch traced here: 21.3 us
  starting transfers between devices  12.2 us (56%)
  Pallas kernels  5.01 us (23%)
  waiting for transfers between devices  2.04 us (9%)
  between operations  1.4 us (6%)
  local copies, waits for them, and re-layouts  0.67 us (3%)
    ppermute x6, starting transfers between devices, shifted(): return lax.ppermute(v, 'sample', pairs)  10.3 us
    pallas_call x7, Pallas kernels, call(): pl.pallas_call(kernel, in_specs=[pl.BlockSpec(memory_space=space) for spa...  5.01 us
    ppermute x3, starting transfers between devices, layer(): lax.ppermute(pay, 'head', [(j, j ^ k) for j in range(head_parts)])  1.86 us
    ppermute x3, waiting for transfers between devices, layer(): lax.ppermute(pay, 'head', [(j, j ^ k) for j in range(head_parts)])  1.78 us
    unnamed x18, local copies, waits for them, and re-layouts  0.67 us
  transfers between devices with their start and end apart: 9, of which 4 were waited for; matrix products, arithmetic and copies ran while one was open for 0% of the time, Pallas kernels for 18%

profile of v7, /device:TPU:0, one launch (start us, length us, event | category | flops | bytes accessed | tf_op | source)
XLA Modules:
  0.0 21.3 jit_solution(2909261225674709571)
XLA Ops:
  0.6 3.1 %collective-permute-start = (bf16[4,512]{1,0:T(4,128)(2,1)}, bf16[4,512]{1,0:T(4,128)(2,1)S(1)}, u32[]{:S(2)}, u32[]{:S(2)}) collective-permute-start(bf16[4,512]{1,0:T(4,128)(2,1)} %bitcast.29), channel_id=1, source_target_pairs={{0,4},{4,8},{8,12},{12,0},{1,5},{5,9},{9,13},{13,1},{2,6},{6,10},{... | collective-permute-start | bytes 12296 | tf_op jit(solution)/shard_map/ppermute | solution.py:305
  3.7 2.1 %collective-permute-start.2 = (bf16[4,512]{1,0:T(4,128)(2,1)}, bf16[4,512]{1,0:T(4,128)(2,1)S(1)}, u32[]{:S(2)}, u32[]{:S(2)}) collective-permute-start(bf16[4,512]{1,0:T(4,128)(2,1)} %bitcast.30), channel_id=1, source_target_pairs={{0,12},{4,0},{8,4},{12,8},{1,13},{5,1},{9,5},{13,9},{2,14},{6,2},{... | collective-permute-start | bytes 12296 | tf_op jit(solution)/shard_map/ppermute | solution.py:305
  5.8 0.9 %collective-permute-start.4 = (bf16[4,512]{1,0:T(4,128)(2,1)}, bf16[4,512]{1,0:T(4,128)(2,1)S(1)}, u32[]{:S(2)}, u32[]{:S(2)}) collective-permute-start(bf16[4,512]{1,0:T(4,128)(2,1)} %bitcast.31), channel_id=1, source_target_pairs={{0,8},{4,12},{8,0},{12,4},{1,9},{5,13},{9,1},{13,5},{2,10},{6,14},... | collective-permute-start | bytes 12296 | tf_op jit(solution)/shard_map/ppermute | solution.py:305
  7.4 1.8 %shard_map.175 = (bf16[128,2048]{1,0:T(8,128)(2,1)S(1)}, f32[32,128]{1,0:T(8,128)S(1)}, f32[32,128]{1,0:T(8,128)S(1)}, bf16[128,2048]{1,0:T(8,128)(2,1)S(1)}, bf...) custom-call(f32[1,128]{1,0:T(1,128)S(1)} %compare_convert_fusion.valid_ref.refs, ...), custom_call_target="tpu_custom_call" | custom-call | tf_op jit(solution)/shard_map/pallas_call | solution.py:264
  9.2 0.2 shard_map.177
  9.4 1.4 %collective-permute-start.1 = (bf16[16,128]{1,0:T(8,128)(2,1)S(1)}, bf16[16,128]{1,0:T(8,128)(2,1)S(1)}, u32[]{:S(2)}, u32[]{:S(2)}) collective-permute-start(bf16[16,128]{1,0:T(8,128)(2,1)S(1)} %shard_map.177), channel_id=1, source_target_pairs={{0,12},{4,0},{8,4},{12,8},{1,13},{5,1},{9,5},{13,9},{2,14},{6,2},{... | collective-permute-start | bytes 12296 | tf_op jit(solution)/shard_map/ppermute | solution.py:305
  10.8 0.2 shard_map.178
  11.0 0.7 %collective-permute-start.3 = (bf16[16,128]{1,0:T(8,128)(2,1)S(1)}, bf16[16,128]{1,0:T(8,128)(2,1)S(1)}, u32[]{:S(2)}, u32[]{:S(2)}) collective-permute-start(bf16[16,128]{1,0:T(8,128)(2,1)S(1)} %shard_map.178), channel_id=1, source_target_pairs={{0,4},{4,8},{8,12},{12,0},{1,5},{5,9},{9,13},{13,1},{2,6},{6,10},{... | collective-permute-start | bytes 12296 | tf_op jit(solution)/shard_map/ppermute | solution.py:305
  11.7 0.0 collective-permute-done.4.query_ref
  11.8 0.0 copy-start.8
  11.8 0.2 shard_map.179
  12.0 2.0 %collective-permute-start.5 = (bf16[16,128]{1,0:T(8,128)(2,1)S(1)}, bf16[16,128]{1,0:T(8,128)(2,1)S(1)}, u32[]{:S(2)}, u32[]{:S(2)}) collective-permute-start(bf16[16,128]{1,0:T(8,128)(2,1)S(1)} %shard_map.179), channel_id=1, source_target_pairs={{0,8},{4,12},{8,0},{12,4},{1,9},{5,13},{9,1},{13,5},{2,10},{6,14},... | collective-permute-start | bytes 12296 | tf_op jit(solution)/shard_map/ppermute | solution.py:305
  14.1 0.6 %copy-done.2 = f32[2048]{0:T(1024)S(1)} copy-done((f32[2048]{0:T(1024)S(1)}, f32[2048]{0:T(1024)}, u32[]{:S(2)}) %copy-start.2) | copy-done | bytes 8216
  14.7 0.0 copy-done.5
  14.7 1.6 %shard_map.176 = (f32[128,2048]{1,0:T(8,128)S(1)}, f32[1,128]{1,0:T(1,128)S(1)}, f32[4,2048]{1,0:T(4,128)S(1)}, f32[4,2048]{1,0:T(4,128)S(1)}, f32[1,2048]{1,0:T(1,128)S(1)}, /*index=5*/bf16[128,2048]{1,0:T(8,128)(2,1)}) custom-call(bf16[128,2048]{1,0:T(8,128)(2,1)S(1)} %get-tuple-element.21.fs_ref, bf16[128,2048]{1,0:T(8,128)(2,1)S(1)} %get-tuple-element.22.x_ref, ...), custom_call_target="tpu_custom_call" | custom-call | tf_op jit(solution)/shard_map/pallas_call | solution.py:264
  16.3 0.0 collective-permute-done.1.refs_4_
  16.3 0.2 collective-permute-done.3.refs_5_
  16.5 0.1 collective-permute-done.5.refs_6_
  16.5 0.1 shard_map.180
  16.7 1.6 %collective-permute-start.7 = (f32[2,128]{1,0:T(2,128)S(1)}, f32[2,128]{1,0:T(2,128)S(1)}, u32[]{:S(2)}, u32[]{:S(2)}) collective-permute-start(f32[2,128]{1,0:T(2,128)S(1)} %get-tuple-element.35.refs_4_), channel_id=1, source_target_pairs={{0,2},{1,3},{2,0},{3,1},{4,6},{5,7},{6,4},{7,5},{8,10},{9,11},{10,... | collective-permute-start | bytes 3080 | tf_op jit(solution)/shard_map/ppermute | solution.py:340
  18.2 0.3 %collective-permute-start.8 = (f32[2,128]{1,0:T(2,128)S(1)}, f32[2,128]{1,0:T(2,128)S(1)}, u32[]{:S(2)}, u32[]{:S(2)}) collective-permute-start(f32[2,128]{1,0:T(2,128)S(1)} %get-tuple-element.35.refs_4_), channel_id=1, source_target_pairs={{0,1},{1,0},{2,3},{3,2},{4,5},{5,4},{6,7},{7,6},{8,9},{9,8},{10,11... | collective-permute-start | bytes 3080 | tf_op jit(solution)/shard_map/ppermute | solution.py:340
  18.5 1.1 %collective-permute-done.6.refs_5_ = f32[2,128]{1,0:T(2,128)S(1)} collective-permute-done((f32[2,128]{1,0:T(2,128)S(1)}, f32[2,128]{1,0:T(2,128)S(1)}, u32[]{:S(2)}, u32[]{:S(2)}) %collective-permute-start.6) | collective-permute-done | bytes 1056 | tf_op jit(solution)/shard_map/ppermute | solution.py:340
  19.7 0.6 %collective-permute-done.7.refs_6_ = f32[2,128]{1,0:T(2,128)S(1)} collective-permute-done((f32[2,128]{1,0:T(2,128)S(1)}, f32[2,128]{1,0:T(2,128)S(1)}, u32[]{:S(2)}, u32[]{:S(2)}) %collective-permute-start.7) | collective-permute-done | bytes 1056 | tf_op jit(solution)/shard_map/ppermute | solution.py:340
  20.3 1.0 %shard_map.181 = (bf16[128,2048]{1,0:T(8,128)(2,1)}, bf16[4,2048]{1,0:T(4,128)(2,1)}) custom-call(f32[1,128]{1,0:T(1,128)S(1)} %compare_convert_fusion.valid_ref.refs_0_, f32[128,2048]{1,0:T(8,128)S(1)} %get-tuple-element.29.refs_1_, f32[4,2048]{1,0:T(4,128)S(1)} %get-tuple-element.34.refs_2_, f32[1,2048]{1,0:T(1,128)S(1)} %bitcast.25, ...), custom_call_target="tpu_custom_call" | custom-call | tf_op jit(solution)/shard_map/pallas_call | solution.py:264
  (20 shorter events, 0.0 us)
Async XLA Ops:
  0.6 8.6 %collective-permute-start = (bf16[4,512]{1,0:T(4,128)(2,1)}, bf16[4,512]{1,0:T(4,128)(2,1)S(1)}, u32[]{:S(2)}, u32[]{:S(2)}) collective-permute-start(bf16[4,512]{1,0:T(4,128)(2,1)} %bitcast.29), channel_id=1, source_target_pairs={{0,4},{4,8},{8,12},{12,0},{1,5},{5,9},{9,13},{13,1},{2,6},{6,10},{... | collective-permute-start | bytes 12296 | tf_op jit(solution)/shard_map/ppermute | solution.py:305
  3.7 7.1 %collective-permute-start.2 = (bf16[4,512]{1,0:T(4,128)(2,1)}, bf16[4,512]{1,0:T(4,128)(2,1)S(1)}, u32[]{:S(2)}, u32[]{:S(2)}) collective-permute-start(bf16[4,512]{1,0:T(4,128)(2,1)} %bitcast.30), channel_id=1, source_target_pairs={{0,12},{4,0},{8,4},{12,8},{1,13},{5,1},{9,5},{13,9},{2,14},{6,2},{... | collective-permute-start | bytes 12296 | tf_op jit(solution)/shard_map/ppermute | solution.py:305
  5.8 5.9 %collective-permute-start.4 = (bf16[4,512]{1,0:T(4,128)(2,1)}, bf16[4,512]{1,0:T(4,128)(2,1)S(1)}, u32[]{:S(2)}, u32[]{:S(2)}) collective-permute-start(bf16[4,512]{1,0:T(4,128)(2,1)} %bitcast.31), channel_id=1, source_target_pairs={{0,8},{4,12},{8,0},{12,4},{1,9},{5,13},{9,1},{13,5},{2,10},{6,14},... | collective-permute-start | bytes 12296 | tf_op jit(solution)/shard_map/ppermute | solution.py:305
  9.4 4.6 %copy-start = (bf16[1,128,2048]{2,1,0:T(8,128)(2,1)S(1)}, bf16[1,128,2048]{2,1,0:T(8,128)(2,1)}, u32[]{:S(2)}) copy-start(bf16[1,128,2048]{2,1,0:T(8,128)(2,1)} %param.17) | copy-start | bytes 1572868
  9.4 6.8 %collective-permute-start.1 = (bf16[16,128]{1,0:T(8,128)(2,1)S(1)}, bf16[16,128]{1,0:T(8,128)(2,1)S(1)}, u32[]{:S(2)}, u32[]{:S(2)}) collective-permute-start(bf16[16,128]{1,0:T(8,128)(2,1)S(1)} %shard_map.177), channel_id=1, source_target_pairs={{0,12},{4,0},{8,4},{12,8},{1,13},{5,1},{9,5},{13,9},{2,14},{6,2},{... | collective-permute-start | bytes 12296 | tf_op jit(solution)/shard_map/ppermute | solution.py:305
  11.0 3.0 %copy-start.1 = (bf16[1,128,512]{2,1,0:T(8,128)(2,1)S(1)}, bf16[1,128,512]{2,1,0:T(8,128)(2,1)}, u32[]{:S(2)}) copy-start(bf16[1,128,512]{2,1,0:T(8,128)(2,1)} %param.19) | copy-start | bytes 393220
  11.0 5.5 %collective-permute-start.3 = (bf16[16,128]{1,0:T(8,128)(2,1)S(1)}, bf16[16,128]{1,0:T(8,128)(2,1)S(1)}, u32[]{:S(2)}, u32[]{:S(2)}) collective-permute-start(bf16[16,128]{1,0:T(8,128)(2,1)S(1)} %shard_map.178), channel_id=1, source_target_pairs={{0,4},{4,8},{8,12},{12,0},{1,5},{5,9},{9,13},{13,1},{2,6},{6,10},{... | collective-permute-start | bytes 12296 | tf_op jit(solution)/shard_map/ppermute | solution.py:305
  11.7 2.3 %copy-start.4 = (bf16[1,4,2048]{2,1,0:T(4,128)(2,1)S(1)}, bf16[1,4,2048]{2,1,0:T(4,128)(2,1)}, u32[]{:S(2)}) copy-start(bf16[1,4,2048]{2,1,0:T(4,128)(2,1)} %param.28) | copy-start | bytes 49156
  11.7 2.3 %copy-start.6 = (bf16[1,4,512]{2,1,0:T(4,128)(2,1)S(1)}, bf16[1,4,512]{2,1,0:T(4,128)(2,1)}, u32[]{:S(2)}) copy-start(bf16[1,4,512]{2,1,0:T(4,128)(2,1)} %param.30) | copy-start | bytes 12292
  11.8 2.3 %copy-start.7 = (f32[1,4,32]{2,1,0:T(4,128)S(1)}, f32[1,4,32]{2,1,0:T(4,128)}, u32[]{:S(2)}) copy-start(f32[1,4,32]{2,1,0:T(4,128)} %param.31) | copy-start | bytes 1540
  11.8 2.3 %copy-start.8 = (f32[32]{0:T(128)S(1)}, f32[32]{0:T(128)}, u32[]{:S(2)}) copy-start(f32[32]{0:T(128)} %param.25) | copy-start | bytes 388
  12.0 2.1 %copy-start.3 = (bf16[1,4,2048]{2,1,0:T(4,128)(2,1)S(1)}, bf16[1,4,2048]{2,1,0:T(4,128)(2,1)}, u32[]{:S(2)}) copy-start(bf16[1,4,2048]{2,1,0:T(4,128)(2,1)} %param.27) | copy-start | bytes 49156
  12.0 4.6 %collective-permute-start.5 = (bf16[16,128]{1,0:T(8,128)(2,1)S(1)}, bf16[16,128]{1,0:T(8,128)(2,1)S(1)}, u32[]{:S(2)}, u32[]{:S(2)}) collective-permute-start(bf16[16,128]{1,0:T(8,128)(2,1)S(1)} %shard_map.179), channel_id=1, source_target_pairs={{0,8},{4,12},{8,0},{12,4},{1,9},{5,13},{9,1},{13,5},{2,10},{6,14},... | collective-permute-start | bytes 12296 | tf_op jit(solution)/shard_map/ppermute | solution.py:305
  14.0 0.7 %copy-start.2 = (f32[2048]{0:T(1024)S(1)}, f32[2048]{0:T(1024)}, u32[]{:S(2)}) copy-start(f32[2048]{0:T(1024)} %param.26) | copy-start | bytes 24580
  14.0 0.7 %copy-start.5 = (bf16[1,4,512]{2,1,0:T(4,128)(2,1)S(1)}, bf16[1,4,512]{2,1,0:T(4,128)(2,1)}, u32[]{:S(2)}) copy-start(bf16[1,4,512]{2,1,0:T(4,128)(2,1)} %param.29) | copy-start | bytes 12292
  16.7 3.0 %collective-permute-start.6 = (f32[2,128]{1,0:T(2,128)S(1)}, f32[2,128]{1,0:T(2,128)S(1)}, u32[]{:S(2)}, u32[]{:S(2)}) collective-permute-start(f32[2,128]{1,0:T(2,128)S(1)} %get-tuple-element.35.refs_4_), channel_id=1, source_target_pairs={{0,3},{1,2},{2,1},{3,0},{4,7},{5,6},{6,5},{7,4},{8,11},{9,10},{10,... | collective-permute-start | bytes 3080 | tf_op jit(solution)/shard_map/ppermute | solution.py:340
  16.7 3.6 %collective-permute-start.7 = (f32[2,128]{1,0:T(2,128)S(1)}, f32[2,128]{1,0:T(2,128)S(1)}, u32[]{:S(2)}, u32[]{:S(2)}) collective-permute-start(f32[2,128]{1,0:T(2,128)S(1)} %get-tuple-element.35.refs_4_), channel_id=1, source_target_pairs={{0,2},{1,3},{2,0},{3,1},{4,6},{5,7},{6,4},{7,5},{8,10},{9,11},{10,... | collective-permute-start | bytes 3080 | tf_op jit(solution)/shard_map/ppermute | solution.py:340
  18.2 2.1 %collective-permute-start.8 = (f32[2,128]{1,0:T(2,128)S(1)}, f32[2,128]{1,0:T(2,128)S(1)}, u32[]{:S(2)}, u32[]{:S(2)}) collective-permute-start(f32[2,128]{1,0:T(2,128)S(1)} %get-tuple-element.35.refs_4_), channel_id=1, source_target_pairs={{0,1},{1,0},{2,3},{3,2},{4,5},{5,4},{6,7},{7,6},{8,9},{9,8},{10,11... | collective-permute-start | bytes 3080 | tf_op jit(solution)/shard_map/ppermute | solution.py:340

commit v8 on v7

--- a/solution.py
+++ b/solution.py
@@ -126,15 +126,21 @@
         fs_ref[rows, :] = (fresh_ref[rows, :] + total * s0_ref[rows, :]).astype(bf16)
 
 
-def read_kernel(fs_ref, query_ref, out_ref):
+def read_kernel(fs_ref, *refs):
+    count = len(refs) // 2
     states, width = fs_ref.shape
     me = lax.axis_index("sample")
-    block = query_ref[:, group_lanes(states, width // 64)].astype(f32)
-    mine = lax.broadcasted_iota(jnp.int32, block.shape, 0) == me
-    query = jnp.sum(jnp.where(mine, block, 0.0), axis=0, keepdims=True).astype(bf16)
+    lanes = group_lanes(states, width // 64)
+    queries = []
+    for query_ref in refs[:count]:
+        block = query_ref[:, lanes].astype(f32)
+        mine = lax.broadcasted_iota(jnp.int32, block.shape, 0) == me
+        queries.append(jnp.sum(jnp.where(mine, block, 0.0), axis=0, keepdims=True))
+    query = jnp.concatenate(queries, axis=0).astype(bf16)
     reads = jnp.dot(query, fs_ref[...], preferred_element_type=f32)
-    rows = [reads[:, i * 128 : (i + 1) * 128] for i in range(width // 128)]
-    out_ref[...] = jnp.concatenate(rows, axis=0).astype(bf16)
+    for k, out_ref in enumerate(refs[count:]):
+        rows = [reads[k : k + 1, i * 128 : (i + 1) * 128] for i in range(width // 128)]
+        out_ref[...] = jnp.concatenate(rows, axis=0).astype(bf16)
 
 
 def prompt_kernel(
@@ -321,8 +327,11 @@
             ), fetch=True,
         )
         reads = []
-        for k, query in zip(shifts(samples), queries):
-            (answer,) = call(read_kernel, (fs, query), (((width // 128, 128), bf16),))
+        answers = []
+        for some in (queries[:1], queries[1:]):
+            shape = ((width // 128, 128), bf16)
+            answers += call(read_kernel, (fs, *some), (shape,) * len(some))
+        for k, answer in zip(shifts(samples), answers):
             reads.append(shifted(answer, -k))
         gated, sq, u, v, mine, fs = call(
             prompt_kernel,

time: 21.6 us -> 22.2 us (1.028)
  waiting for transfers between devices: 2.04 us -> 3.04 us
    ppermute x6, waiting for transfers between devices: 0.26 us -> 1.26 us  [shifted(): return lax.ppermute(v, 'sample', pairs)]
    ppermute x6, starting transfers between devices: 10.3 us -> 10.1 us  [shifted(): return lax.ppermute(v, 'sample', pairs)]
    pallas_call x7 -> x6, Pallas kernels: 5.01 us -> 4.82 us  [call(): pl.pallas_call(kernel, in_specs=[pl.BlockSpec(memory_space=space) for spa...]
  transfers between devices with their start and end apart: 9 -> 9, of which waited for: 4 -> 3; matrix products, arithmetic and copies ran while one was open for 0% -> 0% of each run, Pallas kernels for 18% -> 17%
where the time goes in v8:
time: 22.2 us; the launch traced here: 21.9 us
  starting transfers between devices  12 us (54%)
  Pallas kernels  4.82 us (22%)
  waiting for transfers between devices  3.04 us (14%)
  between operations  1.41 us (6%)
  local copies, waits for them, and re-layouts  0.67 us (3%)
    ppermute x6, starting transfers between devices, shifted(): return lax.ppermute(v, 'sample', pairs)  10.1 us
    pallas_call x6, Pallas kernels, call(): pl.pallas_call(kernel, in_specs=[pl.BlockSpec(memory_space=space) for spa...  4.82 us
    ppermute x3, starting transfers between devices, layer(): lax.ppermute(pay, 'head', [(j, j ^ k) for j in range(head_parts)])  1.86 us
    ppermute x3, waiting for transfers between devices, layer(): lax.ppermute(pay, 'head', [(j, j ^ k) for j in range(head_parts)])  1.78 us
    ppermute x6, waiting for transfers between devices, shifted(): return lax.ppermute(v, 'sample', pairs)  1.26 us
    unnamed x18, local copies, waits for them, and re-layouts  0.67 us
  transfers between devices with their start and end apart: 9, of which 3 were waited for; matrix products, arithmetic and copies ran while one was open for 0% of the time, Pallas kernels for 17%

profile of v8, /device:TPU:0, one launch (start us, length us, event | category | flops | bytes accessed | tf_op | source)
XLA Modules:
  0.0 21.9 jit_solution(189336118909720363)
XLA Ops:
  0.6 5.1 %collective-permute-start.2 = (bf16[4,512]{1,0:T(4,128)(2,1)}, bf16[4,512]{1,0:T(4,128)(2,1)S(1)}, u32[]{:S(2)}, u32[]{:S(2)}) collective-permute-start(bf16[4,512]{1,0:T(4,128)(2,1)} %bitcast.29), channel_id=1, source_target_pairs={{0,12},{4,0},{8,4},{12,8},{1,13},{5,1},{9,5},{13,9},{2,14},{6,2},{... | collective-permute-start | bytes 12296 | tf_op jit(solution)/shard_map/ppermute | solution.py:311
  5.8 0.0 collective-permute-start.3
  5.8 1.0 %collective-permute-start = (bf16[4,512]{1,0:T(4,128)(2,1)}, bf16[4,512]{1,0:T(4,128)(2,1)S(1)}, u32[]{:S(2)}, u32[]{:S(2)}) collective-permute-start(bf16[4,512]{1,0:T(4,128)(2,1)} %bitcast.31), channel_id=1, source_target_pairs={{0,4},{4,8},{8,12},{12,0},{1,5},{5,9},{9,13},{13,1},{2,6},{6,10},{... | collective-permute-start | bytes 12296 | tf_op jit(solution)/shard_map/ppermute | solution.py:311
  7.4 1.8 %shard_map.175 = (bf16[128,2048]{1,0:T(8,128)(2,1)S(1)}, f32[32,128]{1,0:T(8,128)S(1)}, f32[32,128]{1,0:T(8,128)S(1)}, bf16[128,2048]{1,0:T(8,128)(2,1)S(1)}, bf...) custom-call(f32[1,128]{1,0:T(1,128)S(1)} %compare_convert_fusion.valid_ref.refs, ...), custom_call_target="tpu_custom_call" | custom-call | tf_op jit(solution)/shard_map/pallas_call | solution.py:270
  9.2 1.2 %collective-permute-done.3.refs_1_ = bf16[4,512]{1,0:T(4,128)(2,1)S(1)} collective-permute-done((bf16[4,512]{1,0:T(4,128)(2,1)}, bf16[4,512]{1,0:T(4,128)(2,1)S(1)}, u32[]{:S(2)}, u32[]{:S(2)}) %collective-permute-start.3) | collective-permute-done | bytes 4128 | tf_op jit(solution)/shard_map/ppermute | solution.py:311
  10.5 0.2 shard_map.178
  10.7 1.3 %collective-permute-start.4 = (bf16[16,128]{1,0:T(8,128)(2,1)S(1)}, bf16[16,128]{1,0:T(8,128)(2,1)S(1)}, u32[]{:S(2)}, u32[]{:S(2)}) collective-permute-start(bf16[16,128]{1,0:T(8,128)(2,1)S(1)} %get-tuple-element.36), channel_id=1, source_target_pairs={{0,4},{4,8},{8,12},{12,0},{1,5},{5,9},{9,13},{13,1},{2,6},{6,10},{... | collective-permute-start | bytes 12296 | tf_op jit(solution)/shard_map/ppermute | solution.py:311
  12.0 0.9 %collective-permute-start.5 = (bf16[16,128]{1,0:T(8,128)(2,1)S(1)}, bf16[16,128]{1,0:T(8,128)(2,1)S(1)}, u32[]{:S(2)}, u32[]{:S(2)}) collective-permute-start(bf16[16,128]{1,0:T(8,128)(2,1)S(1)} %get-tuple-element.37), channel_id=1, source_target_pairs={{0,8},{4,12},{8,0},{12,4},{1,9},{5,13},{9,1},{13,5},{2,10},{6,14},... | collective-permute-start | bytes 12296 | tf_op jit(solution)/shard_map/ppermute | solution.py:311
  12.9 0.0 collective-permute-done.refs_0_
  12.9 0.0 copy-start.8
  12.9 0.2 shard_map.177
  13.1 1.8 %collective-permute-start.1 = (bf16[16,128]{1,0:T(8,128)(2,1)S(1)}, bf16[16,128]{1,0:T(8,128)(2,1)S(1)}, u32[]{:S(2)}, u32[]{:S(2)}) collective-permute-start(bf16[16,128]{1,0:T(8,128)(2,1)S(1)} %shard_map.177), channel_id=1, source_target_pairs={{0,12},{4,0},{8,4},{12,8},{1,13},{5,1},{9,5},{13,9},{2,14},{6,2},{... | collective-permute-start | bytes 12296 | tf_op jit(solution)/shard_map/ppermute | solution.py:311
  14.9 0.6 %copy-done.2 = f32[2048]{0:T(1024)S(1)} copy-done((f32[2048]{0:T(1024)S(1)}, f32[2048]{0:T(1024)}, u32[]{:S(2)}) %copy-start.2) | copy-done | bytes 8216
  15.5 0.0 copy-done.5
  15.5 1.5 %shard_map.176 = (f32[128,2048]{1,0:T(8,128)S(1)}, f32[1,128]{1,0:T(1,128)S(1)}, f32[4,2048]{1,0:T(4,128)S(1)}, f32[4,2048]{1,0:T(4,128)S(1)}, f32[1,2048]{1,0:T(1,128)S(1)}, /*index=5*/bf16[128,2048]{1,0:T(8,128)(2,1)}) custom-call(bf16[128,2048]{1,0:T(8,128)(2,1)S(1)} %get-tuple-element.23.fs_ref, bf16[128,2048]{1,0:T(8,128)(2,1)S(1)} %get-tuple-element.24.x_ref, ...), custom_call_target="tpu_custom_call" | custom-call | tf_op jit(solution)/shard_map/pallas_call | solution.py:270
  17.1 0.0 collective-permute-done.5.refs_6_
  17.1 0.0 collective-permute-done.1.refs_4_
  17.1 0.1 shard_map.179
  17.3 0.0 collective-permute-start.6
  17.3 1.6 %collective-permute-start.7 = (f32[2,128]{1,0:T(2,128)S(1)}, f32[2,128]{1,0:T(2,128)S(1)}, u32[]{:S(2)}, u32[]{:S(2)}) collective-permute-start(f32[2,128]{1,0:T(2,128)S(1)} %get-tuple-element.39.refs_4_), channel_id=1, source_target_pairs={{0,2},{1,3},{2,0},{3,1},{4,6},{5,7},{6,4},{7,5},{8,10},{9,11},{10,... | collective-permute-start | bytes 3080 | tf_op jit(solution)/shard_map/ppermute | solution.py:349
  18.8 0.3 %collective-permute-start.8 = (f32[2,128]{1,0:T(2,128)S(1)}, f32[2,128]{1,0:T(2,128)S(1)}, u32[]{:S(2)}, u32[]{:S(2)}) collective-permute-start(f32[2,128]{1,0:T(2,128)S(1)} %get-tuple-element.39.refs_4_), channel_id=1, source_target_pairs={{0,1},{1,0},{2,3},{3,2},{4,5},{5,4},{6,7},{7,6},{8,9},{9,8},{10,11... | collective-permute-start | bytes 3080 | tf_op jit(solution)/shard_map/ppermute | solution.py:349
  19.1 1.1 %collective-permute-done.6.refs_5_ = f32[2,128]{1,0:T(2,128)S(1)} collective-permute-done((f32[2,128]{1,0:T(2,128)S(1)}, f32[2,128]{1,0:T(2,128)S(1)}, u32[]{:S(2)}, u32[]{:S(2)}) %collective-permute-start.6) | collective-permute-done | bytes 1056 | tf_op jit(solution)/shard_map/ppermute | solution.py:349
  20.3 0.6 %collective-permute-done.7.refs_6_ = f32[2,128]{1,0:T(2,128)S(1)} collective-permute-done((f32[2,128]{1,0:T(2,128)S(1)}, f32[2,128]{1,0:T(2,128)S(1)}, u32[]{:S(2)}, u32[]{:S(2)}) %collective-permute-start.7) | collective-permute-done | bytes 1056 | tf_op jit(solution)/shard_map/ppermute | solution.py:349
  20.9 1.0 %shard_map.180 = (bf16[128,2048]{1,0:T(8,128)(2,1)}, bf16[4,2048]{1,0:T(4,128)(2,1)}) custom-call(f32[1,128]{1,0:T(1,128)S(1)} %compare_convert_fusion.valid_ref.refs_0_, f32[128,2048]{1,0:T(8,128)S(1)} %get-tuple-element.31.refs_1_, f32[4,2048]{1,0:T(4,128)S(1)} %get-tuple-element.38.refs_2_, f32[1,2048]{1,0:T(1,128)S(1)} %bitcast.25, ...), custom_call_target="tpu_custom_call" | custom-call | tf_op jit(solution)/shard_map/pallas_call | solution.py:270
  (19 shorter events, 0.0 us)
Async XLA Ops:
  0.6 8.6 %collective-permute-start.2 = (bf16[4,512]{1,0:T(4,128)(2,1)}, bf16[4,512]{1,0:T(4,128)(2,1)S(1)}, u32[]{:S(2)}, u32[]{:S(2)}) collective-permute-start(bf16[4,512]{1,0:T(4,128)(2,1)} %bitcast.29), channel_id=1, source_target_pairs={{0,12},{4,0},{8,4},{12,8},{1,13},{5,1},{9,5},{13,9},{2,14},{6,2},{... | collective-permute-start | bytes 12296 | tf_op jit(solution)/shard_map/ppermute | solution.py:311
  5.8 4.7 %collective-permute-start.3 = (bf16[4,512]{1,0:T(4,128)(2,1)}, bf16[4,512]{1,0:T(4,128)(2,1)S(1)}, u32[]{:S(2)}, u32[]{:S(2)}) collective-permute-start(bf16[4,512]{1,0:T(4,128)(2,1)} %bitcast.30), channel_id=1, source_target_pairs={{0,8},{4,12},{8,0},{12,4},{1,9},{5,13},{9,1},{13,5},{2,10},{6,14},... | collective-permute-start | bytes 12296 | tf_op jit(solution)/shard_map/ppermute | solution.py:311
  5.8 7.1 %collective-permute-start = (bf16[4,512]{1,0:T(4,128)(2,1)}, bf16[4,512]{1,0:T(4,128)(2,1)S(1)}, u32[]{:S(2)}, u32[]{:S(2)}) collective-permute-start(bf16[4,512]{1,0:T(4,128)(2,1)} %bitcast.31), channel_id=1, source_target_pairs={{0,4},{4,8},{8,12},{12,0},{1,5},{5,9},{9,13},{13,1},{2,6},{6,10},{... | collective-permute-start | bytes 12296 | tf_op jit(solution)/shard_map/ppermute | solution.py:311
  10.5 4.4 %copy-start = (bf16[1,128,2048]{2,1,0:T(8,128)(2,1)S(1)}, bf16[1,128,2048]{2,1,0:T(8,128)(2,1)}, u32[]{:S(2)}) copy-start(bf16[1,128,2048]{2,1,0:T(8,128)(2,1)} %param.17) | copy-start | bytes 1572868
  10.7 6.4 %collective-permute-start.4 = (bf16[16,128]{1,0:T(8,128)(2,1)S(1)}, bf16[16,128]{1,0:T(8,128)(2,1)S(1)}, u32[]{:S(2)}, u32[]{:S(2)}) collective-permute-start(bf16[16,128]{1,0:T(8,128)(2,1)S(1)} %get-tuple-element.36), channel_id=1, source_target_pairs={{0,4},{4,8},{8,12},{12,0},{1,5},{5,9},{9,13},{13,1},{2,6},{6,10},{... | collective-permute-start | bytes 12296 | tf_op jit(solution)/shard_map/ppermute | solution.py:311
  12.0 2.9 %copy-start.1 = (bf16[1,128,512]{2,1,0:T(8,128)(2,1)S(1)}, bf16[1,128,512]{2,1,0:T(8,128)(2,1)}, u32[]{:S(2)}) copy-start(bf16[1,128,512]{2,1,0:T(8,128)(2,1)} %param.19) | copy-start | bytes 393220
  12.0 5.1 %collective-permute-start.5 = (bf16[16,128]{1,0:T(8,128)(2,1)S(1)}, bf16[16,128]{1,0:T(8,128)(2,1)S(1)}, u32[]{:S(2)}, u32[]{:S(2)}) collective-permute-start(bf16[16,128]{1,0:T(8,128)(2,1)S(1)} %get-tuple-element.37), channel_id=1, source_target_pairs={{0,8},{4,12},{8,0},{12,4},{1,9},{5,13},{9,1},{13,5},{2,10},{6,14},... | collective-permute-start | bytes 12296 | tf_op jit(solution)/shard_map/ppermute | solution.py:311
  12.9 2.0 %copy-start.4 = (bf16[1,4,2048]{2,1,0:T(4,128)(2,1)S(1)}, bf16[1,4,2048]{2,1,0:T(4,128)(2,1)}, u32[]{:S(2)}) copy-start(bf16[1,4,2048]{2,1,0:T(4,128)(2,1)} %param.28) | copy-start | bytes 49156
  12.9 2.0 %copy-start.6 = (bf16[1,4,512]{2,1,0:T(4,128)(2,1)S(1)}, bf16[1,4,512]{2,1,0:T(4,128)(2,1)}, u32[]{:S(2)}) copy-start(bf16[1,4,512]{2,1,0:T(4,128)(2,1)} %param.30) | copy-start | bytes 12292
  12.9 2.0 %copy-start.7 = (f32[1,4,32]{2,1,0:T(4,128)S(1)}, f32[1,4,32]{2,1,0:T(4,128)}, u32[]{:S(2)}) copy-start(f32[1,4,32]{2,1,0:T(4,128)} %param.31) | copy-start | bytes 1540
  12.9 2.0 %copy-start.8 = (f32[32]{0:T(128)S(1)}, f32[32]{0:T(128)}, u32[]{:S(2)}) copy-start(f32[32]{0:T(128)} %param.25) | copy-start | bytes 388
  13.1 1.8 %copy-start.3 = (bf16[1,4,2048]{2,1,0:T(4,128)(2,1)S(1)}, bf16[1,4,2048]{2,1,0:T(4,128)(2,1)}, u32[]{:S(2)}) copy-start(bf16[1,4,2048]{2,1,0:T(4,128)(2,1)} %param.27) | copy-start | bytes 49156
  13.1 4.0 %collective-permute-start.1 = (bf16[16,128]{1,0:T(8,128)(2,1)S(1)}, bf16[16,128]{1,0:T(8,128)(2,1)S(1)}, u32[]{:S(2)}, u32[]{:S(2)}) collective-permute-start(bf16[16,128]{1,0:T(8,128)(2,1)S(1)} %shard_map.177), channel_id=1, source_target_pairs={{0,12},{4,0},{8,4},{12,8},{1,13},{5,1},{9,5},{13,9},{2,14},{6,2},{... | collective-permute-start | bytes 12296 | tf_op jit(solution)/shard_map/ppermute | solution.py:311
  14.8 0.7 %copy-start.2 = (f32[2048]{0:T(1024)S(1)}, f32[2048]{0:T(1024)}, u32[]{:S(2)}) copy-start(f32[2048]{0:T(1024)} %param.26) | copy-start | bytes 24580
  14.8 0.7 %copy-start.5 = (bf16[1,4,512]{2,1,0:T(4,128)(2,1)S(1)}, bf16[1,4,512]{2,1,0:T(4,128)(2,1)}, u32[]{:S(2)}) copy-start(bf16[1,4,512]{2,1,0:T(4,128)(2,1)} %param.29) | copy-start | bytes 12292
  17.3 3.0 %collective-permute-start.6 = (f32[2,128]{1,0:T(2,128)S(1)}, f32[2,128]{1,0:T(2,128)S(1)}, u32[]{:S(2)}, u32[]{:S(2)}) collective-permute-start(f32[2,128]{1,0:T(2,128)S(1)} %get-tuple-element.39.refs_4_), channel_id=1, source_target_pairs={{0,3},{1,2},{2,1},{3,0},{4,7},{5,6},{6,5},{7,4},{8,11},{9,10},{10,... | collective-permute-start | bytes 3080 | tf_op jit(solution)/shard_map/ppermute | solution.py:349
  17.3 3.6 %collective-permute-start.7 = (f32[2,128]{1,0:T(2,128)S(1)}, f32[2,128]{1,0:T(2,128)S(1)}, u32[]{:S(2)}, u32[]{:S(2)}) collective-permute-start(f32[2,128]{1,0:T(2,128)S(1)} %get-tuple-element.39.refs_4_), channel_id=1, source_target_pairs={{0,2},{1,3},{2,0},{3,1},{4,6},{5,7},{6,4},{7,5},{8,10},{9,11},{10,... | collective-permute-start | bytes 3080 | tf_op jit(solution)/shard_map/ppermute | solution.py:349
  18.8 2.1 %collective-permute-start.8 = (f32[2,128]{1,0:T(2,128)S(1)}, f32[2,128]{1,0:T(2,128)S(1)}, u32[]{:S(2)}, u32[]{:S(2)}) collective-permute-start(f32[2,128]{1,0:T(2,128)S(1)} %get-tuple-element.39.refs_4_), channel_id=1, source_target_pairs={{0,1},{1,0},{2,3},{3,2},{4,5},{5,4},{6,7},{7,6},{8,9},{9,8},{10,11... | collective-permute-start | bytes 3080 | tf_op jit(solution)/shard_map/ppermute | solution.py:349
